TPU v7x, 32 devices: a whole 2x2x4 slice. The times are simulated.
32 devices in a mesh: dp: 2 (over y), seq: 16 (over z, x, core).
Axes of the slice: x: 2, y: 2, z: 4, core: 2. Of those that a mesh axis runs over, the one named last changes fastest.
Arguments:
- layer_input: bfloat16 [4096, 1024], P(('dp', 'seq')), may hold values from -6 to 6
- norm_gain: bfloat16 [1024], P('dp'), may hold values from 0.5 to 1.5
- in_weight: bfloat16 [1024, 4384], P('dp'), may hold values from -0.1875 to 0.1875
- conv_weight: bfloat16 [4, 2304], P(None, 'dp'), may hold values from -3 to 3
- conv_bias: bfloat16 [2304], P('dp'), may hold values from -2 to 2
- step_bias: bfloat16 [32], P('dp'), may hold values from -5 to -1
- rate_log: bfloat16 [32], P('dp'), may hold values from -4 to 2
- skip_gain: bfloat16 [32], P('dp'), may hold values from 0.5 to 2
- gate_gain: bfloat16 [2048], P('dp'), may hold values from 0.5 to 1.5
- out_weight: bfloat16 [2048, 1024], P('dp'), may hold values from -0.125 to 0.125
- cotangent: bfloat16 [4096, 1024], P(('dp', 'seq')), may hold values from -6 to 6
Outputs:
- layer_output: bfloat16 [4096, 1024], P(('dp', 'seq'))
- input_grad: float32 [4096, 1024], P(('dp', 'seq'))
- norm_gain_grad: float32 [1024], P('dp')
- in_weight_grad: float32 [1024, 4384], P('dp')
- conv_weight_grad: float32 [4, 2304], P(None, 'dp')
- conv_bias_grad: float32 [2304], P('dp')
- step_bias_grad: float32 [32], P('dp')
- rate_log_grad: float32 [32], P('dp')
- skip_gain_grad: float32 [32], P('dp')
- gate_gain_grad: float32 [2048], P('dp')
- out_weight_grad: float32 [2048, 1024], P('dp')
All inputs are finite; a program needn't handle non-finite values.
Results may differ from a plain program's by a relative error of at most 0.012.
Values may be sent and summed in bfloat16 or wider, within the bound.
No kernel may reach another device: no remote copies, remote signals or barrier semaphores. Data moves between devices by JAX's collectives and lax.ppermute only.
A program may use at most 192 MiB of HBM per device.

v0:
```python
import jax
import jax.numpy as jnp
from jax import lax
from jax.sharding import PartitionSpec as P

BLOCK = 256


epsilon = 1e-05
highest = lax.Precision.HIGHEST


def front_norm(values, gain):
    scale = lax.rsqrt(jnp.mean(values * values, axis=-1, keepdims=True) + epsilon)
    return values * scale * gain


def gated_norm(mixer_out, gate_in, gain):
    gated = mixer_out * jax.nn.silu(gate_in)
    scale = lax.rsqrt(jnp.mean(gated * gated, axis=-1, keepdims=True) + epsilon)
    return gated * scale * gain


def causal_conv(values, taps, offset):
    width = taps.shape[0]
    length = values.shape[0]
    padded = jnp.concatenate(
        [jnp.zeros((width - 1, values.shape[1]), values.dtype), values], axis=0
    )
    total = offset[None, :] + jnp.zeros_like(values)
    for index in range(width):
        total = total + taps[index][None, :] * padded[index : index + length]
    return jax.nn.silu(total)


def scan_blocks(values, steps, rates, keys, queries):
    length, heads, hdim = values.shape
    states = keys.shape[1]
    blocks = length // BLOCK
    items = (
        values.reshape(blocks, BLOCK, heads, hdim),
        steps.reshape(blocks, BLOCK, heads),
        keys.reshape(blocks, BLOCK, states),
        queries.reshape(blocks, BLOCK, states),
    )

    def one_block(state, item):
        val_blk, step_blk, key_blk, query_blk = item
        logs = (step_blk * rates[None, :]).T
        cums = jnp.cumsum(logs, axis=1)
        rows = lax.broadcasted_iota(jnp.int32, (BLOCK, BLOCK), 0)
        cols = lax.broadcasted_iota(jnp.int32, (BLOCK, BLOCK), 1)
        lower = (rows >= cols)[None]
        spread = cums[:, :, None] - cums[:, None, :]
        decay = jnp.where(lower, jnp.exp(jnp.where(lower, spread, 0.0)), 0.0)
        scores = jnp.dot(query_blk, key_blk.T, precision=highest)
        weights = scores[None] * decay * step_blk.T[:, None, :]
        inside = jnp.einsum("hts,shp->thp", weights, val_blk, precision=highest)
        carried = (
            jnp.einsum("tn,hpn->thp", query_blk, state, precision=highest)
            * jnp.exp(cums).T[:, :, None]
        )
        tail = jnp.exp(cums[:, -1:] - cums) * step_blk.T
        update = jnp.einsum("hs,shp,sn->hpn", tail, val_blk, key_blk, precision=highest)
        fresh = state * jnp.exp(cums[:, -1])[:, None, None] + update
        return (fresh, inside + carried)

    start = jnp.zeros((heads, hdim, states), jnp.float32)
    final_state, outputs = lax.scan(jax.checkpoint(one_block), start, items)
    return outputs.reshape(length, heads, hdim)


def mixer(
    x_head, step_raw, key_query, x_taps, x_offset, kq_taps, kq_offset, step_shift, rate_logs, skips
):
    x_conv = causal_conv(x_head, x_taps, x_offset)
    kq_conv = causal_conv(key_query, kq_taps, kq_offset)
    states = kq_conv.shape[1] // 2
    keys = kq_conv[:, :states]
    queries = kq_conv[:, states:]
    steps = jax.nn.softplus(step_raw + step_shift[None, :])
    rates = -jnp.exp(rate_logs)
    heads = step_shift.shape[0]
    length = x_head.shape[0]
    values = x_conv.reshape(length, heads, -1)
    mixed = scan_blocks(values, steps, rates, keys, queries) + values * skips[None, :, None]
    return mixed.reshape(length, -1)


def own_block(values, dim):
    parts = lax.axis_size("dp")
    width = values.shape[dim] // parts
    return lax.dynamic_slice_in_dim(values, lax.axis_index("dp") * width, width, dim)


def local(
    layer_input,
    norm_gain,
    in_weight,
    conv_weight,
    conv_bias,
    step_bias,
    rate_log,
    skip_gain,
    gate_gain,
    out_weight,
    cotangent,
):
    (
        full_gain,
        full_in,
        full_taps,
        full_offset,
        full_shift,
        full_rates,
        full_skip,
        full_gate,
        full_out,
    ) = (
        lax.all_gather(norm_gain, "dp", axis=0, tiled=True),
        lax.all_gather(in_weight, "dp", axis=0, tiled=True),
        lax.all_gather(conv_weight, "dp", axis=1, tiled=True),
        lax.all_gather(conv_bias, "dp", axis=0, tiled=True),
        lax.all_gather(step_bias, "dp", axis=0, tiled=True),
        lax.all_gather(rate_log, "dp", axis=0, tiled=True),
        lax.all_gather(skip_gain, "dp", axis=0, tiled=True),
        lax.all_gather(gate_gain, "dp", axis=0, tiled=True),
        lax.all_gather(out_weight, "dp", axis=0, tiled=True),
    )
    inner = full_out.shape[0]
    heads = full_shift.shape[0]
    states = (full_taps.shape[1] - inner) // 2
    group = lax.axis_size("seq")
    local_heads = heads // group
    span = local_heads * (inner // heads)
    rank = lax.axis_index("seq")
    tok_vals = layer_input.astype(jnp.float32)
    normed, pull_front = jax.vjp(front_norm, tok_vals, full_gain.astype(jnp.float32))
    normed_low = normed.astype(jnp.bfloat16)
    proj_low = jnp.dot(normed_low, full_in, preferred_element_type=jnp.float32).astype(jnp.bfloat16)
    gate_in = proj_low[:, :inner]
    x_part = proj_low[:, inner : 2 * inner]
    kq_part = proj_low[:, 2 * inner : 2 * inner + 2 * states]
    step_part = proj_low[:, 2 * inner + 2 * states :]
    x_head, step_head = (
        lax.all_to_all(x_part, "seq", split_axis=1, concat_axis=0, tiled=True),
        lax.all_to_all(step_part, "seq", split_axis=1, concat_axis=0, tiled=True),
    )
    kq_whole = lax.all_gather(kq_part, "seq", axis=0, tiled=True)
    taps_f = full_taps.astype(jnp.float32)
    offset_f = full_offset.astype(jnp.float32)
    x_taps = lax.dynamic_slice_in_dim(taps_f, rank * span, span, 1)
    x_offset = lax.dynamic_slice_in_dim(offset_f, rank * span, span, 0)
    shift_own = lax.dynamic_slice_in_dim(
        full_shift.astype(jnp.float32), rank * local_heads, local_heads, 0
    )
    rates_own = lax.dynamic_slice_in_dim(
        full_rates.astype(jnp.float32), rank * local_heads, local_heads, 0
    )
    skip_own = lax.dynamic_slice_in_dim(
        full_skip.astype(jnp.float32), rank * local_heads, local_heads, 0
    )
    mixed, pull_mix = jax.vjp(
        mixer,
        x_head.astype(jnp.float32),
        step_head.astype(jnp.float32),
        kq_whole.astype(jnp.float32),
        x_taps,
        x_offset,
        taps_f[:, inner:],
        offset_f[inner:],
        shift_own,
        rates_own,
        skip_own,
    )
    mixer_tok = lax.all_to_all(
        mixed.astype(jnp.bfloat16), "seq", split_axis=0, concat_axis=1, tiled=True
    )
    gate_out, pull_gate = jax.vjp(
        gated_norm,
        mixer_tok.astype(jnp.float32),
        gate_in.astype(jnp.float32),
        full_gate.astype(jnp.float32),
    )
    gate_low = gate_out.astype(jnp.bfloat16)
    layer_output = (
        tok_vals + jnp.dot(gate_low, full_out, preferred_element_type=jnp.float32)
    ).astype(jnp.bfloat16)
    out_grad = jnp.dot(gate_low.T, cotangent, preferred_element_type=jnp.float32)
    d_gate_out = jnp.dot(cotangent, full_out.T, preferred_element_type=jnp.float32)
    d_mixer_tok, d_gate_in, gate_grad = pull_gate(d_gate_out)
    d_mixer_head = lax.all_to_all(
        d_mixer_tok.astype(jnp.bfloat16), "seq", split_axis=1, concat_axis=0, tiled=True
    )
    (
        d_x_head,
        d_step_head,
        d_kq_whole,
        d_x_taps,
        d_x_offset,
        d_kq_taps,
        d_kq_offset,
        d_shift_own,
        d_rates_own,
        d_skip_own,
    ) = pull_mix(d_mixer_head.astype(jnp.float32))
    d_x_tok, d_step_tok = (
        lax.all_to_all(
            d_x_head.astype(jnp.bfloat16), "seq", split_axis=0, concat_axis=1, tiled=True
        ),
        lax.all_to_all(
            d_step_head.astype(jnp.bfloat16), "seq", split_axis=0, concat_axis=1, tiled=True
        ),
    )
    d_kq_tok = lax.psum_scatter(
        d_kq_whole.astype(jnp.bfloat16), "seq", scatter_dimension=0, tiled=True
    )
    d_proj = jnp.concatenate(
        [d_gate_in.astype(jnp.bfloat16), d_x_tok, d_kq_tok, d_step_tok], axis=1
    )
    in_grad = jnp.dot(normed_low.T, d_proj, preferred_element_type=jnp.float32)
    d_normed = jnp.dot(d_proj, full_in.T, preferred_element_type=jnp.float32)
    d_front, gain_grad = pull_front(d_normed)
    input_grad = d_front + cotangent.astype(jnp.float32)
    x_tap_grad = lax.dynamic_update_slice_in_dim(
        jnp.zeros((taps_f.shape[0], inner), jnp.float32), d_x_taps, rank * span, 1
    )
    taps_grad = jnp.concatenate([x_tap_grad, d_kq_taps], axis=1)
    x_off_grad = lax.dynamic_update_slice_in_dim(
        jnp.zeros((inner,), jnp.float32), d_x_offset, rank * span, 0
    )
    offset_grad = jnp.concatenate([x_off_grad, d_kq_offset], axis=0)
    head_zeros = jnp.zeros((heads,), jnp.float32)
    shift_grad = lax.dynamic_update_slice_in_dim(head_zeros, d_shift_own, rank * local_heads, 0)
    rates_grad = lax.dynamic_update_slice_in_dim(head_zeros, d_rates_own, rank * local_heads, 0)
    skip_grad = lax.dynamic_update_slice_in_dim(head_zeros, d_skip_own, rank * local_heads, 0)
    in_part, out_part = (
        lax.psum_scatter(in_grad, ("dp", "seq"), scatter_dimension=0, tiled=True),
        lax.psum_scatter(out_grad, ("dp", "seq"), scatter_dimension=0, tiled=True),
    )
    in_shard, out_shard = (
        lax.all_gather(in_part, "seq", axis=0, tiled=True),
        lax.all_gather(out_part, "seq", axis=0, tiled=True),
    )
    gain_all, taps_all, offset_all, shift_all, rates_all, skip_all, gate_all = lax.psum(
        (gain_grad, taps_grad, offset_grad, shift_grad, rates_grad, skip_grad, gate_grad),
        ("dp", "seq"),
    )
    gain_shard = own_block(gain_all, 0)
    taps_shard = own_block(taps_all, 1)
    offset_shard = own_block(offset_all, 0)
    shift_shard = own_block(shift_all, 0)
    rates_shard = own_block(rates_all, 0)
    skip_shard = own_block(skip_all, 0)
    gate_shard = own_block(gate_all, 0)
    return (
        layer_output,
        input_grad,
        gain_shard,
        in_shard,
        taps_shard,
        offset_shard,
        shift_shard,
        rates_shard,
        skip_shard,
        gate_shard,
        out_shard,
    )


def solution(mesh):
    return jax.shard_map(
        local,
        mesh=mesh,
        in_specs=(
            P(("dp", "seq"), None),
            P("dp"),
            P("dp", None),
            P(None, "dp"),
            P("dp"),
            P("dp"),
            P("dp"),
            P("dp"),
            P("dp"),
            P("dp", None),
            P(("dp", "seq"), None),
        ),
        out_specs=(
            P(("dp", "seq"), None),
            P(("dp", "seq"), None),
            P("dp"),
            P("dp", None),
            P(None, "dp"),
            P("dp"),
            P("dp"),
            P("dp"),
            P("dp"),
            P("dp"),
            P("dp", None),
        ),
        check_vma=False,
    )
```

profile of v0, /device:TPU:0, one launch (start us, length us, event | category | flops | bytes accessed | tf_op | source)
XLA Modules:
  0.0 1092.2 jit_solution(7979534498139653313)
XLA Ops:
  8.0 5.3 all-gather
  13.4 111.9 %all-gather.8.cloned.1.call-done = bf16[1024,4384]{0,1:T(8,128)(2,1)} async-done(((bf16[512,4384]{0,1:T(8,128)(2,1)}), bf16[1024,4384]{0,1:T(8,128)(2,1)}) %all-gather.8.cloned.1.call-update) | async-done | bytes 8978448 | tf_op jit(solution)/shard_map/all_gather | solution.py:121
  125.3 6.1 convolution_convert_fusion
  133.0 4.3 all-gather.1
  137.9 5.6 all-to-all-start
  145.6 4.9 all-reduce.26
  150.5 4.4 all_gather.41
  157.2 6.2 all-to-all-start.1
  164.9 13.1 %all-to-all-done.1 = bf16[128,16,128]{2,0,1:T(8,128)(2,1)S(1)} async-done(((bf16[128,16,128]{2,0,1:T(8,128)(2,1)}), bf16[128,16,128]{2,0,1:T(8,128)(2,1)S(1)}, u32[]{:S(2)}, u32[]{:S(2)}) %all-to-all-start.1) | async-done | bytes 524320 | tf_op jit(solution)/shard_map/all_to_all | solution.py:146
  185.9 3.1 fusion.89
  192.1 2.7 copy.149
  195.8 75.2 %while.44 = (s32[]{:T(128)}, f32[2,64,128]{2,1,0:T(8,128)S(1)}, f32[8,256,2,64]{1,3,2,0:T(8,128)}, f32[8,2,64,128]{3,2,1,0:T(8,128)}, f32[8,256,2]{1,2,0:T(2,128...) while((s32[]{:T(128)}, f32[2,64,128]{2,1,0:T(8,128)S(1)}, ...), condition=%wide.region_4.5_spmd.clone.clone, body=%wide.region_1.4_spmd.clone.clone.sunk | while | flops 302892544 | bytes 2142528 | solution.py:69
  271.0 3.9 copy.138
  274.9 3.3 reshape.488
  280.4 4.6 all-to-all-start.2
  285.1 4.3 all_gather.44
  289.5 10.1 all-to-all-done.2
  301.5 4.2 multiply_reduce_fusion.8
  305.7 2.9 fusion.96
  310.7 4.1 all-to-all-start.3
  315.8 13.5 %all-to-all-done.3 = bf16[128,16,128]{2,0,1:T(8,128)(2,1)S(1)} async-done(((bf16[128,16,128]{2,0,1:T(8,128)(2,1)}), bf16[128,16,128]{2,0,1:T(8,128)(2,1)S(1)}, u32[]{:S(2)}, u32[]{:S(2)}) %all-to-all-start.3) | async-done | bytes 524320 | tf_op jit(solution)/shard_map/all_to_all | solution.py:192
  330.5 3.3 reshape.489
  333.8 3.9 copy.123
  341.5 173.5 %while.43 = (s32[]{:T(128)}, f32[2]{0:T(128)}, f32[2,64,128]{2,1,0:T(8,128)S(1)}, f32[8,256,2,64]{1,3,2,0:T(8,128)}, f32[8,256,2]{1,2,0:T(2,128)}, /*index=5*/f3...) while((s32[]{:T(128)}, f32[2]{0:T(128)}, ...), condition=%wide.region_20.21_spmd.clone, body=%wide.region_7.20_spmd.clone.sunk | while | flops 758179328 | bytes 7921532 | solution.py:69
  372.9 2.5 reduce-window.74
  394.6 2.5 reduce-window.74
  416.3 2.5 reduce-window.74
  459.7 2.5 reduce-window.74
  481.4 2.5 reduce-window.74
  503.1 2.5 reduce-window.74
  515.0 2.7 copy.143
  520.3 4.7 multiply_reduce_fusion.6
  529.1 4.7 fusion.131
  537.4 3.5 reshape.490
  540.9 3.5 multiply_reduce_fusion.11
  545.9 4.2 all-to-all-start.4
  550.9 16.4 %all-to-all-done.4 = bf16[16,128,128]{2,1,0:T(8,128)(2,1)S(1)} async-done(((bf16[16,128,128]{2,1,0:T(8,128)(2,1)}), bf16[16,128,128]{2,1,0:T(8,128)(2,1)S(1)}, u32[]{:S(2)}, u32[]{:S(2)}) %all-to-all-start.4) | async-done | bytes 524320 | tf_op jit(solution)/shard_map/all_to_all | solution.py:208
  567.4 5.4 all-to-all-start.5
  573.1 13.7 %reduce-scatter.10.cloned.1.call-done = bf16[128,256]{1,0:T(8,128)(2,1)} async-done(((bf16[2048,256]{1,0:T(8,128)(2,1)}), bf16[128,256]{1,0:T(8,128)(2,1)}) %reduce-scatter.10.cloned.1.call-update) | async-done | bytes 65552
  587.8 8.0 fusion.110
  595.8 141.3 %reduce-scatter.8.cloned.1.call-done = f32[64,1024]{1,0:T(8,128)} async-done(((f32[2048,1024]{1,0:T(8,128)}), f32[64,1024]{1,0:T(8,128)}) %reduce-scatter.8.cloned.1.call-update) | async-done | bytes 262160 | tf_op jit(solution)/shard_map/reduce_scatter | solution.py:239
  737.2 194.9 %reduce-scatter.6.cloned.1.call-done = f32[32,4384]{1,0:T(8,128)} async-done(((f32[1024,4384]{1,0:T(8,128)}), f32[32,4384]{1,0:T(8,128)}) %reduce-scatter.6.cloned.1.call-update) | async-done | bytes 561168 | tf_op jit(solution)/shard_map/reduce_scatter | solution.py:238
  932.3 4.1 fusion.90
  938.0 5.1 fusion.106
  943.1 47.0 %all-reduce.25 = (f32[1024]{0:T(1024)S(1)}, f32[4,2304]{1,0:T(4,128)S(1)}, f32[2304]{0:T(1024)S(1)}, f32[32]{0:T(128)S(1)}, f32[32]{0:T(128)S(1)}, /*index=5*/f32[32]{0:T(128)S(1)}, f32[2048]{0:T(1024)S(1)}) all-reduce(f32[1024]{0:T(1024)S(1)} %get-tuple-element.697, ...), channel_id=1, replica_groups=mesh['dp'=2,'seq'=16] {'dp','seq'}, use_global_device_ids=true, to_apply=%region_24.25 | all-reduce | flops 14688 | bytes 117504 | tf_op jit(solution)/shard_map/psum | solution.py:245
  995.4 75.6 %all-gather.14.cloned.1.call-done = f32[512,4384]{1,0:T(8,128)} async-done(((f32[32,4384]{1,0:T(8,128)}), f32[512,4384]{1,0:T(8,128)}) %all-gather.14.cloned.1.call-update) | async-done | bytes 8978448 | tf_op jit(solution)/shard_map/all_gather | solution.py:242
  1071.0 9.4 copy.130
  1080.5 4.8 copy.253
  (786 shorter events, 284.6 us)
Async XLA Ops:
  7.2 118.1 %all-gather.8.cloned.1.call-start = ((), (), s32[]{:S(2)}) async-start(), calls=%async_computation.9 | async-start | bytes 13467648 | tf_op jit(solution)/shard_map/all_gather | solution.py:121
  7.9 176.3 %all-gather.10.cloned.1.call-start = ((), (), s32[]{:S(2)}) async-start(), calls=%async_computation.10 | async-start | bytes 1114112 | tf_op jit(solution)/shard_map/all_gather | solution.py:149
  13.4 118.0 %copy-start.65 = (f32[128]{0:T(128)}, f32[128]{0:T(128)S(1)}, u32[]{:S(2)}) copy-start(f32[128]{0:T(128)S(1)} %fusion.108) | copy-start | bytes 1540
  13.4 118.0 %copy-start.27 = (f32[128]{0:T(128)}, f32[128]{0:T(128)S(1)}, u32[]{:S(2)}) copy-start(f32[128]{0:T(128)S(1)} %fusion.126) | copy-start | bytes 1540
  131.5 25.7 %copy-start.7 = (bf16[128,4384]{0,1:T(8,128)(2,1)}, bf16[128,4384]{0,1:T(8,128)(2,1)S(1)}, u32[]{:S(2)}) copy-start(bf16[128,4384]{0,1:T(8,128)(2,1)S(1)} %convolution_convert_fusion) | copy-start | bytes 3366916
  131.5 12.1 %copy-start.75 = (u32[32]{0:T(128)S(1)}, u32[32]{0:T(128)}, u32[]{:S(2)}) copy-start(u32[32]{0:T(128)} %constant.205) | copy-start | bytes 388
  131.5 13.4 %copy-start.72 = (bf16[16]{0:T(256)(128)(2,1)S(1)}, bf16[16]{0:T(256)(128)(2,1)}, u32[]{:S(2)}) copy-start(bf16[16]{0:T(256)(128)(2,1)} %param.20) | copy-start | bytes 100
  131.5 13.6 %copy-start.73 = (bf16[16]{0:T(256)(128)(2,1)S(1)}, bf16[16]{0:T(256)(128)(2,1)}, u32[]{:S(2)}) copy-start(bf16[16]{0:T(256)(128)(2,1)} %param.22) | copy-start | bytes 100
  131.5 13.8 %copy-start.74 = (bf16[16]{0:T(256)(128)(2,1)S(1)}, bf16[16]{0:T(256)(128)(2,1)}, u32[]{:S(2)}) copy-start(bf16[16]{0:T(256)(128)(2,1)} %param.21) | copy-start | bytes 100
  131.5 19.0 %copy-start.43 = (bf16[4,1152]{1,0:T(4,128)(2,1)S(1)}, bf16[4,1152]{1,0:T(4,128)(2,1)}, u32[]{:S(2)}) copy-start(bf16[4,1152]{1,0:T(4,128)(2,1)} %param.18) | copy-start | bytes 27652
  132.2 169.3 %all-gather.12.cloned.1.call-start = ((), (), s32[]{:S(2)}) async-start(), calls=%async_computation.11 | async-start | bytes 6291456 | tf_op jit(solution)/shard_map/all_gather | solution.py:128
  137.9 19.3 %all-to-all-start = ((bf16[128,16,2]{0,2,1:T(2,128)(2,1)}), bf16[128,16,2]{0,2,1:T(2,128)(2,1)S(1)}, u32[]{:S(2)}, u32[]{:S(2)}) async-start(bf16[128,16,2]{0,2,1:T(2,128)(2,1)} %bitcast.3), calls=%async_computation | async-start | bytes 16384 | tf_op jit(solution)/shard_map/all_to_all | solution.py:147
  150.5 27.7 %copy-start.69 = (f32[32]{0:T(128)}, f32[32]{0:T(128)S(1)}, u32[]{:S(2)}) copy-start(f32[32]{0:T(128)S(1)} %convert_element_type.120) | copy-start | bytes 388
  155.1 23.1 %copy-start.44 = (f32[2]{0:T(128)}, f32[2]{0:T(128)S(1)}, u32[]{:S(2)}) copy-start(f32[2]{0:T(128)S(1)} %dynamic_slice.118) | copy-start | bytes 28
  157.2 23.7 %copy-start.23 = (bf16[128,16,2]{0,2,1:T(2,128)(2,1)}, bf16[128,16,2]{0,2,1:T(2,128)(2,1)S(1)}, u32[]{:S(2)}) copy-start(bf16[128,16,2]{0,2,1:T(2,128)(2,1)S(1)} %all-to-all-done) | copy-start | bytes 24580
  157.2 20.9 %all-to-all-start.1 = ((bf16[128,16,128]{2,0,1:T(8,128)(2,1)}), bf16[128,16,128]{2,0,1:T(8,128)(2,1)S(1)}, u32[]{:S(2)}, u32[]{:S(2)}) async-start(bf16[128,16,128]{2,0,1:T(8,128)(2,1)} %copy.109), calls=%async_computation.1 | async-start | bytes 1048576 | tf_op jit(solution)/shard_map/all_to_all | solution.py:146
  164.1 16.8 %copy-start.46 = (f32[128]{0:T(128)}, f32[128]{0:T(128)S(1)}, u32[]{:S(2)}) copy-start(f32[128]{0:T(128)S(1)} %get-tuple-element.796) | copy-start | bytes 1540
  164.1 16.8 %copy-start.48 = (f32[128]{0:T(128)}, f32[128]{0:T(128)S(1)}, u32[]{:S(2)}) copy-start(f32[128]{0:T(128)S(1)} %get-tuple-element.797) | copy-start | bytes 1540
  164.1 16.8 %copy-start.50 = (f32[128]{0:T(128)}, f32[128]{0:T(128)S(1)}, u32[]{:S(2)}) copy-start(f32[128]{0:T(128)S(1)} %get-tuple-element.798) | copy-start | bytes 1540
  164.1 16.8 %copy-start.52 = (f32[128]{0:T(128)}, f32[128]{0:T(128)S(1)}, u32[]{:S(2)}) copy-start(f32[128]{0:T(128)S(1)} %get-tuple-element.799) | copy-start | bytes 1540
  164.2 21.7 %copy-start.35 = (f32[1,256]{1,0:T(1,128)}, f32[1,256]{1,0:T(1,128)S(1)}, u32[]{:S(2)}) copy-start(f32[1,256]{1,0:T(1,128)S(1)} %get-tuple-element.792) | copy-start | bytes 3076
  164.2 21.7 %copy-start.37 = (f32[1,256]{1,0:T(1,128)}, f32[1,256]{1,0:T(1,128)S(1)}, u32[]{:S(2)}) copy-start(f32[1,256]{1,0:T(1,128)S(1)} %get-tuple-element.793) | copy-start | bytes 3076
  164.2 21.7 %copy-start.39 = (f32[1,256]{1,0:T(1,128)}, f32[1,256]{1,0:T(1,128)S(1)}, u32[]{:S(2)}) copy-start(f32[1,256]{1,0:T(1,128)S(1)} %get-tuple-element.794) | copy-start | bytes 3076
  164.2 21.7 %copy-start.41 = (f32[1,256]{1,0:T(1,128)}, f32[1,256]{1,0:T(1,128)S(1)}, u32[]{:S(2)}) copy-start(f32[1,256]{1,0:T(1,128)S(1)} %get-tuple-element.795) | copy-start | bytes 3076
  164.2 16.7 %copy-start.19 = (f32[128,16,2]{0,2,1:T(2,128)}, f32[128,16,2]{0,2,1:T(2,128)S(1)}, u32[]{:S(2)}) copy-start(f32[128,16,2]{0,2,1:T(2,128)S(1)} %convert_element_type.151) | copy-start | bytes 49156
  180.9 97.4 %copy-start.2 = (f32[2048,128]{1,0:T(8,128)}, f32[2048,128]{1,0:T(8,128)S(1)}, u32[]{:S(2)}) copy-start(f32[2048,128]{1,0:T(8,128)S(1)} %get-tuple-element.765) | copy-start | bytes 3145732
  280.4 19.1 %all-to-all-start.2 = ((bf16[16,128,128]{2,1,0:T(8,128)(2,1)}), bf16[16,128,128]{2,1,0:T(8,128)(2,1)S(1)}, u32[]{:S(2)}, u32[]{:S(2)}) async-start(bf16[16,128,128]{2,1,0:T(8,128)(2,1)} %bitcast.20), calls=%async_computation.2 | async-start | bytes 1048576 | tf_op jit(solution)/shard_map/all_to_all | solution.py:176
  289.5 16.3 %copy-start.16 = (f32[2048]{0:T(1024)}, f32[2048]{0:T(1024)S(1)}, u32[]{:S(2)}) copy-start(f32[2048]{0:T(1024)S(1)} %convert_element_type.133) | copy-start | bytes 24580
  310.7 18.6 %all-to-all-start.3 = ((bf16[128,16,128]{2,0,1:T(8,128)(2,1)}), bf16[128,16,128]{2,0,1:T(8,128)(2,1)S(1)}, u32[]{:S(2)}, u32[]{:S(2)}) async-start(bf16[128,16,128]{2,0,1:T(8,128)(2,1)} %copy.118), calls=%async_computation.3 | async-start | bytes 1048576 | tf_op jit(solution)/shard_map/all_to_all | solution.py:192
  314.8 272.0 %reduce-scatter.10.cloned.1.call-start = ((), (), s32[]{:S(2)}) async-start(), calls=%async_computation.16 | async-start | bytes 1114112
  354.1 7.7 copy-start.15
  375.8 7.7 copy-start.15
  397.4 7.7 copy-start.15
  419.1 7.7 copy-start.15
  440.8 7.7 copy-start.15
  462.5 7.7 copy-start.15
  484.2 7.7 copy-start.15
  505.9 7.7 copy-start.15
  528.7 208.5 %reduce-scatter.8.cloned.1.call-start = ((), (), s32[]{:S(2)}) async-start(), calls=%async_computation.14 | async-start | bytes 8650752 | tf_op jit(solution)/shard_map/reduce_scatter | solution.py:239
  545.9 41.9 %copy-start.14 = (bf16[128,2048]{0,1:T(8,128)(2,1)S(1)}, bf16[128,2048]{0,1:T(8,128)(2,1)}, u32[]{:S(2)}) copy-start(bf16[128,2048]{0,1:T(8,128)(2,1)} %get-tuple-element.779) | copy-start | bytes 1572868
  545.9 41.9 %copy-start.28 = (f32[128]{0:T(128)S(1)}, f32[128]{0:T(128)}, u32[]{:S(2)}) copy-start(f32[128]{0:T(128)} %copy-done.27) | copy-start | bytes 1540
  545.9 21.4 %all-to-all-start.4 = ((bf16[16,128,128]{2,1,0:T(8,128)(2,1)}), bf16[16,128,128]{2,1,0:T(8,128)(2,1)S(1)}, u32[]{:S(2)}, u32[]{:S(2)}) async-start(bf16[16,128,128]{2,1,0:T(8,128)(2,1)} %bitcast.441), calls=%async_computation.4 | async-start | bytes 1048576 | tf_op jit(solution)/shard_map/all_to_all | solution.py:208
  567.4 20.4 %all-to-all-start.5 = ((bf16[16,128,2]{1,2,0:T(2,128)(2,1)}), bf16[16,128,2]{1,2,0:T(2,128)(2,1)S(1)}, u32[]{:S(2)}, u32[]{:S(2)}) async-start(bf16[16,128,2]{1,2,0:T(2,128)(2,1)} %fusion.124), calls=%async_computation.5 | async-start | bytes 16384 | tf_op jit(solution)/shard_map/all_to_all | solution.py:211
  572.7 359.4 %reduce-scatter.6.cloned.1.call-start = ((), (), s32[]{:S(2)}) async-start(), calls=%async_computation.12 | async-start | bytes 18923520 | tf_op jit(solution)/shard_map/reduce_scatter | solution.py:238
  595.8 399.6 %all-gather.16.cloned.1.call-start = ((), (), s32[]{:S(2)}) async-start(), calls=%async_computation.15 | async-start | bytes 4456448 | tf_op jit(solution)/shard_map/all_gather | solution.py:243
  737.2 333.8 %all-gather.14.cloned.1.call-start = ((), (), s32[]{:S(2)}) async-start(), calls=%async_computation.13 | async-start | bytes 9748480 | tf_op jit(solution)/shard_map/all_gather | solution.py:242
  938.0 55.8 %copy-start.66 = (f32[128]{0:T(128)S(1)}, f32[128]{0:T(128)}, u32[]{:S(2)}) copy-start(f32[128]{0:T(128)} %copy-done.65) | copy-start | bytes 1540
  938.0 56.4 %copy-start.13 = (bf16[128,1024]{1,0:T(8,128)(2,1)S(1)}, bf16[128,1024]{1,0:T(8,128)(2,1)}, u32[]{:S(2)}) copy-start(bf16[128,1024]{1,0:T(8,128)(2,1)} %param.25) | copy-start | bytes 786436
  (85 other events, 311.0 us)
Sparse Core Ops, SparseCore 0:
  9.6 115.6 all-gather.7
  132.3 39.9 all-gather.9
  173.8 56.6 all-gather.11
  528.8 57.9 reduce-scatter.9
  589.6 147.4 reduce-scatter.7
  739.5 192.5 reduce-scatter.5
  934.3 56.0 all-gather.15
  992.6 78.3 all-gather.13
where the time goes:
time: 1100 us; the launch traced here: 1090 us
  waiting for transfers between devices  592 us (54%)
  matrix products  155 us (14%)
  local copies, waits for them, and re-layouts  116 us (11%)
  other arithmetic  111 us (10%)
  blocking collectives  70.2 us (6%)
  starting transfers between devices  31.1 us (3%)
  between operations  16 us (1%)
    reduce_scatter x1, waiting for transfers between devices, local(): lax.psum_scatter(in_grad, ('dp', 'seq'), scatter_dimension=0, tiled=True)  195 us
    reduce_scatter x1, waiting for transfers between devices, local(): lax.psum_scatter(out_grad, ('dp', 'seq'), scatter_dimension=0, tiled=True)  141 us
    all_gather x1, waiting for transfers between devices, local(): lax.all_gather(in_weight, 'dp', axis=0, tiled=True)  112 us
    all_gather x1, waiting for transfers between devices, local(): lax.all_gather(in_part, 'seq', axis=0, tiled=True)  75.6 us
    dot_general x24, matrix products, one_block(): inside = jnp.einsum('hts,shp->thp', weights, val_blk, precision=highest)  48.4 us
    psum x1, blocking collectives, local(): lax.psum((gain_grad, taps_grad, offset_grad, shift_grad, rates_grad, skip...  47 us
    another operation x50, other arithmetic  37.1 us
    dot_general x32, matrix products, one_block(): scores = jnp.dot(query_blk, key_blk.T, precision=highest)  31.6 us
  transfers between devices with their start and end apart: 14, of which 9 were waited for; matrix products, arithmetic and copies ran while one was open for 14% of the time, Pallas kernels for 0%

commit v1 on v0

v1 whole, which is shorter than its diff:
```python
import jax
import jax.numpy as jnp
from jax import lax
from jax.experimental import pallas as pl
from jax.experimental.pallas import tpu as pltpu
from jax.sharding import Mesh
from jax.sharding import PartitionSpec as P

BLOCK = 256
PRE = 16
LANES = 128
EPS = 1e-05
HIGHEST = lax.Precision.HIGHEST
F32 = jnp.float32
BF16 = jnp.bfloat16


def mm(a, b, da=1, db=0):
    return lax.dot_general(a, b, (((da,), (db,)), ((), ())), preferred_element_type=F32)


def mm_exact(a, b, da=1, db=0):
    return lax.dot_general(
        a, b, (((da,), (db,)), ((), ())), precision=HIGHEST, preferred_element_type=F32
    )


def iota(shape, dim):
    return lax.broadcasted_iota(jnp.int32, shape, dim)


def head_map(channels, hdim):
    return (jnp.right_shift(iota((LANES, channels), 1), hdim.bit_length() - 1) == iota((LANES, channels), 0)).astype(F32)


def unit(u):
    return u * lax.rsqrt(jnp.mean(u * u, axis=-1, keepdims=True) + EPS)


def sigmoid(v):
    return jax.nn.sigmoid(v)


def softplus(v):
    return jnp.maximum(v, 0.0) + jnp.log1p(jnp.exp(-jnp.abs(v)))


def masked(values, head, hdim):
    lanes = iota(values.shape, 1)
    own = (lanes >= head * hdim) & (lanes < (head + 1) * hdim)
    return jnp.where(own, values, jnp.zeros_like(values))


def front_kernel(hdim, x_ref, halo_ref, gain_ref, w_ref, cw_ref, cb_ref, sb_ref, rate_ref,
                 normed_ref, z_ref, raw_ref, pre_ref, xs_ref, kq_ref, dtb_ref, cums_ref,
                 stin_ref, cd_ref, fin_ref, dtot_ref, buf, st, cd):
    step_id = pl.program_id(0)
    ch = z_ref.shape[1]
    conv_ch = pre_ref.shape[1]
    gain = gain_ref[...]

    @pl.when(step_id == 0)
    def _():
        hn = (unit(halo_ref[...].astype(F32)) * gain).astype(BF16)
        hp = mm(hn, w_ref[:, ch : ch + conv_ch])
        buf[0:PRE, :] = hp.astype(BF16).astype(F32)
        st[...] = jnp.zeros_like(st)
        cd[...] = jnp.ones_like(cd)

    @pl.when(step_id > 0)
    def _():
        buf[0:PRE, :] = buf[BLOCK : BLOCK + PRE, :]

    normed = (unit(x_ref[...].astype(F32)) * gain).astype(BF16)
    normed_ref[...] = normed
    proj = mm(normed, w_ref[...])
    z_ref[...] = proj[:, :ch].astype(BF16)
    buf[PRE : PRE + BLOCK, :] = proj[:, ch : ch + conv_ch].astype(BF16).astype(F32)
    raw_ref[0] = buf[...].astype(BF16)
    pre = cb_ref[0:1, :] + cw_ref[0:1, :] * buf[PRE - 3 : PRE - 3 + BLOCK, :]
    for k in range(1, 4):
        pre = pre + cw_ref[k : k + 1, :] * buf[PRE - 3 + k : PRE - 3 + k + BLOCK, :]
    pre_ref[...] = pre
    act = pre * sigmoid(pre)
    dtb = proj[:, ch + conv_ch :].astype(BF16).astype(F32) + sb_ref[0:1, :]
    dtb_ref[...] = dtb
    step = softplus(dtb)
    logs = step * rate_ref[0:1, :]
    lower = (iota((BLOCK, BLOCK), 0) >= iota((BLOCK, BLOCK), 1)).astype(F32)
    cums = mm_exact(lower, logs)
    cums_ref[...] = cums
    hmap = head_map(ch, hdim)
    cums_b = mm_exact(cums, hmap)
    xs = act[:, :ch] * mm_exact(step, hmap)
    xs_ref[...] = xs.astype(BF16)
    kq = act[:, ch:].astype(BF16)
    kq_ref[...] = kq
    last = cums_b[BLOCK - 1 : BLOCK, :]
    tail = jnp.exp(last - cums_b)
    update = mm(kq[:, : kq.shape[1] // 2], (xs * tail).astype(BF16), 0, 0)
    stin_ref[0] = st[...]
    cd_ref[0] = cd[...]
    decay = jnp.exp(last)
    st[...] = st[...] * decay + update
    cd[...] = cd[...] * decay
    fin_ref[...] = st[...]
    dtot_ref[...] = cd[...]


def decay_of(cums, cums_t, head, keep):
    spread = cums[:, head : head + 1] - cums_t[head : head + 1, :]
    return jnp.where(keep, jnp.exp(jnp.where(keep, spread, 0.0)), 0.0)


def intra_kernel(hdim, heads, kq_ref, xs_ref, cums_ref, out_ref):
    ns = kq_ref.shape[1] // 2
    keys, queries = kq_ref[:, :ns], kq_ref[:, ns:]
    scores = mm(queries, keys, 1, 1)
    cums = cums_ref[...]
    cums_t = cums.T
    xs = xs_ref[...]
    keep = iota((BLOCK, BLOCK), 0) >= iota((BLOCK, BLOCK), 1)
    total = jnp.zeros(xs.shape, F32)
    for h in range(heads):
        v = (scores * decay_of(cums, cums_t, h, keep)).astype(BF16)
        total = total + mm(v, masked(xs, h, hdim))
    out_ref[...] = total


def gate_kernel(hdim, kq_ref, cums_ref, ins_ref, pre_ref, z_ref, stin_ref, cd_ref, s0_ref,
                skip_ref, gain_ref, ow_ref, c_ref, mo_ref, a_ref, y_ref, stat_ref):
    ns = kq_ref.shape[1] // 2
    ch = ins_ref.shape[1]
    hmap = head_map(ch, hdim)
    st = stin_ref[0] + cd_ref[0, 0:1, :] * s0_ref[...]
    expc = jnp.exp(mm_exact(cums_ref[...], hmap))
    carried = expc * mm(kq_ref[:, ns:], st.astype(BF16))
    px = pre_ref[...]
    xc = px * sigmoid(px)
    mo = (ins_ref[...] + carried + skip_ref[0:1, :] * xc).astype(BF16)
    mo_ref[...] = mo
    zf = z_ref[...].astype(F32)
    gated = mo.astype(F32) * (zf * sigmoid(zf))
    gain = gain_ref[0:1, :]
    y_ref[...] = mm((gated * gain).astype(BF16), ow_ref[...]).astype(BF16)
    a = mm(c_ref[...], ow_ref[...], 1, 1) * gain
    a_ref[...] = a.astype(BF16)
    sq = jnp.sum(gated * gated, axis=1, keepdims=True)
    pj = jnp.sum(gated * a, axis=1, keepdims=True)
    lanes = iota((BLOCK, LANES), 1)
    both = jnp.where(lanes == 0, sq, jnp.where(lanes == 1, pj, 0.0))
    stat_ref[...] = both.T[:8, :]


def back_gate_kernel(hdim, inner, stat_ref, mo_ref, a_ref, z_ref, c_ref, normed_ref, gain_ref, kq_ref, cums_ref,
                     do_ref, dz_ref, og_ref, gz_ref, gg_ref, dst_ref, rd_ref, g0_ref, dst, rd):
    step_id = pl.program_id(0)
    ns = kq_ref.shape[1] // 2
    ch = mo_ref.shape[1]

    @pl.when(step_id == 0)
    def _():
        dst[...] = jnp.zeros_like(dst)
        rd[...] = jnp.ones_like(rd)
        og_ref[...] = jnp.zeros_like(og_ref)
        gz_ref[...] = jnp.zeros_like(gz_ref)
        gg_ref[...] = jnp.zeros_like(gg_ref)

    stat = jnp.concatenate([stat_ref[...], jnp.zeros((LANES - 8, BLOCK), F32)], axis=0).T
    r = lax.rsqrt(stat[:, 0:1] * (1.0 / inner) + EPS)
    pj = stat[:, 1:2] * (1.0 / inner)
    mo = mo_ref[...].astype(F32)
    zf = z_ref[...].astype(F32)
    sz = sigmoid(zf)
    silu = zf * sz
    gated = mo * silu
    a = a_ref[...].astype(F32)
    n = gated * r
    gg_ref[0:1, :] += jnp.sum(a * n, axis=0, keepdims=True)
    dgated = r * (a - n * (r * pj))
    og_ref[...] += mm((n * gain_ref[0:1, :]).astype(BF16), c_ref[...], 0, 0)
    do = (dgated * silu).astype(BF16)
    do_ref[...] = do
    dz = (dgated * mo * (sz * (1.0 + zf * (1.0 - sz)))).astype(BF16)
    dz_ref[...] = dz
    gz_ref[...] += mm(normed_ref[...], dz, 0, 0)
    cums_b = mm_exact(cums_ref[...], head_map(ch, hdim))
    dst_ref[0] = dst[...]
    rd_ref[0] = rd[...]
    decay = jnp.exp(cums_b[BLOCK - 1 : BLOCK, :])
    carry = mm(kq_ref[:, ns:], (do.astype(F32) * jnp.exp(cums_b)).astype(BF16), 0, 0)
    dst[...] = dst[...] * decay + carry
    rd[...] = rd[...] * decay
    g0_ref[...] = dst[...]


def back_intra_kernel(hdim, heads, kq_ref, xs_ref, cums_ref, do_ref, dxs_ref, dkq_ref, str_ref):
    ns = kq_ref.shape[1] // 2
    keys, queries = kq_ref[:, :ns], kq_ref[:, ns:]
    scores = mm(queries, keys, 1, 1)
    cums = cums_ref[...]
    cums_t = cums.T
    xs, do = xs_ref[...], do_ref[...]
    rows, cols = iota((BLOCK, BLOCK), 0), iota((BLOCK, BLOCK), 1)
    keep = rows >= cols
    before = (rows < cols).astype(BF16)
    dxs = jnp.zeros(xs.shape, F32)
    ds = jnp.zeros((BLOCK, BLOCK), F32)
    stri = jnp.zeros((LANES, BLOCK), F32)
    lane_rows = iota((LANES, BLOCK), 0)
    for h in range(heads):
        dec = decay_of(cums, cums_t, h, keep)
        v = scores * dec
        doh = masked(do, h, hdim)
        dxs = dxs + mm(v.astype(BF16), doh, 0, 0)
        dv = mm(doh, xs, 1, 1)
        ds = ds + dv * dec
        left = mm((dv * v).astype(BF16), before)
        line = jnp.sum(jnp.where(keep, left, 0.0), axis=0, keepdims=True)
        stri = jnp.where(lane_rows == h, line, stri)
    dsl = ds.astype(BF16)
    dxs_ref[...] = dxs
    dkq_ref[:, :ns] = mm(dsl, queries, 0, 0)
    dkq_ref[:, ns:] = mm(dsl, keys)
    str_ref[...] = stri.T


def back_kernel(hdim, kq_ref, xs_ref, cums_ref, dtb_ref, pre_ref, raw_ref, do_ref, dxs_ref, dkq_ref, str_ref,
                stin_ref, cd_ref, s0_ref, dst_ref, rd_ref, inc_ref, skip_ref, cw_ref, rate_ref,
                dx_ref, ddt_ref, halo_ref, cg_ref, hg_ref, buf, rbuf):
    step_id = pl.program_id(0)
    ns = kq_ref.shape[1] // 2
    ch = xs_ref.shape[1]

    @pl.when(step_id == 0)
    def _():
        cg_ref[...] = jnp.zeros_like(cg_ref)
        hg_ref[...] = jnp.zeros_like(hg_ref)
        buf[0:PRE, :] = jnp.zeros_like(buf[0:PRE, :])
        buf[PRE + BLOCK :, :] = jnp.zeros_like(buf[PRE + BLOCK :, :])

    @pl.when(step_id > 0)
    def _():
        buf[PRE + BLOCK :, :] = buf[PRE : 2 * PRE, :]

    hmap = head_map(ch, hdim)
    keys, queries = kq_ref[:, :ns], kq_ref[:, ns:]
    cums = cums_ref[...]
    cums_b = mm_exact(cums, hmap)
    expc = jnp.exp(cums_b)
    tail = jnp.exp(cums_b[BLOCK - 1 : BLOCK, :] - cums_b)
    st = stin_ref[0] + cd_ref[0, 0:1, :] * s0_ref[...]
    dst = dst_ref[0] + rd_ref[0, 0:1, :] * inc_ref[...]
    st_low, dst_low = st.astype(BF16), dst.astype(BF16)
    do = do_ref[...].astype(F32)
    xs = xs_ref[...].astype(F32)
    carried = expc * mm(queries, st_low)
    dq = dkq_ref[:, ns:] + mm((do * expc).astype(BF16), st_low, 1, 1)
    dxs_up = tail * mm(keys, dst_low)
    dk = dkq_ref[:, :ns] + mm((xs * tail).astype(BF16), dst_low, 1, 1)
    dxs = dxs_ref[...] + dxs_up
    px = pre_ref[:, :ch]
    xc = px * sigmoid(px)
    dtb = dtb_ref[...]
    step = softplus(dtb)
    rate = rate_ref[0:1, :]
    dxc = mm_exact(step, hmap) * dxs + skip_ref[0:1, :] * do
    dstep = mm_exact(xc * dxs, hmap, 1, 1)
    arr = mm_exact(do * carried, hmap, 1, 1)
    upd = mm_exact(xs * dxs_up, hmap, 1, 1)
    rows, cols = iota((BLOCK, BLOCK), 0), iota((BLOCK, BLOCK), 1)
    through = mm_exact(jnp.sum(st * dst, axis=0, keepdims=True) * jnp.ones((8, 1), F32), hmap, 1, 1)[0:1, :]
    dlogs = (
        str_ref[...]
        + mm_exact((cols >= rows).astype(F32), arr)
        + mm_exact((cols < rows).astype(F32), upd)
        + jnp.exp(cums[BLOCK - 1 : BLOCK, :]) * through
    )
    ddtb = (dstep + dlogs * rate) * sigmoid(dtb)
    ddt_ref[...] = ddtb.astype(BF16)
    dskip = mm_exact(do * xc, hmap, 1, 1)
    hg_ref[0:1, :] += jnp.sum(ddtb, axis=0, keepdims=True)
    hg_ref[1:2, :] += jnp.sum(dlogs * step, axis=0, keepdims=True) * rate
    hg_ref[2:3, :] += jnp.sum(dskip, axis=0, keepdims=True)
    pre = pre_ref[...]
    sp = sigmoid(pre)
    dpre = jnp.concatenate([dxc, dk, dq], axis=1) * (sp * (1.0 + pre * (1.0 - sp)))
    buf[PRE : PRE + BLOCK, :] = dpre
    rbuf[...] = raw_ref[0].astype(F32)
    cg_ref[4:5, :] += jnp.sum(dpre, axis=0, keepdims=True)
    dx = jnp.zeros_like(dpre)
    halo = jnp.zeros((PRE, dpre.shape[1]), F32)
    for k in range(4):
        tap = cw_ref[k : k + 1, :]
        dx = dx + tap * buf[PRE + 3 - k : PRE + 3 - k + BLOCK, :]
        halo = halo + tap * buf[3 - k : 3 - k + PRE, :]
        cg_ref[k : k + 1, :] += jnp.sum(
            dpre * rbuf[PRE - 3 + k : PRE - 3 + k + BLOCK, :], axis=0, keepdims=True
        )
    dx_ref[...] = dx.astype(BF16)
    halo_ref[...] = halo


def rows_of(width, rows=BLOCK, rev=None):
    if rev is None:
        return pl.BlockSpec((rows, width), lambda i: (i, 0))
    return pl.BlockSpec((rows, width), lambda i: (rev - 1 - i, 0))


def slabs_of(a, b, rev=None):
    if rev is None:
        return pl.BlockSpec((1, a, b), lambda i: (i, 0, 0))
    return pl.BlockSpec((1, a, b), lambda i: (rev - 1 - i, 0, 0))


def fixed(a, b):
    return pl.BlockSpec((a, b), lambda i: (0, 0))


def sds(shape, dtype=F32):
    return jax.ShapeDtypeStruct(shape, dtype)


def shifted(values, axis, size, by):
    pairs = [(i, i + by) for i in range(size) if 0 <= i + by < size]
    return lax.ppermute(values, axis, pairs)


def gather_dp(values, axis=0):
    return lax.all_gather(values, "dp", axis=axis, tiled=True)


def carry_over(state, decay, axis, size, way):
    total = None
    for j in range(size - 1, 0, -1):
        part = shifted(state, axis, size, way * j)
        if total is None:
            total = part
        else:
            total = part + shifted(decay, axis, size, way * j)[0:1, :] * total
    return jnp.zeros_like(state) if total is None else total


def local(layer_input, norm_gain, in_weight, conv_weight, conv_bias, step_bias, rate_log, skip_gain,
          gate_gain, out_weight, cotangent):
    dp, cp, tp = lax.axis_size("dp"), lax.axis_size("cp"), lax.axis_size("tp")
    d_id, k_id = lax.axis_index("dp"), lax.axis_index("tp")
    own_rows, width = layer_input.shape
    inner = out_weight.shape[0] * dp
    conv_all = conv_weight.shape[1] * dp
    heads = step_bias.shape[0] * dp
    hdim = inner // heads
    ns = (conv_all - inner) // 2
    lh = heads // tp
    ch = inner // tp
    conv_ch = ch + 2 * ns
    tokens = own_rows * tp
    nb = tokens // BLOCK
    cols = ch + conv_ch + LANES
    taps = conv_weight.shape[0]

    x_all = lax.all_gather(layer_input, "tp", axis=0, tiled=True)
    halo = lax.all_gather(shifted(layer_input[-PRE:], "cp", cp, 1), "tp", axis=0, tiled=True)[-PRE:]
    c_all = lax.all_gather(cotangent, "tp", axis=0, tiled=True)

    def cut(values, start, size, axis=1):
        return lax.dynamic_slice_in_dim(values, start, size, axis)

    own_cols = jnp.concatenate(
        [
            cut(in_weight, k_id * ch, ch),
            cut(in_weight, inner + k_id * ch, ch),
            in_weight[:, 2 * inner : 2 * inner + 2 * ns],
            cut(in_weight, inner + conv_all + k_id * lh, lh),
            jnp.zeros((in_weight.shape[0], LANES - lh), BF16),
        ],
        axis=1,
    )
    w = gather_dp(own_cols)
    share = tp // dp
    ow = lax.all_gather(cut(out_weight, (k_id % share) * ch, ch, 0), "dp", axis=0, tiled=False)
    ow = lax.dynamic_index_in_dim(ow, k_id // share, 0, keepdims=False)
    taps_all = gather_dp(conv_weight, 1).astype(F32)
    small = gather_dp(
        jnp.concatenate([norm_gain, conv_bias, gate_gain, step_bias, rate_log, skip_gain])[None], 0
    ).astype(F32)
    widths = [width, conv_all, inner, heads, heads, heads]
    pieces, at = [], 0
    for size in widths:
        pieces.append(small[:, at : at + size // dp].reshape(-1))
        at += size // dp
    gain, offset, ggain, sbias, rlog, skip = pieces

    def own_conv(values):
        return jnp.concatenate([cut(values, k_id * ch, ch), values[:, inner:]], axis=1)

    def pad8(values):
        return jnp.pad(values, ((0, 8 - values.shape[0]), (0, 0)))

    def head_row(values):
        return jnp.pad(cut(values[None], k_id * lh, lh), ((0, 7), (0, LANES - lh)))

    cw = pad8(own_conv(taps_all))
    cb = pad8(own_conv(offset[None]))
    sb = head_row(sbias)
    rate = head_row(-jnp.exp(rlog))
    skip_b = pad8(jnp.repeat(cut(skip[None], k_id * lh, lh), hdim, axis=1))
    own_gate = pad8(cut(ggain[None], k_id * ch, ch))
    gain_row = gain[None]

    def params(**kw):
        return pltpu.CompilerParams(dimension_semantics=("arbitrary",), **kw)

    normed, z, raw, pre, xs, kq, dtb, cums, stin, cd, fin, dtot = pl.pallas_call(
        lambda *refs: front_kernel(hdim, *refs),
        grid=(nb,),
        in_specs=[rows_of(width), fixed(PRE, width), fixed(1, width), fixed(width, cols), fixed(8, conv_ch),
                  fixed(8, conv_ch), fixed(8, LANES), fixed(8, LANES)],
        out_specs=[rows_of(width), rows_of(ch), slabs_of(PRE + BLOCK, conv_ch), rows_of(conv_ch), rows_of(ch),
                   rows_of(2 * ns), rows_of(LANES), rows_of(LANES), slabs_of(ns, ch), slabs_of(8, ch),
                   fixed(ns, ch), fixed(8, ch)],
        out_shape=[sds((tokens, width), BF16), sds((tokens, ch), BF16), sds((nb, PRE + BLOCK, conv_ch), BF16),
                   sds((tokens, conv_ch)), sds((tokens, ch), BF16), sds((tokens, 2 * ns), BF16),
                   sds((tokens, LANES)), sds((tokens, LANES)), sds((nb, ns, ch)), sds((nb, 8, ch)),
                   sds((ns, ch)), sds((8, ch))],
        scratch_shapes=[pltpu.VMEM((PRE + BLOCK, conv_ch), F32), pltpu.VMEM((ns, ch), F32), pltpu.VMEM((8, ch), F32)],
        compiler_params=params(),
        name="front",
    )(x_all, halo, gain_row, w, cw, cb, sb, rate)

    s0 = carry_over(fin, dtot, "cp", cp, 1)

    inside = pl.pallas_call(
        lambda *refs: intra_kernel(hdim, lh, *refs),
        grid=(nb,),
        in_specs=[rows_of(2 * ns), rows_of(ch), rows_of(LANES)],
        out_specs=rows_of(ch),
        out_shape=sds((tokens, ch)),
        compiler_params=params(),
        name="intra",
    )(kq, xs, cums)

    mo, a, y, stat = pl.pallas_call(
        lambda *refs: gate_kernel(hdim, *refs),
        grid=(nb,),
        in_specs=[rows_of(2 * ns), rows_of(LANES), rows_of(ch), rows_of(ch), rows_of(ch), slabs_of(ns, ch),
                  slabs_of(8, ch), fixed(ns, ch), fixed(8, ch), fixed(8, ch), fixed(ch, width), rows_of(width)],
        out_specs=[rows_of(ch), rows_of(ch), rows_of(width), pl.BlockSpec((8, BLOCK), lambda i: (0, i))],
        out_shape=[sds((tokens, ch), BF16), sds((tokens, ch), BF16), sds((tokens, width), BF16), sds((8, tokens))],
        compiler_params=params(),
        name="gate",
    )(kq, cums, inside, pre, z, stin, cd, s0, skip_b, own_gate, ow, c_all)

    stats = lax.psum(stat, "tp")

    do, dz, og, gz, gg, dstl, rd, g0 = pl.pallas_call(
        lambda *refs: back_gate_kernel(hdim, inner, *refs),
        grid=(nb,),
        in_specs=[pl.BlockSpec((8, BLOCK), lambda i: (0, nb - 1 - i)), rows_of(ch, rev=nb), rows_of(ch, rev=nb),
                  rows_of(ch, rev=nb), rows_of(width, rev=nb), rows_of(width, rev=nb), fixed(8, ch),
                  rows_of(2 * ns, rev=nb), rows_of(LANES, rev=nb)],
        out_specs=[rows_of(ch, rev=nb), rows_of(ch, rev=nb), fixed(ch, width), fixed(width, ch), fixed(8, ch),
                   slabs_of(ns, ch, nb), slabs_of(8, ch, nb), fixed(ns, ch)],
        out_shape=[sds((tokens, ch), BF16), sds((tokens, ch), BF16), sds((ch, width)), sds((width, ch)), sds((8, ch)),
                   sds((nb, ns, ch)), sds((nb, 8, ch)), sds((ns, ch))],
        scratch_shapes=[pltpu.VMEM((ns, ch), F32), pltpu.VMEM((8, ch), F32)],
        compiler_params=params(),
        name="back_gate",
    )(stats, mo, a, z, c_all, normed, own_gate, kq, cums)

    incoming = carry_over(g0, dtot, "cp", cp, -1)

    dxs, dkq, stri = pl.pallas_call(
        lambda *refs: back_intra_kernel(hdim, lh, *refs),
        grid=(nb,),
        in_specs=[rows_of(2 * ns), rows_of(ch), rows_of(LANES), rows_of(ch)],
        out_specs=[rows_of(ch), rows_of(2 * ns), rows_of(LANES)],
        out_shape=[sds((tokens, ch)), sds((tokens, 2 * ns)), sds((tokens, LANES))],
        compiler_params=params(),
        name="back_intra",
    )(kq, xs, cums, do)

    dxbc, ddt, dhalo, cg, hg = pl.pallas_call(
        lambda *refs: back_kernel(hdim, *refs),
        grid=(nb,),
        in_specs=[rows_of(2 * ns, rev=nb), rows_of(ch, rev=nb), rows_of(LANES, rev=nb), rows_of(LANES, rev=nb),
                  rows_of(conv_ch, rev=nb), slabs_of(PRE + BLOCK, conv_ch, nb), rows_of(ch, rev=nb),
                  rows_of(ch, rev=nb), rows_of(2 * ns, rev=nb), rows_of(LANES, rev=nb), slabs_of(ns, ch, nb),
                  slabs_of(8, ch, nb), fixed(ns, ch), slabs_of(ns, ch, nb), slabs_of(8, ch, nb), fixed(ns, ch),
                  fixed(8, ch), fixed(8, conv_ch), fixed(8, LANES)],
        out_specs=[rows_of(conv_ch, rev=nb), rows_of(LANES, rev=nb), fixed(PRE, conv_ch), fixed(8, conv_ch),
                   fixed(8, LANES)],
        out_shape=[sds((tokens, conv_ch), BF16), sds((tokens, LANES), BF16), sds((PRE, conv_ch)), sds((8, conv_ch)),
                   sds((8, LANES))],
        scratch_shapes=[pltpu.VMEM((2 * PRE + BLOCK, conv_ch), F32), pltpu.VMEM((PRE + BLOCK, conv_ch), F32)],
        compiler_params=params(),
        name="back",
    )(kq, xs, cums, dtb, pre, raw, do, dxs, dkq, stri, stin, cd, s0, dstl, rd, incoming, skip_b, cw, rate)

    back_halo = shifted(dhalo, "cp", cp, -1)
    dxbc = jnp.concatenate([dxbc[:-PRE], (dxbc[-PRE:].astype(F32) + back_halo).astype(BF16)], axis=0)
    dproj = jnp.concatenate([dz, dxbc, ddt], axis=1)
    dn_part = mm(dproj, w, 1, 1).astype(BF16)
    grad_rest = mm(normed, dproj[:, ch:], 0, 0)

    y_own = lax.psum_scatter(y, "tp", scatter_dimension=0, tiled=True).astype(F32)
    r_own = lax.rsqrt(cut(stats, k_id * own_rows, own_rows)[0] * (1.0 / inner) + EPS)[:, None]
    u = layer_input.astype(F32)
    layer_output = (u + y_own * r_own).astype(BF16)
    dn = lax.psum_scatter(dn_part, "tp", scatter_dimension=0, tiled=True).astype(F32)
    q = lax.rsqrt(jnp.mean(u * u, axis=-1, keepdims=True) + EPS)
    m = u * q
    dg = dn * gain_row
    input_grad = cotangent.astype(F32) + q * (dg - m * jnp.mean(dg * m, axis=-1, keepdims=True))

    grp = dp * cp
    quarter = ch // grp
    src = d_id * cp + lax.axis_index("cp")
    og_low = og.astype(BF16)
    og_own = jnp.zeros((quarter, width), F32)
    for j in range(grp):
        pairs = []
        for d in range(dp):
            for p in range(cp):
                for k in range(tp):
                    piece = (d * cp + p + j) % grp
                    slot = (k % share) * grp + piece
                    pairs.append(((d * cp + p) * tp + k, (k // share) * cp * tp + slot))
        send = cut(og_low, ((src + j) % grp) * quarter, quarter, 0)
        og_own = og_own + lax.ppermute(send, ("dp", "cp", "tp"), pairs).astype(F32)
    out_grad = lax.all_gather(og_own.astype(BF16), ("cp", "tp"), axis=0, tiled=True).astype(F32)

    zx = jnp.concatenate([gz, grad_rest[:, :ch], grad_rest[:, ch + 2 * ns :]], axis=1).astype(BF16)
    zx = lax.psum_scatter(zx, "dp", scatter_dimension=0, tiled=True)
    zx = lax.psum(zx.astype(F32), "cp").astype(BF16)
    zx = lax.all_gather(zx, "tp", axis=0, tiled=False).astype(F32)
    half = zx.shape[1]
    kqg = grad_rest[:, ch : ch + 2 * ns].astype(BF16)
    kqg = lax.psum_scatter(kqg, ("dp", "cp", "tp"), scatter_dimension=0, tiled=True)
    kqg = lax.all_gather(kqg, ("cp", "tp"), axis=0, tiled=True).astype(F32)

    def across(values):
        return values.transpose(1, 0, 2).reshape(half, -1)

    in_grad = jnp.concatenate(
        [across(zx[:, :, :ch]), across(zx[:, :, ch : 2 * ch]), kqg, across(zx[:, :, 2 * ch : 2 * ch + lh])], axis=1
    )

    gain_part = jnp.sum(jnp.concatenate([gz, grad_rest], axis=1) * w.astype(F32), axis=1) / gain

    def spread(values, total, start):
        return lax.dynamic_update_slice_in_dim(
            jnp.zeros(values.shape[:-1] + (total,), F32), values, start, values.ndim - 1
        )

    def spread_conv(values):
        return jnp.concatenate([spread(values[:, :ch], inner, k_id * ch), values[:, ch:]], axis=1)

    gate_part = spread(gg[0] / own_gate[0], inner, k_id * ch)
    head_part = spread(hg[0:3, :lh], heads, k_id * lh)
    conv_part = spread_conv(cg[: taps + 1])
    gain_all, conv_sum, head_all, gate_all = lax.psum(
        (gain_part, conv_part, head_part, gate_part), ("dp", "cp", "tp")
    )

    def own(values):
        size = values.shape[-1] // dp
        return lax.dynamic_slice_in_dim(values, d_id * size, size, values.ndim - 1)

    conv_own, head_own = own(conv_sum), own(head_all)
    return (
        layer_output,
        input_grad,
        own(gain_all),
        in_grad,
        conv_own[:taps],
        conv_own[taps],
        head_own[0],
        head_own[1],
        head_own[2],
        own(gate_all),
        out_grad,
    )


def solution(mesh):
    dp, group = mesh.devices.shape
    tp = 8 if group % 8 == 0 else group
    inner_mesh = Mesh(mesh.devices.reshape(dp, group // tp, tp), ("dp", "cp", "tp"))
    tok = P(("dp", "cp", "tp"), None)
    return jax.shard_map(
        local,
        mesh=inner_mesh,
        in_specs=(tok, P("dp"), P("dp", None), P(None, "dp"), P("dp"), P("dp"), P("dp"), P("dp"), P("dp"),
                  P("dp", None), tok),
        out_specs=(tok, tok, P("dp"), P("dp", None), P(None, "dp"), P("dp"), P("dp"), P("dp"), P("dp"), P("dp"),
                   P("dp", None)),
        check_vma=False,
    )
```

time: 1100 us -> 597 us (0.54)
  waiting for transfers between devices: 592 us -> 326 us
  matrix products: 155 us -> 8.47 us
  other arithmetic: 111 us -> 25.2 us
  local copies, waits for them, and re-layouts: 116 us -> 35.6 us
  Pallas kernels: 0 us -> 55.9 us
  blocking collectives: 70.2 us -> 108 us
    reduce_scatter x2 -> x4, waiting for transfers between devices: 336 us -> 172 us  [the longest x1 89.4 us: local(): lax.psum_scatter(kqg, ('dp', 'cp', 'tp'), scatter_dimension=0, tiled=True)]
    dot_general x118 -> x2, matrix products: 155 us -> 8.47 us  [mm(): lax.dot_general(a, b, (((da,), (db,)), ((), ())), preferred_element_type=...]
    all_gather x5 -> x6, waiting for transfers between devices: 188 us -> 95.4 us  [the longest x1 35.5 us: local(): zx = lax.all_gather(zx, 'tp', axis=0, tiled=False).astype(F32)]
    pallas_call x0 -> x6, Pallas kernels: none -> 55.9 us  [the longest x1 16.2 us: local(): pl.pallas_call(lambda *refs: back_kernel(hdim, *refs), grid=(nb,), in_spe...]
    all_to_all x6 -> x0, waiting for transfers between devices: 53.2 us -> none  [the longest x1 16.4 us: local(): lax.all_to_all(d_x_head.astype(jnp.bfloat16), 'seq', split_axis=0, concat...]
    ppermute x0 -> x8, waiting for transfers between devices: none -> 39.1 us  [the longest x4 33.4 us: local(): og_own = og_own + lax.ppermute(send, ('dp', 'cp', 'tp'), pairs).astype(F32)]
    another operation x58 -> x1, other arithmetic: 37.2 us -> 0.05 us
    all_to_all x6 -> x0, starting transfers between devices: 30.1 us -> none  [the longest x1 6.19 us: local(): lax.all_to_all(x_part, 'seq', split_axis=1, concat_axis=0, tiled=True)]
  transfers between devices with their start and end apart: 14 -> 19, of which waited for: 9 -> 14; matrix products, arithmetic and copies ran while one was open for 14% -> 5% of each run, Pallas kernels for 0% -> 4%
where the time goes in v1:
time: 597 us; the launch traced here: 595 us
  waiting for transfers between devices  326 us (55%)
  blocking collectives  108 us (18%)
  Pallas kernels  55.9 us (9%)
  local copies, waits for them, and re-layouts  35.6 us (6%)
  other arithmetic  25.2 us (4%)
  starting transfers between devices  21.7 us (4%)
  between operations  15.2 us (3%)
  matrix products  8.47 us (1%)
    reduce_scatter x1, waiting for transfers between devices, local(): lax.psum_scatter(kqg, ('dp', 'cp', 'tp'), scatter_dimension=0, tiled=True)  89.4 us
    psum x1, blocking collectives, local(): lax.psum((gain_part, conv_part, head_part, gate_part), ('dp', 'cp', 'tp'))  39.1 us
    all_gather x1, waiting for transfers between devices, local(): zx = lax.all_gather(zx, 'tp', axis=0, tiled=False).astype(F32)  35.5 us
    ppermute x4, waiting for transfers between devices, local(): og_own = og_own + lax.ppermute(send, ('dp', 'cp', 'tp'), pairs).astype(F32)  33.4 us
    reduce_scatter x1, waiting for transfers between devices, local(): lax.psum_scatter(y, 'tp', scatter_dimension=0, tiled=True).astype(F32)  33.2 us
    reduce_scatter x1, waiting for transfers between devices, local(): lax.psum_scatter(dn_part, 'tp', scatter_dimension=0, tiled=True).astype(F32)  28 us
    psum x1, blocking collectives, local(): stats = lax.psum(stat, 'tp')  24.8 us
    reduce_scatter x1, waiting for transfers between devices, local(): zx = lax.psum_scatter(zx, 'dp', scatter_dimension=0, tiled=True)  21.7 us
  transfers between devices with their start and end apart: 19, of which 14 were waited for; matrix products, arithmetic and copies ran while one was open for 5% of the time, Pallas kernels for 4%

profile of v1, /device:TPU:0, one launch (start us, length us, event | category | flops | bytes accessed | tf_op | source)
XLA Modules:
  0.0 595.4 jit_solution(3478174529157710589)
XLA Ops:
  7.2 1.3 fusion.26
  13.5 5.9 collective-permute-start
  19.4 4.4 all_gather.40
  25.5 8.4 %all-reduce.6 = bf16[5472]{0:T(1024)(128)(2,1)S(1)} all-reduce(bf16[5472]{0:T(1024)(128)(2,1)S(1)} %dynamic-update-slice), channel_id=2, replica_groups=mesh['dp'=2,'cp'=2,'tp'=8] {'dp'}, use_global_device_ids=true, to_apply=%add.6 | all-reduce | flops 5472 | bytes 21888
  37.5 12.5 %all_gather.37 = bf16[128,1024]{1,0:T(8,128)(2,1)S(1)} all-gather(bf16[16,1024]{1,0:T(8,128)(2,1)S(1)} %collective-permute-done), channel_id=1, replica_groups=mesh['dp'=2,'cp'=2,'tp'=8] {'tp'}, dimensions={0}, use_global_device_ids=true | all-gather | bytes 294912 | tf_op jit(solution)/shard_map/all_gather | solution.py:363
  50.6 17.0 %all-gather.10.cloned.1.call-done.refs_0_ = bf16[1024,1024]{1,0:T(8,128)(2,1)} async-done(((bf16[128,1024]{1,0:T(8,128)(2,1)}), bf16[1024,1024]{1,0:T(8,128)(2,1)}) %all-gather.10.cloned.1.call-update) | async-done | bytes 2097168 | tf_op jit(solution)/shard_map/all_gather | solution.py:362
  67.7 12.5 %front.1 = (bf16[1024,1024]{1,0:T(8,128)(2,1)}, bf16[1024,256]{1,0:T(8,128)(2,1)}, bf16[4,272,512]{2,1,0:T(8,128)(2,1)}, f32[1024,512]{1,0:T(8,128)}, bf16[1024,...) custom-call(bf16[1024,1024]{1,0:T(8,128)(2,1)} %all-gather.10.cloned, ...), custom_call_target="tpu_custom_call" | custom-call | tf_op jit(solution)/shard_map/front/pallas_call | solution.py:414
  80.2 4.5 collective-permute-start.1
  86.1 4.6 all-gather.18.cloned.1.call-done
  90.7 1.9 dynamic-slice_bitcast_fusion.refs_10_
  92.6 4.5 intra.1.refs_2_
  97.1 16.6 %all-gather.14.cloned.1.call-done.refs_11_.refs_4_ = bf16[1024,1024]{1,0:T(8,128)(2,1)} async-done(((bf16[128,1024]{1,0:T(8,128)(2,1)}), bf16[1024,1024]{1,0:T(8,128)(2,1)}) %all-gather.14.cloned.1.call-update) | async-done | bytes 2097168 | tf_op jit(solution)/shard_map/all_gather | solution.py:364
  114.4 8.2 %gate.1 = (bf16[1024,256]{1,0:T(8,128)(2,1)}, bf16[1024,256]{1,0:T(8,128)(2,1)}, bf16[1024,1024]{1,0:T(8,128)(2,1)}, f32[8,1024]{1,0:T(8,128)}) custom-call(bf16[1024,256]{1,0:T(8,128)(2,1)} %get-tuple-element.42.refs_0_.refs_7_, f32[1024,128]{1,0:T(8,128)} %get-tuple-element.43.refs_2_.refs_1_.refs_8_, f32[1024,256]{1,0:T(8,128)} %intra.1.refs_2_, ...), custom_call_target="tpu_custom_call" | custom-call | tf_op jit(solution)/shard_map/gate/pallas_call | solution.py:443
  122.5 24.8 %psum.42.refs_0_ = f32[8,1024]{1,0:T(8,128)} all-reduce(f32[8,1024]{1,0:T(8,128)} %get-tuple-element.51), channel_id=1, replica_groups=mesh['dp'=2,'cp'=2,'tp'=8] {'tp'}, use_global_device_ids=true, to_apply=%region_1.2 | all-reduce | flops 8192 | bytes 65536 | tf_op jit(solution)/shard_map/psum | solution.py:454
  147.3 8.1 %back_gate.1 = (bf16[1024,256]{1,0:T(8,128)(2,1)}, bf16[1024,256]{1,0:T(8,128)(2,1)}, f32[256,1024]{1,0:T(8,128)}, f32[1024,256]{1,0:T(8,128)}, f32[8,256]{1,0:T...) custom-call(f32[8,1024]{1,0:T(8,128)} %psum.42.refs_0_, ...), custom_call_target="tpu_custom_call" | custom-call | tf_op jit(solution)/shard_map/back_gate/pallas_call | solution.py:456
  155.4 1.5 collective-permute-start.2
  156.9 6.4 %back_intra.1 = (f32[1024,256]{1,0:T(8,128)}, f32[1024,256]{1,0:T(8,128)}, f32[1024,128]{1,0:T(8,128)}) custom-call(bf16[1024,256]{1,0:T(8,128)(2,1)} %get-tuple-element.42.refs_0_.refs_7_, bf16[1024,256]{1,0:T(8,128)(2,1)} %get-tuple-element.44.refs_1_, f32[1024,128]{1,0:T(8,128)} %get-tuple-element.43.refs_2_.refs_1_.refs_8_, ...), custom_call_target="tpu_custom_call" | custom-call | tf_op jit(solution)/shard_map/back_intra/pallas_call | solution.py:473
  163.3 1.5 collective-permute-done.2.refs_15_
  165.4 16.2 %back.1 = (bf16[1024,512]{1,0:T(8,128)(2,1)}, bf16[1024,128]{1,0:T(8,128)(2,1)}, f32[16,512]{1,0:T(8,128)}, f32[8,512]{1,0:T(8,128)}, f32[8,128]{1,0:T(8,128)}) custom-call(bf16[1024,256]{1,0:T(8,128)(2,1)} %get-tuple-element.42.refs_0_.refs_7_, bf16[1024,256]{1,0:T(8,128)(2,1)} %get-tuple-element.44.refs_1_, ...), custom_call_target="tpu_custom_call" | custom-call | tf_op jit(solution)/shard_map/back/pallas_call | solution.py:483
  181.6 1.4 collective-permute-start.3
  183.1 1.3 slice.108
  184.4 4.2 collective-permute-done.3
  189.4 3.4 fusion.29
  193.6 1.2 pad_maximum_fusion.1
  194.9 21.7 %reduce-scatter.9.cloned.1.call-done = bf16[512,640]{1,0:T(8,128)(2,1)} async-done(((bf16[1024,640]{1,0:T(8,128)(2,1)}), bf16[512,640]{1,0:T(8,128)(2,1)}) %reduce-scatter.9.cloned.1.call-update) | async-done | bytes 655376 | tf_op jit(solution)/shard_map/reduce_scatter | solution.py:534
  217.5 1.3 convert_element_type.93
  218.8 2.8 collective-permute-start.7
  221.7 2.5 collective-permute-start.6
  224.1 2.0 collective-permute-start.5
  226.8 21.7 %collective-permute-done.7 = bf16[64,1024]{1,0:T(8,128)(2,1)S(1)} collective-permute-done((bf16[64,1024]{1,0:T(8,128)(2,1)S(1)}, bf16[64,1024]{1,0:T(8,128)(2,1)S(1)}, u32[]{:S(2)}, u32[]{:S(2)}) %collective-permute-start.7) | collective-permute-done | bytes 131104 | tf_op jit(solution)/shard_map/ppermute | solution.py:530
  248.5 11.7 %collective-permute-done.5 = bf16[64,1024]{1,0:T(8,128)(2,1)S(1)} collective-permute-done((bf16[64,1024]{1,0:T(8,128)(2,1)S(1)}, bf16[64,1024]{1,0:T(8,128)(2,1)S(1)}, u32[]{:S(2)}, u32[]{:S(2)}) %collective-permute-start.5) | collective-permute-done | bytes 131104 | tf_op jit(solution)/shard_map/ppermute | solution.py:530
  261.0 5.1 convolution_convert_fusion
  266.8 16.3 %all-reduce.10.cloned.1.call-done = bf16[512,640]{1,0:T(8,128)(2,1)} async-done(((bf16[512,640]{1,0:T(8,128)(2,1)}), bf16[512,640]{1,0:T(8,128)(2,1)}) %all-reduce.10.cloned.1.call-update) | async-done | bytes 655376 | tf_op jit(solution)/shard_map/psum | solution.py:535
  285.1 2.2 fusion
  287.3 39.1 %all-reduce.7 = (f32[1024]{0:T(1024)S(1)}, f32[5,2304]{1,0:T(8,128)S(1)}, f32[3,32]{1,0:T(4,128)S(1)}, f32[2048]{0:T(1024)S(1)}) all-reduce(f32[1024]{0:T(1024)S(1)} %div.28, f32[5,2304]{1,0:T(8,128)S(1)} %pad_maximum_fusion.2, f32[3,32]{1,0:T(4,128)S(1)} %dynamic_update_slice.10, ...), channel_id=1, replica_groups=mesh['dp'=2,'cp'=2,'tp'=8] {'dp','cp','tp'}, use_global_device_ids=true, to_apply=%region_6.7 | all-reduce | flops 14688 | bytes 117504 | tf_op jit(solution)/shard_map/psum | solution.py:562
  329.5 89.4 %reduce-scatter.11.cloned.1.call-done = bf16[32,256]{1,0:T(8,128)(2,1)} async-done(((bf16[1024,256]{1,0:T(8,128)(2,1)}), bf16[32,256]{1,0:T(8,128)(2,1)}) %reduce-scatter.11.cloned.1.call-update) | async-done | bytes 16400 | tf_op jit(solution)/shard_map/reduce_scatter | solution.py:539
  419.0 18.6 %all_gather.46 = bf16[512,256]{1,0:T(8,128)(2,1)S(1)} all-gather(bf16[32,256]{1,0:T(8,128)(2,1)} %reduce-scatter.11.cloned.1.call-done), channel_id=1, replica_groups=mesh['dp'=2,'cp'=2,'tp'=8] {'cp','tp'}, dimensions={0}, use_global_device_ids=true | all-gather | bytes 278528 | tf_op jit(solution)/shard_map/all_gather | solution.py:540
  437.7 21.6 %all-gather.16.cloned.1.call-done = bf16[1024,1024]{1,0:T(8,128)(2,1)} async-done(((bf16[64,1024]{1,0:T(8,128)(2,1)}), bf16[1024,1024]{1,0:T(8,128)(2,1)}) %all-gather.16.cloned.1.call-update) | async-done | bytes 2097168 | tf_op jit(solution)/shard_map/all_gather | solution.py:531
  459.3 4.1 convert_element_type.99
  463.4 28.0 %reduce-scatter.7.cloned.1.call-done = bf16[128,1024]{1,0:T(8,128)(2,1)} async-done(((bf16[1024,1024]{1,0:T(8,128)(2,1)}), bf16[128,1024]{1,0:T(8,128)(2,1)}) %reduce-scatter.7.cloned.1.call-update) | async-done | bytes 262160 | tf_op jit(solution)/shard_map/reduce_scatter | solution.py:510
  492.5 33.2 %reduce-scatter.5.cloned.1.call-done = bf16[128,1024]{1,0:T(8,128)(2,1)} async-done(((bf16[1024,1024]{1,0:T(8,128)(2,1)}), bf16[128,1024]{1,0:T(8,128)(2,1)}) %reduce-scatter.5.cloned.1.call-update) | async-done | bytes 262160 | tf_op jit(solution)/shard_map/reduce_scatter | solution.py:506
  525.8 2.1 fusion.19
  527.9 35.5 %all-gather.20.cloned.1.call-done = bf16[4096,640]{1,0:T(8,128)(2,1)} async-done(((bf16[512,640]{1,0:T(8,128)(2,1)}), bf16[4096,640]{1,0:T(8,128)(2,1)}) %all-gather.20.cloned.1.call-update) | async-done | bytes 5242896 | tf_op jit(solution)/shard_map/all_gather | solution.py:536
  563.4 3.2 convert.12
  566.8 4.3 slice_bitcast_fusion.1
  571.8 5.4 copy.29
  577.1 5.4 copy.28
  582.6 6.3 %pad_maximum_fusion = f32[512,4384]{0,1:T(8,128)} fusion(f32[512,32]{0,1:T(8,128)S(1)} %reshape.69, f32[512,256]{0,1:T(8,128)S(1)} %copy.31, f32[512,2048]{0,1:T(8,128)} %bitcast.46, f32[512,2048]{0,1:T(8,128)} %bitcast.47), kind=kLoop, calls=%fused_computation | loop fusion | flops 6733824 | bytes 17956864 | tf_op jit(solution)/shard_map/concatenate | solution.py:545
  (144 shorter events, 24.6 us)
Async XLA Ops:
  7.2 4.8 copy-start
  7.2 43.4 %all-gather.12.cloned.1.call-start = ((), (), s32[]{:S(2)}) async-start(), calls=%async_computation.5 | async-start | bytes 2752512 | tf_op jit(solution)/shard_map/all_gather | solution.py:330
  9.7 3.7 copy-start.3
  9.9 9.5 %copy-start.11 = (bf16[4,1152]{1,0:T(4,128)(2,1)S(1)}, bf16[4,1152]{1,0:T(4,128)(2,1)}, u32[]{:S(2)}) copy-start(bf16[4,1152]{1,0:T(4,128)(2,1)} %param.14) | copy-start | bytes 27652
  9.9 13.9 %copy-start.20 = (u32[32]{0:T(128)S(1)}, u32[32]{0:T(128)}, u32[]{:S(2)}) copy-start(u32[32]{0:T(128)} %constant.122) | copy-start | bytes 388
  9.9 15.1 %copy-start.12 = (bf16[1152]{0:T(1024)(128)(2,1)S(1)}, bf16[1152]{0:T(1024)(128)(2,1)}, u32[]{:S(2)}) copy-start(bf16[1152]{0:T(1024)(128)(2,1)} %param.15) | copy-start | bytes 6916
  9.9 15.1 %copy-start.13 = (bf16[1024]{0:T(1024)(128)(2,1)S(1)}, bf16[1024]{0:T(1024)(128)(2,1)}, u32[]{:S(2)}) copy-start(bf16[1024]{0:T(1024)(128)(2,1)} %param.19) | copy-start | bytes 6148
  9.9 15.1 %copy-start.15 = (bf16[512]{0:T(512)(128)(2,1)S(1)}, bf16[512]{0:T(512)(128)(2,1)}, u32[]{:S(2)}) copy-start(bf16[512]{0:T(512)(128)(2,1)} %param.12) | copy-start | bytes 3076
  10.0 15.1 %copy-start.16 = (bf16[16]{0:T(256)(128)(2,1)S(1)}, bf16[16]{0:T(256)(128)(2,1)}, u32[]{:S(2)}) copy-start(bf16[16]{0:T(256)(128)(2,1)} %param.16) | copy-start | bytes 100
  10.0 15.1 %copy-start.17 = (bf16[16]{0:T(256)(128)(2,1)S(1)}, bf16[16]{0:T(256)(128)(2,1)}, u32[]{:S(2)}) copy-start(bf16[16]{0:T(256)(128)(2,1)} %param.17) | copy-start | bytes 100
  10.0 15.1 %copy-start.18 = (bf16[16]{0:T(256)(128)(2,1)S(1)}, bf16[16]{0:T(256)(128)(2,1)}, u32[]{:S(2)}) copy-start(bf16[16]{0:T(256)(128)(2,1)} %param.18) | copy-start | bytes 100
  11.1 56.5 %all-gather.10.cloned.1.call-start = ((), (), s32[]{:S(2)}) async-start(), calls=%async_computation.4 | async-start | bytes 2359296 | tf_op jit(solution)/shard_map/all_gather | solution.py:362
  11.9 78.8 %all-gather.18.cloned.1.call-start = ((), (), s32[]{:S(2)}) async-start(), calls=%async_computation.13 | async-start | bytes 1572864 | tf_op jit(solution)/shard_map/all_gather | solution.py:381
  12.8 100.9 %all-gather.14.cloned.1.call-start = ((), (), s32[]{:S(2)}) async-start(), calls=%async_computation.6 | async-start | bytes 2359296 | tf_op jit(solution)/shard_map/all_gather | solution.py:364
  13.4 203.2 %reduce-scatter.9.cloned.1.call-start = ((), (), s32[]{:S(2)}) async-start(), calls=%async_computation.9 | async-start | bytes 1966080 | tf_op jit(solution)/shard_map/reduce_scatter | solution.py:534
  13.5 24.0 %collective-permute-start = (bf16[16,1024]{1,0:T(8,128)(2,1)S(1)}, bf16[16,1024]{1,0:T(8,128)(2,1)S(1)}, u32[]{:S(2)}, u32[]{:S(2)}) collective-permute-start(bf16[16,1024]{1,0:T(8,128)(2,1)S(1)} %slice.96), channel_id=1, source_target_pairs={{0,8},{1,9},{2,10},{3,11},{4,12},{5,13},{6,14},{7,15},{16,24},{17,... | collective-permute-start | bytes 98312 | tf_op jit(solution)/shard_map/ppermute | solution.py:326
  80.2 33.5 %collective-permute-start.1 = (f32[128,256]{1,0:T(8,128)}, f32[128,256]{1,0:T(8,128)S(1)}, u32[]{:S(2)}, u32[]{:S(2)}) collective-permute-start(f32[128,256]{1,0:T(8,128)} %get-tuple-element.49), channel_id=1, source_target_pairs={{0,8},{1,9},{2,10},{3,11},{4,12},{5,13},{6,14},{7,15},{16,24},{17,... | collective-permute-start | bytes 393224 | tf_op jit(solution)/shard_map/ppermute | solution.py:326
  113.7 0.6 copy-start.8
  155.4 9.4 %collective-permute-start.2 = (f32[128,256]{1,0:T(8,128)}, f32[128,256]{1,0:T(8,128)S(1)}, u32[]{:S(2)}, u32[]{:S(2)}) collective-permute-start(f32[128,256]{1,0:T(8,128)} %get-tuple-element.64), channel_id=1, source_target_pairs={{8,0},{9,1},{10,2},{11,3},{12,4},{13,5},{14,6},{15,7},{24,16},{25,... | collective-permute-start | bytes 393224 | tf_op jit(solution)/shard_map/ppermute | solution.py:326
  164.8 0.7 copy-start.9
  165.4 17.6 %copy-start.4 = (f32[1024,256]{1,0:T(8,128)S(1)}, f32[1024,256]{1,0:T(8,128)}, u32[]{:S(2)}) copy-start(f32[1024,256]{1,0:T(8,128)} %get-tuple-element.68) | copy-start | bytes 3145732
  181.6 7.8 %copy-start.5 = (bf16[1024,1024]{1,0:T(8,128)(2,1)S(1)}, bf16[1024,1024]{1,0:T(8,128)(2,1)}, u32[]{:S(2)}) copy-start(bf16[1024,1024]{1,0:T(8,128)(2,1)} %get-tuple-element.54.refs_5_) | copy-start | bytes 6291460
  181.6 7.8 %copy-start.19 = (bf16[1024,128]{1,0:T(8,128)(2,1)S(1)}, bf16[1024,128]{1,0:T(8,128)(2,1)}, u32[]{:S(2)}) copy-start(bf16[1024,128]{1,0:T(8,128)(2,1)} %get-tuple-element.67) | copy-start | bytes 786436
  181.6 7.0 %collective-permute-start.3 = (f32[16,512]{1,0:T(8,128)}, f32[16,512]{1,0:T(8,128)S(1)}, u32[]{:S(2)}, u32[]{:S(2)}) collective-permute-start(f32[16,512]{1,0:T(8,128)} %get-tuple-element.66), channel_id=1, source_target_pairs={{8,0},{9,1},{10,2},{11,3},{12,4},{13,5},{14,6},{15,7},{24,16},{25,... | collective-permute-start | bytes 98312 | tf_op jit(solution)/shard_map/ppermute | solution.py:326
  184.4 8.3 %copy-start.7 = (bf16[1008,512]{1,0:T(8,128)(2,1)}, bf16[1008,512]{1,0:T(8,128)(2,1)S(1)}, u32[]{:S(2)}) copy-start(bf16[1008,512]{1,0:T(8,128)(2,1)S(1)} %slice.108) | copy-start | bytes 3096580
  194.8 66.2 %copy-start.2 = (bf16[1024,896]{1,0:T(8,128)(2,1)S(1)}, bf16[1024,896]{1,0:T(8,128)(2,1)}, u32[]{:S(2)}) copy-start(bf16[1024,896]{1,0:T(8,128)(2,1)} %all-gather.12.cloned.1.call-done.refs_3_) | copy-start | bytes 5505028
  194.8 88.2 %all-reduce.10.cloned.1.call-start = ((), (), s32[]{:S(2)}) async-start(), calls=%async_computation.10 | async-start | bytes 1310720 | tf_op jit(solution)/shard_map/psum | solution.py:535
  216.6 202.3 %reduce-scatter.11.cloned.1.call-start = ((), (), s32[]{:S(2)}) async-start(), calls=%async_computation.11 | async-start | bytes 540672 | tf_op jit(solution)/shard_map/reduce_scatter | solution.py:539
  217.4 242.0 %all-gather.16.cloned.1.call-start = ((), (), s32[]{:S(2)}) async-start(), calls=%async_computation.12 | async-start | bytes 2228224 | tf_op jit(solution)/shard_map/all_gather | solution.py:531
  218.8 29.6 %collective-permute-start.7 = (bf16[64,1024]{1,0:T(8,128)(2,1)S(1)}, bf16[64,1024]{1,0:T(8,128)(2,1)S(1)}, u32[]{:S(2)}, u32[]{:S(2)}) collective-permute-start(bf16[64,1024]{1,0:T(8,128)(2,1)S(1)} %get-tuple-element.85), channel_id=1, source_target_pairs={{0,3},{1,7},{2,11},{3,15},{4,19},{5,23},{6,27},{7,31},{8,0},{9,4},... | collective-permute-start | bytes 393224 | tf_op jit(solution)/shard_map/ppermute | solution.py:530
  221.7 26.8 %collective-permute-start.6 = (bf16[64,1024]{1,0:T(8,128)(2,1)S(1)}, bf16[64,1024]{1,0:T(8,128)(2,1)S(1)}, u32[]{:S(2)}, u32[]{:S(2)}) collective-permute-start(bf16[64,1024]{1,0:T(8,128)(2,1)S(1)} %get-tuple-element.86), channel_id=1, source_target_pairs={{0,2},{1,6},{2,10},{3,14},{4,18},{5,22},{6,26},{7,30},{8,3},{9,7},... | collective-permute-start | bytes 393224 | tf_op jit(solution)/shard_map/ppermute | solution.py:530
  224.1 36.0 %collective-permute-start.5 = (bf16[64,1024]{1,0:T(8,128)(2,1)S(1)}, bf16[64,1024]{1,0:T(8,128)(2,1)S(1)}, u32[]{:S(2)}, u32[]{:S(2)}) collective-permute-start(bf16[64,1024]{1,0:T(8,128)(2,1)S(1)} %get-tuple-element.87), channel_id=1, source_target_pairs={{0,1},{1,5},{2,9},{3,13},{4,17},{5,21},{6,25},{7,29},{8,2},{9,6},{... | collective-permute-start | bytes 393224 | tf_op jit(solution)/shard_map/ppermute | solution.py:530
  226.1 34.0 %collective-permute-start.4 = (bf16[64,1024]{1,0:T(8,128)(2,1)S(1)}, bf16[64,1024]{1,0:T(8,128)(2,1)S(1)}, u32[]{:S(2)}, u32[]{:S(2)}) collective-permute-start(bf16[64,1024]{1,0:T(8,128)(2,1)S(1)} %get-tuple-element.84), channel_id=1, source_target_pairs={{0,0},{1,4},{2,8},{3,12},{4,16},{5,20},{6,24},{7,28},{8,1},{9,5},{... | collective-permute-start | bytes 393224 | tf_op jit(solution)/shard_map/ppermute | solution.py:530
  260.9 230.4 %reduce-scatter.7.cloned.1.call-start = ((), (), s32[]{:S(2)}) async-start(), calls=%async_computation.8 | async-start | bytes 2359296 | tf_op jit(solution)/shard_map/reduce_scatter | solution.py:510
  266.1 18.7 %copy-start.14 = (f32[8,128]{1,0:T(8,128)S(1)}, f32[8,128]{1,0:T(8,128)}, u32[]{:S(2)}) copy-start(f32[8,128]{1,0:T(8,128)} %get-tuple-element.70) | copy-start | bytes 12292
  266.1 18.9 %copy-start.10 = (f32[8,512]{1,0:T(8,128)S(1)}, f32[8,512]{1,0:T(8,128)}, u32[]{:S(2)}) copy-start(f32[8,512]{1,0:T(8,128)} %get-tuple-element.69) | copy-start | bytes 49156
  266.1 259.6 %reduce-scatter.5.cloned.1.call-start = ((), (), s32[]{:S(2)}) async-start(), calls=%async_computation.7 | async-start | bytes 2359296 | tf_op jit(solution)/shard_map/reduce_scatter | solution.py:506
  266.7 296.7 %all-gather.20.cloned.1.call-start = ((), (), s32[]{:S(2)}) async-start(), calls=%async_computation.14 | async-start | bytes 5898240 | tf_op jit(solution)/shard_map/all_gather | solution.py:536
  437.7 88.1 %copy-start.6 = (bf16[128,1024]{1,0:T(8,128)(2,1)S(1)}, bf16[128,1024]{1,0:T(8,128)(2,1)}, u32[]{:S(2)}) copy-start(bf16[128,1024]{1,0:T(8,128)(2,1)} %param.21) | copy-start | bytes 786436
  582.6 6.3 %copy-start.1 = (bf16[1024,1024]{1,0:T(8,128)(2,1)S(1)}, bf16[1024,1024]{1,0:T(8,128)(2,1)}, u32[]{:S(2)}) copy-start(bf16[1024,1024]{1,0:T(8,128)(2,1)} %param.20) | copy-start | bytes 6291460
Sparse Core Ops, SparseCore 0:
  11.3 33.2 all-gather.11
  46.1 21.5 all-gather.9
  69.2 21.4 all-gather.17
  92.2 21.5 all-gather.13
  194.9 21.6 reduce-scatter.8
  218.9 64.1 all-reduce.9
  285.9 133.0 reduce-scatter.10
  421.4 37.9 all-gather.15
  462.3 29.0 reduce-scatter.6
  493.6 32.1 reduce-scatter.4
  527.5 35.8 all-gather.19

commit v2 on v1

--- a/solution.py
+++ b/solution.py
@@ -301,6 +301,13 @@
     halo_ref[...] = halo
 
 
+def assemble_kernel(ch, inner, z_ref, x_ref, kq_ref, out_ref):
+    for k in range(z_ref.shape[0]):
+        out_ref[:, k * ch : (k + 1) * ch] = z_ref[k].astype(F32)
+        out_ref[:, inner + k * ch : inner + (k + 1) * ch] = x_ref[k].astype(F32)
+    out_ref[:, 2 * inner :] = kq_ref[:, : out_ref.shape[1] - 2 * inner].astype(F32)
+
+
 def rows_of(width, rows=BLOCK, rev=None):
     if rev is None:
         return pl.BlockSpec((rows, width), lambda i: (i, 0))
@@ -326,8 +333,63 @@
     return lax.ppermute(values, axis, pairs)
 
 
-def gather_dp(values, axis=0):
-    return lax.all_gather(values, "dp", axis=axis, tiled=True)
+def gather_dp(values, dp, d_id):
+    parts = [values] + [
+        lax.ppermute(values, "dp", [(i, (i - j) % dp) for i in range(dp)]) for j in range(1, dp)
+    ]
+    if dp == 2:
+        first = d_id == 0
+        return jnp.stack([jnp.where(first, parts[0], parts[1]), jnp.where(first, parts[1], parts[0])])
+    stacked = jnp.stack(parts)
+    return jnp.take(stacked, (jnp.arange(dp) - d_id) % dp, axis=0)
+
+
+def scatter_dp(values, dp, d_id, axis=0):
+    size = values.shape[axis] // dp
+
+    def part(index):
+        return lax.dynamic_slice_in_dim(values, index * size, size, axis)
+
+    total = part(d_id)
+    for j in range(1, dp):
+        sent = part((d_id + j) % dp).astype(BF16)
+        total = total + lax.ppermute(sent, "dp", [(i, (i + j) % dp) for i in range(dp)]).astype(F32)
+    return total
+
+
+def swap(values, axis, size, bit):
+    return lax.ppermute(values, axis, [(i, i ^ bit) for i in range(size)])
+
+
+def sum_over(values, axis, size, kind=F32):
+    bit = 1
+    while bit < size:
+        values = values + swap(values.astype(kind), axis, size, bit).astype(F32)
+        bit *= 2
+    return values
+
+
+def scatter_over(values, axis, size, index):
+    bit = size // 2
+    while bit:
+        half = values.shape[0] // 2
+        upper = (index & bit) != 0
+        low, high = values[:half], values[half:]
+        kept = jnp.where(upper, high, low)
+        sent = jnp.where(upper, low, high).astype(BF16)
+        values = kept + swap(sent, axis, size, bit).astype(F32)
+        bit //= 2
+    return values
+
+
+def gather_over(values, axis, size, index):
+    bit = 1
+    while bit < size:
+        other = swap(values, axis, size, bit)
+        upper = (index & bit) != 0
+        values = jnp.concatenate([jnp.where(upper, other, values), jnp.where(upper, values, other)], axis=0)
+        bit *= 2
+    return values
 
 
 def carry_over(state, decay, axis, size, way):
@@ -359,13 +421,10 @@
     cols = ch + conv_ch + LANES
     taps = conv_weight.shape[0]
 
-    x_all = lax.all_gather(layer_input, "tp", axis=0, tiled=True)
-    halo = lax.all_gather(shifted(layer_input[-PRE:], "cp", cp, 1), "tp", axis=0, tiled=True)[-PRE:]
-    c_all = lax.all_gather(cotangent, "tp", axis=0, tiled=True)
-
     def cut(values, start, size, axis=1):
         return lax.dynamic_slice_in_dim(values, start, size, axis)
 
+    share = tp // dp
     own_cols = jnp.concatenate(
         [
             cut(in_weight, k_id * ch, ch),
@@ -376,20 +435,32 @@
         ],
         axis=1,
     )
-    w = gather_dp(own_cols)
-    share = tp // dp
-    ow = lax.all_gather(cut(out_weight, (k_id % share) * ch, ch, 0), "dp", axis=0, tiled=False)
+    row_size = conv_all // dp
+
+    def wide(values):
+        return jnp.pad(values, ((0, 0), (0, row_size - values.shape[1])))
+
+    heads_own = jnp.concatenate([step_bias, rate_log, skip_gain])[None]
+    small = jnp.concatenate(
+        [conv_weight, conv_bias[None], wide(norm_gain[None]), wide(gate_gain[None]), wide(heads_own)], axis=0
+    )
+    small = gather_dp(small, dp, d_id).astype(F32)
+    w = gather_dp(own_cols, dp, d_id).reshape(width, cols)
+    x_all = lax.all_gather(layer_input, "tp", axis=0, tiled=True)
+    halo = lax.all_gather(shifted(layer_input[-PRE:], "cp", cp, 1), "tp", axis=0, tiled=True)[-PRE:]
+    c_all = lax.all_gather(cotangent, "tp", axis=0, tiled=True)
+    ow = gather_dp(cut(out_weight, (k_id % share) * ch, ch, 0), dp, d_id)
     ow = lax.dynamic_index_in_dim(ow, k_id // share, 0, keepdims=False)
-    taps_all = gather_dp(conv_weight, 1).astype(F32)
-    small = gather_dp(
-        jnp.concatenate([norm_gain, conv_bias, gate_gain, step_bias, rate_log, skip_gain])[None], 0
-    ).astype(F32)
-    widths = [width, conv_all, inner, heads, heads, heads]
-    pieces, at = [], 0
-    for size in widths:
-        pieces.append(small[:, at : at + size // dp].reshape(-1))
-        at += size // dp
-    gain, offset, ggain, sbias, rlog, skip = pieces
+
+    def row_of(index, size, at=0):
+        return small[:, index, at : at + size].reshape(-1)
+
+    taps_all = small[:, :taps].transpose(1, 0, 2).reshape(taps, conv_all)
+    offset = row_of(taps, row_size)
+    gain = row_of(taps + 1, width // dp)
+    ggain = row_of(taps + 2, inner // dp)
+    hs = heads // dp
+    sbias, rlog, skip = (row_of(taps + 3, hs, i * hs) for i in range(3))
 
     def own_conv(values):
         return jnp.concatenate([cut(values, k_id * ch, ch), values[:, inner:]], axis=1)
@@ -451,7 +522,7 @@
         name="gate",
     )(kq, cums, inside, pre, z, stin, cd, s0, skip_b, own_gate, ow, c_all)
 
-    stats = lax.psum(stat, "tp")
+    stats = sum_over(stat, "tp", tp)
 
     do, dz, og, gz, gg, dstl, rd, g0 = pl.pallas_call(
         lambda *refs: back_gate_kernel(hdim, inner, *refs),
@@ -515,7 +586,8 @@
 
     grp = dp * cp
     quarter = ch // grp
-    src = d_id * cp + lax.axis_index("cp")
+    c_id = lax.axis_index("cp")
+    src = d_id * cp + c_id
     og_low = og.astype(BF16)
     og_own = jnp.zeros((quarter, width), F32)
     for j in range(grp):
@@ -525,26 +597,36 @@
                 for k in range(tp):
                     piece = (d * cp + p + j) % grp
                     slot = (k % share) * grp + piece
-                    pairs.append(((d * cp + p) * tp + k, (k // share) * cp * tp + slot))
+                    pairs.append(((d * cp + p) * tp + k, (k // share) * cp * tp + (slot % cp) * tp + slot // cp))
         send = cut(og_low, ((src + j) % grp) * quarter, quarter, 0)
         og_own = og_own + lax.ppermute(send, ("dp", "cp", "tp"), pairs).astype(F32)
-    out_grad = lax.all_gather(og_own.astype(BF16), ("cp", "tp"), axis=0, tiled=True).astype(F32)
-
-    zx = jnp.concatenate([gz, grad_rest[:, :ch], grad_rest[:, ch + 2 * ns :]], axis=1).astype(BF16)
-    zx = lax.psum_scatter(zx, "dp", scatter_dimension=0, tiled=True)
-    zx = lax.psum(zx.astype(F32), "cp").astype(BF16)
-    zx = lax.all_gather(zx, "tp", axis=0, tiled=False).astype(F32)
-    half = zx.shape[1]
-    kqg = grad_rest[:, ch : ch + 2 * ns].astype(BF16)
-    kqg = lax.psum_scatter(kqg, ("dp", "cp", "tp"), scatter_dimension=0, tiled=True)
-    kqg = lax.all_gather(kqg, ("cp", "tp"), axis=0, tiled=True).astype(F32)
-
-    def across(values):
-        return values.transpose(1, 0, 2).reshape(half, -1)
-
-    in_grad = jnp.concatenate(
-        [across(zx[:, :, :ch]), across(zx[:, :, ch : 2 * ch]), kqg, across(zx[:, :, 2 * ch : 2 * ch + lh])], axis=1
+    og_own = gather_over(og_own.astype(BF16), "cp", cp, c_id)
+    out_grad = lax.all_gather(og_own, "tp", axis=0, tiled=True).astype(F32)
+
+    def total_of(values):
+        return sum_over(scatter_dp(values, dp, d_id), "cp", cp, BF16)
+
+    zg = lax.all_gather(total_of(gz).astype(BF16), "tp", axis=0, tiled=False)
+    xg = lax.all_gather(total_of(grad_rest[:, :ch]).astype(BF16), "tp", axis=0, tiled=False)
+    dt_grad = lax.dynamic_update_slice_in_dim(
+        jnp.zeros((width, LANES), F32), grad_rest[:, ch + 2 * ns : ch + 2 * ns + lh], k_id * lh, 1
     )
+    kqg = total_of(jnp.concatenate([grad_rest[:, ch : ch + 2 * ns], dt_grad], axis=1))
+    kqg = scatter_over(kqg, "tp", tp, k_id).astype(BF16)
+    kqg = gather_over(kqg, "tp", tp, k_id)
+    half = kqg.shape[0]
+    tile = 64
+    proj_all = in_weight.shape[1]
+    in_grad = pl.pallas_call(
+        lambda *refs: assemble_kernel(ch, inner, *refs),
+        grid=(half // tile,),
+        in_specs=[pl.BlockSpec((tp, tile, ch), lambda i: (0, i, 0)), pl.BlockSpec((tp, tile, ch), lambda i: (0, i, 0)),
+                  rows_of(2 * ns + LANES, tile)],
+        out_specs=rows_of(proj_all, tile),
+        out_shape=sds((half, proj_all)),
+        compiler_params=params(),
+        name="assemble",
+    )(zg, xg, kqg)
 
     gain_part = jnp.sum(jnp.concatenate([gz, grad_rest], axis=1) * w.astype(F32), axis=1) / gain
 
@@ -556,18 +638,22 @@
     def spread_conv(values):
         return jnp.concatenate([spread(values[:, :ch], inner, k_id * ch), values[:, ch:]], axis=1)
 
-    gate_part = spread(gg[0] / own_gate[0], inner, k_id * ch)
-    head_part = spread(hg[0:3, :lh], heads, k_id * lh)
+    def full(values):
+        return jnp.pad(values, ((0, 0), (0, conv_all - values.shape[1])))
+
     conv_part = spread_conv(cg[: taps + 1])
-    gain_all, conv_sum, head_all, gate_all = lax.psum(
-        (gain_part, conv_part, head_part, gate_part), ("dp", "cp", "tp")
-    )
+    gate_part = spread(gg[0:1] / own_gate[0:1], inner, k_id * ch)
+    head_part = spread(hg[0:3, :lh], heads, k_id * lh).reshape(1, 3 * heads)
+    pack = jnp.concatenate([conv_part, full(gate_part), full(gain_part[None]), full(head_part)], axis=0)
+    pack = sum_over(sum_over(sum_over(pack, "tp", tp), "cp", cp), "dp", dp)
 
     def own(values):
         size = values.shape[-1] // dp
         return lax.dynamic_slice_in_dim(values, d_id * size, size, values.ndim - 1)
 
-    conv_own, head_own = own(conv_sum), own(head_all)
+    conv_own = own(pack[: taps + 1])
+    head_own = own(pack[taps + 3, : 3 * heads].reshape(3, heads))
+    gate_all, gain_all = pack[taps + 1, :inner], pack[taps + 2, :width]
     return (
         layer_output,
         input_grad,

time: 597 us -> 354 us (0.59)
  waiting for transfers between devices: 326 us -> 131 us
  blocking collectives: 108 us -> 13.6 us
  starting transfers between devices: 21.7 us -> 49.7 us
  local copies, waits for them, and re-layouts: 35.6 us -> 45.1 us
  Pallas kernels: 55.9 us -> 63.3 us
    ppermute x0 -> x24, waiting for transfers between devices: none -> 113 us  [the longest x18 87.4 us: swap(): return lax.ppermute(values, axis, [(i, i ^ bit) for i in range(size)])]
    reduce_scatter x2 -> x0, waiting for transfers between devices: 111 us -> none  [the longest x1 89.4 us: local(): lax.psum_scatter(kqg, ('dp', 'cp', 'tp'), scatter_dimension=0, tiled=True)]
    psum x2 -> x0, blocking collectives: 63.9 us -> none  [the longest x1 39.1 us: local(): lax.psum((gain_part, conv_part, head_part, gate_part), ('dp', 'cp', 'tp'))]
    all_gather x4 -> x3, waiting for transfers between devices: 61.7 us -> 0.01 us  [the longest x1 0.01 us: local(): out_grad = lax.all_gather(og_own, 'tp', axis=0, tiled=True).astype(F32)]
    reduce_scatter x1, waiting for transfers between devices: 33.2 us -> 0.02 us  [local(): lax.psum_scatter(y, 'tp', scatter_dimension=0, tiled=True).astype(F32)]
    ppermute x0 -> x24, starting transfers between devices: none -> 32.7 us  [the longest x18 19.7 us: swap(): return lax.ppermute(values, axis, [(i, i ^ bit) for i in range(size)])]
    reduce_scatter x1, waiting for transfers between devices: 28 us -> 0.01 us  [local(): lax.psum_scatter(dn_part, 'tp', scatter_dimension=0, tiled=True).astype(F32)]
    ppermute x4, waiting for transfers between devices: 33.4 us -> 10 us  [local(): og_own = og_own + lax.ppermute(send, ('dp', 'cp', 'tp'), pairs).astype(F32)]
  transfers between devices with their start and end apart: 19 -> 39, of which waited for: 14 -> 22; matrix products, arithmetic and copies ran while one was open for 5% -> 20% of each run, Pallas kernels for 4% -> 13%
where the time goes in v2:
time: 354 us; the launch traced here: 352 us
  waiting for transfers between devices  131 us (37%)
  Pallas kernels  63.3 us (18%)
  starting transfers between devices  49.7 us (14%)
  local copies, waits for them, and re-layouts  45.1 us (13%)
  other arithmetic  25.5 us (7%)
  between operations  15 us (4%)
  blocking collectives  13.6 us (4%)
  matrix products  8.97 us (3%)
    ppermute x18, waiting for transfers between devices, swap(): return lax.ppermute(values, axis, [(i, i ^ bit) for i in range(size)])  87.4 us
    ppermute x18, starting transfers between devices, swap(): return lax.ppermute(values, axis, [(i, i ^ bit) for i in range(size)])  19.7 us
    pallas_call x1, Pallas kernels, local(): pl.pallas_call(lambda *refs: back_kernel(hdim, *refs), grid=(nb,), in_spe...  16.1 us
    unnamed x56, local copies, waits for them, and re-layouts  15.2 us
    all_gather x1, blocking collectives, local(): lax.all_gather(shifted(layer_input[-PRE:], 'cp', cp, 1), 'tp', axis=0, ti...  13.6 us
    ppermute x3, waiting for transfers between devices, gather_dp(): lax.ppermute(values, 'dp', [(i, (i - j) % dp) for i in range(dp)])  12.8 us
    ppermute x3, waiting for transfers between devices, scatter_dp(): lax.ppermute(sent, 'dp', [(i, (i + j) % dp) for i in range(dp)]).astype(F32)  12.7 us
    pallas_call x1, Pallas kernels, local(): pl.pallas_call(lambda *refs: front_kernel(hdim, *refs), grid=(nb,), in_sp...  12.5 us
  transfers between devices with their start and end apart: 39, of which 22 were waited for; matrix products, arithmetic and copies ran while one was open for 20% of the time, Pallas kernels for 13%

profile of v2, /device:TPU:0, one launch (start us, length us, event | category | flops | bytes accessed | tf_op | source)
XLA Modules:
  0.0 352.4 jit_solution(2003847701520675807)
XLA Ops:
  11.3 3.0 collective-permute-start.2
  15.1 4.5 %collective-permute-start = (bf16[16,1024]{1,0:T(8,128)(2,1)S(1)}, bf16[16,1024]{1,0:T(8,128)(2,1)S(1)}, u32[]{:S(2)}, u32[]{:S(2)}) collective-permute-start(bf16[16,1024]{1,0:T(8,128)(2,1)S(1)} %slice.117), channel_id=1, source_target_pairs={{0,8},{1,9},{2,10},{3,11},{4,12},{5,13},{6,14},{7,15},{16,24},{17,... | collective-permute-start | bytes 98312 | tf_op jit(solution)/shard_map/ppermute | solution.py:333
  23.1 12.8 %collective-permute-done.1 = bf16[8,1152]{1,0:T(8,128)(2,1)S(1)} collective-permute-done((bf16[8,1152]{1,0:T(8,128)(2,1)S(1)}, bf16[8,1152]{1,0:T(8,128)(2,1)S(1)}, u32[]{:S(2)}, u32[]{:S(2)}) %collective-permute-start.1) | collective-permute-done | bytes 18464 | tf_op jit(solution)/shard_map/ppermute | solution.py:338
  40.9 13.6 %all_gather.25 = bf16[128,1024]{1,0:T(8,128)(2,1)S(1)} all-gather(bf16[16,1024]{1,0:T(8,128)(2,1)S(1)} %collective-permute-done), channel_id=1, replica_groups=mesh['dp'=2,'cp'=2,'tp'=8] {'tp'}, dimensions={0}, use_global_device_ids=true | all-gather | bytes 294912 | tf_op jit(solution)/shard_map/all_gather | solution.py:450
  56.3 2.4 copy.22
  58.7 12.5 %front.1 = (bf16[1024,1024]{1,0:T(8,128)(2,1)}, bf16[1024,256]{1,0:T(8,128)(2,1)}, bf16[4,272,512]{2,1,0:T(8,128)(2,1)}, f32[1024,512]{1,0:T(8,128)}, bf16[1024,...) custom-call(bf16[1024,1024]{1,0:T(8,128)(2,1)} %all-gather.8.cloned., ...), custom_call_target="tpu_custom_call" | custom-call | tf_op jit(solution)/shard_map/front/pallas_call | solution.py:485
  71.2 4.5 %collective-permute-start.3 = (f32[128,256]{1,0:T(8,128)}, f32[128,256]{1,0:T(8,128)S(1)}, u32[]{:S(2)}, u32[]{:S(2)}) collective-permute-start(f32[128,256]{1,0:T(8,128)} %get-tuple-element.49), channel_id=1, source_target_pairs={{0,8},{1,9},{2,10},{3,11},{4,12},{5,13},{6,14},{7,15},{16,24},{17,... | collective-permute-start | bytes 393224 | tf_op jit(solution)/shard_map/ppermute | solution.py:333
  78.2 4.5 %intra.1.refs_2_ = f32[1024,256]{1,0:T(8,128)} custom-call(bf16[1024,256]{1,0:T(8,128)(2,1)} %get-tuple-element.42.refs_0_.refs_7_, bf16[1024,256]{1,0:T(8,128)(2,1)} %get-tuple-element.44.refs_1_, f32[1024,128]{1,0:T(8,128)} %get-tuple-element.43.refs_2_.refs_1_.refs_8_), custom_call_target="tpu_custom_call" | custom-call | tf_op jit(solution)/shard_map/intra/pallas_call | solution.py:504
  83.4 8.2 %gate.1 = (bf16[1024,256]{1,0:T(8,128)(2,1)}, bf16[1024,256]{1,0:T(8,128)(2,1)}, bf16[1024,1024]{1,0:T(8,128)(2,1)}, f32[8,1024]{1,0:T(8,128)}) custom-call(bf16[1024,256]{1,0:T(8,128)(2,1)} %get-tuple-element.42.refs_0_.refs_7_, f32[1024,128]{1,0:T(8,128)} %get-tuple-element.43.refs_2_.refs_1_.refs_8_, f32[1024,256]{1,0:T(8,128)} %intra.1.refs_2_, ...), custom_call_target="tpu_custom_call" | custom-call | tf_op jit(solution)/shard_map/gate/pallas_call | solution.py:514
  95.4 2.4 collective-permute-done.6
  98.9 2.8 collective-permute-done.7
  102.3 8.2 %back_gate.1 = (bf16[1024,256]{1,0:T(8,128)(2,1)}, bf16[1024,256]{1,0:T(8,128)(2,1)}, f32[256,1024]{1,0:T(8,128)}, f32[1024,256]{1,0:T(8,128)}, f32[8,256]{1,0:T...) custom-call(f32[8,1024]{1,0:T(8,128)} %add.243.refs_0_, ...), custom_call_target="tpu_custom_call" | custom-call | tf_op jit(solution)/shard_map/back_gate/pallas_call | solution.py:527
  112.3 3.6 %collective-permute-start.28 = (bf16[64,1024]{1,0:T(8,128)(2,1)S(1)}, bf16[64,1024]{1,0:T(8,128)(2,1)S(1)}, u32[]{:S(2)}, u32[]{:S(2)}) collective-permute-start(bf16[64,1024]{1,0:T(8,128)(2,1)S(1)} %get-tuple-element.99), channel_id=1, source_target_pairs={{0,8},{1,10},{2,12},{3,14},{4,24},{5,26},{6,28},{7,30},{8,1},{9,3}... | collective-permute-start | bytes 393224 | tf_op jit(solution)/shard_map/ppermute | solution.py:602
  116.6 5.2 %collective-permute-done.30 = bf16[64,1024]{1,0:T(8,128)(2,1)S(1)} collective-permute-done((bf16[64,1024]{1,0:T(8,128)(2,1)S(1)}, bf16[64,1024]{1,0:T(8,128)(2,1)S(1)}, u32[]{:S(2)}, u32[]{:S(2)}) %collective-permute-start.30) | collective-permute-done | bytes 131104 | tf_op jit(solution)/shard_map/ppermute | solution.py:602
  121.8 4.8 %collective-permute-done.28 = bf16[64,1024]{1,0:T(8,128)(2,1)S(1)} collective-permute-done((bf16[64,1024]{1,0:T(8,128)(2,1)S(1)}, bf16[64,1024]{1,0:T(8,128)(2,1)S(1)}, u32[]{:S(2)}, u32[]{:S(2)}) %collective-permute-start.28) | collective-permute-done | bytes 131104 | tf_op jit(solution)/shard_map/ppermute | solution.py:602
  126.8 7.0 %collective-permute-done.31 = bf16[64,1024]{1,0:T(8,128)(2,1)S(1)} collective-permute-done((bf16[64,1024]{1,0:T(8,128)(2,1)S(1)}, bf16[64,1024]{1,0:T(8,128)(2,1)S(1)}, u32[]{:S(2)}, u32[]{:S(2)}) %collective-permute-start.31) | collective-permute-done | bytes 131104 | tf_op jit(solution)/shard_map/ppermute | solution.py:361
  136.1 6.4 %back_intra.1 = (f32[1024,256]{1,0:T(8,128)}, f32[1024,256]{1,0:T(8,128)}, f32[1024,128]{1,0:T(8,128)}) custom-call(bf16[1024,256]{1,0:T(8,128)(2,1)} %get-tuple-element.42.refs_0_.refs_7_, bf16[1024,256]{1,0:T(8,128)(2,1)} %get-tuple-element.44.refs_1_, f32[1024,128]{1,0:T(8,128)} %get-tuple-element.43.refs_2_.refs_1_.refs_8_, ...), custom_call_target="tpu_custom_call" | custom-call | tf_op jit(solution)/shard_map/back_intra/pallas_call | solution.py:544
  142.5 2.7 collective-permute-done.8.refs_15_
  145.8 16.1 %back.1 = (bf16[1024,512]{1,0:T(8,128)(2,1)}, bf16[1024,128]{1,0:T(8,128)(2,1)}, f32[16,512]{1,0:T(8,128)}, f32[8,512]{1,0:T(8,128)}, f32[8,128]{1,0:T(8,128)}) custom-call(bf16[1024,256]{1,0:T(8,128)(2,1)} %get-tuple-element.42.refs_0_.refs_7_, bf16[1024,256]{1,0:T(8,128)(2,1)} %get-tuple-element.44.refs_1_, ...), custom_call_target="tpu_custom_call" | custom-call | tf_op jit(solution)/shard_map/back/pallas_call | solution.py:554
  164.6 4.2 %collective-permute-done.9 = f32[16,512]{1,0:T(8,128)S(1)} collective-permute-done((f32[16,512]{1,0:T(8,128)}, f32[16,512]{1,0:T(8,128)S(1)}, u32[]{:S(2)}, u32[]{:S(2)}) %collective-permute-start.9) | collective-permute-done | bytes 32800 | tf_op jit(solution)/shard_map/ppermute | solution.py:333
  169.6 3.2 fusion.8
  175.6 7.0 %collective-permute-start.17 = (bf16[512,256]{0,1:T(8,128)(2,1)}, bf16[512,256]{0,1:T(8,128)(2,1)}, u32[]{:S(2)}, u32[]{:S(2)}) collective-permute-start(bf16[512,256]{0,1:T(8,128)(2,1)} %dynamic-slice_convert_fusion), channel_id=1, source_target_pairs={{0,16},{16,0},{1,17},{17,1},{2,18},{18,2},{3,19},{19,3},{4,20},{20... | collective-permute-start | bytes 786440 | tf_op jit(solution)/shard_map/ppermute | solution.py:356
  182.6 4.7 %collective-permute-done.17 = bf16[512,256]{0,1:T(8,128)(2,1)} collective-permute-done((bf16[512,256]{0,1:T(8,128)(2,1)}, bf16[512,256]{0,1:T(8,128)(2,1)}, u32[]{:S(2)}, u32[]{:S(2)}) %collective-permute-start.17) | collective-permute-done | bytes 262176 | tf_op jit(solution)/shard_map/ppermute | solution.py:356
  188.6 12.2 %collective-permute-done.18 = bf16[512,256]{0,1:T(8,128)(2,1)S(1)} collective-permute-done((bf16[512,256]{0,1:T(8,128)(2,1)S(1)}, bf16[512,256]{0,1:T(8,128)(2,1)S(1)}, u32[]{:S(2)}, u32[]{:S(2)}) %collective-permute-start.18) | collective-permute-done | bytes 262176 | tf_op jit(solution)/shard_map/ppermute | solution.py:361
  200.8 1.9 add_convert_fusion
  204.5 5.8 %collective-permute-done.15 = bf16[512,256]{1,0:T(8,128)(2,1)S(1)} collective-permute-done((bf16[512,256]{1,0:T(8,128)(2,1)S(1)}, bf16[512,256]{1,0:T(8,128)(2,1)S(1)}, u32[]{:S(2)}, u32[]{:S(2)}) %collective-permute-start.15) | collective-permute-done | bytes 262176 | tf_op jit(solution)/shard_map/ppermute | solution.py:356
  211.5 10.1 %collective-permute-done.16 = bf16[512,256]{1,0:T(8,128)(2,1)S(1)} collective-permute-done((bf16[512,256]{1,0:T(8,128)(2,1)S(1)}, bf16[512,256]{1,0:T(8,128)(2,1)S(1)}, u32[]{:S(2)}, u32[]{:S(2)}) %collective-permute-start.16) | collective-permute-done | bytes 262176 | tf_op jit(solution)/shard_map/ppermute | solution.py:361
  221.6 1.8 add_convert_fusion.1
  223.5 5.8 %convolution_convert_fusion = bf16[1024,1024]{1,0:T(8,128)(2,1)} fusion(bf16[1024,896]{1,0:T(8,128)(2,1)} %bitcast.55, bf16[1024,128]{1,0:T(8,128)(2,1)} %get-tuple-element.67, bf16[16,512]{1,0:T(8,128)(2,1)S(1)} %add_convert_fusion.4, bf16[1008,512]{1,0:T(8,128)(2,1)} %copy-done.7, bf16[1024,256]{1,0:T(8,128)(2,1)} %get-tuple-element.55), kind=kOutput, calls=%fused_computation.5 | convolution fusion | flops 1887436800 | bytes 5767168 | tf_op jit(solution)/shard_map/dot_general | solution.py:19
  229.6 2.5 copy.23
  238.5 2.3 dynamic_update_slice.15
  241.0 6.9 %collective-permute-start.11 = (f32[8,2304]{1,0:T(8,128)S(1)}, f32[8,2304]{1,0:T(8,128)S(1)}, u32[]{:S(2)}, u32[]{:S(2)}) collective-permute-start(f32[8,2304]{1,0:T(8,128)S(1)} %fusion.42), channel_id=1, source_target_pairs={{0,2},{1,3},{2,0},{3,1},{4,6},{5,7},{6,4},{7,5},{8,10},{9,11},{10,... | collective-permute-start | bytes 221192 | tf_op jit(solution)/shard_map/ppermute | solution.py:361
  248.1 2.4 collective-permute-done.11
  250.5 2.3 collective-permute-done.19
  252.9 2.3 collective-permute-start.20
  257.0 19.6 %collective-permute-done.13 = f32[8,2304]{1,0:T(8,128)S(1)} collective-permute-done((f32[8,2304]{1,0:T(8,128)S(1)}, f32[8,2304]{1,0:T(8,128)S(1)}, u32[]{:S(2)}, u32[]{:S(2)}) %collective-permute-start.13) | collective-permute-done | bytes 73760 | tf_op jit(solution)/shard_map/ppermute | solution.py:361
  276.8 4.2 %collective-permute-done.14 = f32[8,2304]{1,0:T(8,128)S(1)} collective-permute-done((f32[8,2304]{1,0:T(8,128)S(1)}, f32[8,2304]{1,0:T(8,128)S(1)}, u32[]{:S(2)}, u32[]{:S(2)}) %collective-permute-start.14) | collective-permute-done | bytes 73760 | tf_op jit(solution)/shard_map/ppermute | solution.py:361
  281.9 7.4 %collective-permute-done.21 = bf16[256,384]{1,0:T(8,128)(2,1)S(1)} collective-permute-done((bf16[256,384]{1,0:T(8,128)(2,1)S(1)}, bf16[256,384]{1,0:T(8,128)(2,1)S(1)}, u32[]{:S(2)}, u32[]{:S(2)}) %collective-permute-start.21) | collective-permute-done | bytes 196640 | tf_op jit(solution)/shard_map/ppermute | solution.py:361
  289.4 3.5 collective-permute-start.22
  293.0 2.6 collective-permute-done.22
  298.6 2.1 collective-permute-start.25
  300.7 6.8 %collective-permute-done.25 = bf16[128,384]{1,0:T(8,128)(2,1)S(1)} collective-permute-done((bf16[128,384]{1,0:T(8,128)(2,1)S(1)}, bf16[128,384]{1,0:T(8,128)(2,1)S(1)}, u32[]{:S(2)}, u32[]{:S(2)}) %collective-permute-start.25) | collective-permute-done | bytes 98336 | tf_op jit(solution)/shard_map/ppermute | solution.py:361
  308.2 8.1 %collective-permute-done.26 = bf16[256,384]{1,0:T(8,128)(2,1)S(1)} collective-permute-done((bf16[256,384]{1,0:T(8,128)(2,1)S(1)}, bf16[256,384]{1,0:T(8,128)(2,1)S(1)}, u32[]{:S(2)}, u32[]{:S(2)}) %collective-permute-start.26) | collective-permute-done | bytes 196640 | tf_op jit(solution)/shard_map/ppermute | solution.py:361
  317.1 4.1 %convert_element_type.174 = f32[1024,1024]{1,0:T(8,128)} convert(bf16[1024,1024]{1,0:T(8,128)(2,1)} %all-gather.12.cloned.1.call-done) | non-fusion elementwise | flops 1048576 | bytes 6291456 | tf_op jit(solution)/shard_map/convert_element_type | solution.py:604
  321.2 4.1 %copy.25 = bf16[4096,256]{1,0:T(8,128)(2,1)} copy(bf16[4096,256]{0,1:T(8,128)(2,1)} %all-gather.16.cloned.1.call-done) | data formatting | bytes 4194304 | tf_op jit(solution)/shard_map/all_gather | solution.py:610
  325.3 7.4 %assemble.1 = f32[512,4384]{1,0:T(8,128)} custom-call(bf16[8,512,256]{2,1,0:T(8,128)(2,1)} %bitcast.57, bf16[8,512,256]{2,1,0:T(8,128)(2,1)} %bitcast.53, bf16[512,384]{1,0:T(8,128)(2,1)} %pad_maximum_fusion.1.refs_2_), custom_call_target="tpu_custom_call" | custom-call | tf_op jit(solution)/shard_map/assemble/pallas_call | solution.py:620
  332.7 9.5 %copy.28 = f32[512,4384]{0,1:T(8,128)} copy(f32[512,4384]{1,0:T(8,128)} %assemble.1) | data formatting | bytes 17956864
  343.4 2.2 fusion.23
  (219 shorter events, 55.5 us)
Async XLA Ops:
  7.2 12.4 %copy-start.17 = (bf16[1152]{0:T(1024)(128)(2,1)S(1)}, bf16[1152]{0:T(1024)(128)(2,1)}, u32[]{:S(2)}) copy-start(bf16[1152]{0:T(1024)(128)(2,1)} %param.15) | copy-start | bytes 6916
  7.2 12.4 %copy-start.19 = (bf16[512]{0:T(512)(128)(2,1)S(1)}, bf16[512]{0:T(512)(128)(2,1)}, u32[]{:S(2)}) copy-start(bf16[512]{0:T(512)(128)(2,1)} %param.12) | copy-start | bytes 3076
  7.2 12.4 %copy-start.18 = (bf16[1024]{0:T(1024)(128)(2,1)S(1)}, bf16[1024]{0:T(1024)(128)(2,1)}, u32[]{:S(2)}) copy-start(bf16[1024]{0:T(1024)(128)(2,1)} %param.19) | copy-start | bytes 6148
  7.2 12.5 %copy-start.21 = (bf16[16]{0:T(256)(128)(2,1)S(1)}, bf16[16]{0:T(256)(128)(2,1)}, u32[]{:S(2)}) copy-start(bf16[16]{0:T(256)(128)(2,1)} %param.18) | copy-start | bytes 100
  7.2 12.5 %copy-start.22 = (bf16[16]{0:T(256)(128)(2,1)S(1)}, bf16[16]{0:T(256)(128)(2,1)}, u32[]{:S(2)}) copy-start(bf16[16]{0:T(256)(128)(2,1)} %param.17) | copy-start | bytes 100
  7.2 12.5 %copy-start.23 = (bf16[16]{0:T(256)(128)(2,1)S(1)}, bf16[16]{0:T(256)(128)(2,1)}, u32[]{:S(2)}) copy-start(bf16[16]{0:T(256)(128)(2,1)} %param.16) | copy-start | bytes 100
  7.2 12.5 %copy-start.15 = (bf16[4,1152]{1,0:T(4,128)(2,1)S(1)}, bf16[4,1152]{1,0:T(4,128)(2,1)}, u32[]{:S(2)}) copy-start(bf16[4,1152]{1,0:T(4,128)(2,1)} %param.14) | copy-start | bytes 27652
  7.2 51.5 %all-gather.8.cloned.1.call-start = ((), (), s32[]{:S(2)}) async-start(), calls=%async_computation.2 | async-start | bytes 2359296 | tf_op jit(solution)/shard_map/all_gather | solution.py:449
  8.0 74.8 %all-gather.10.cloned.1.call-start = ((), (), s32[]{:S(2)}) async-start(), calls=%async_computation.3 | async-start | bytes 2359296 | tf_op jit(solution)/shard_map/all_gather | solution.py:451
  8.7 308.4 %all-gather.12.cloned.1.call-start = ((), (), s32[]{:S(2)}) async-start(), calls=%async_computation.6 | async-start | bytes 2359296 | tf_op jit(solution)/shard_map/all_gather | solution.py:604
  11.3 43.8 %collective-permute-start.2 = (bf16[512,896]{0,1:T(8,128)(2,1)S(1)}, bf16[512,896]{0,1:T(8,128)(2,1)S(1)}, u32[]{:S(2)}, u32[]{:S(2)}) collective-permute-start(bf16[512,896]{0,1:T(8,128)(2,1)S(1)} %concatenate.55), channel_id=1, source_target_pairs={{0,16},{16,0},{1,17},{17,1},{2,18},{18,2},{3,19},{19,3},{4,20},{20... | collective-permute-start | bytes 2752520 | tf_op jit(solution)/shard_map/ppermute | solution.py:338
  15.1 25.8 %collective-permute-start = (bf16[16,1024]{1,0:T(8,128)(2,1)S(1)}, bf16[16,1024]{1,0:T(8,128)(2,1)S(1)}, u32[]{:S(2)}, u32[]{:S(2)}) collective-permute-start(bf16[16,1024]{1,0:T(8,128)(2,1)S(1)} %slice.117), channel_id=1, source_target_pairs={{0,8},{1,9},{2,10},{3,11},{4,12},{5,13},{6,14},{7,15},{16,24},{17,... | collective-permute-start | bytes 98312 | tf_op jit(solution)/shard_map/ppermute | solution.py:333
  19.8 16.0 %collective-permute-start.1 = (bf16[8,1152]{1,0:T(8,128)(2,1)S(1)}, bf16[8,1152]{1,0:T(8,128)(2,1)S(1)}, u32[]{:S(2)}, u32[]{:S(2)}) collective-permute-start(bf16[8,1152]{1,0:T(8,128)(2,1)S(1)} %concatenate.54), channel_id=1, source_target_pairs={{0,16},{16,0},{1,17},{17,1},{2,18},{18,2},{3,19},{19,3},{4,20},{20... | collective-permute-start | bytes 55304 | tf_op jit(solution)/shard_map/ppermute | solution.py:338
  21.5 54.2 %collective-permute-start.4 = (bf16[256,1024]{1,0:T(8,128)(2,1)S(1)}, bf16[256,1024]{1,0:T(8,128)(2,1)}, u32[]{:S(2)}, u32[]{:S(2)}) collective-permute-start(bf16[256,1024]{1,0:T(8,128)(2,1)S(1)} %constant_dynamic-slice_fusion.9), channel_id=1, source_target_pairs={{0,16},{16,0},{1,17},{17,1},{2,18},{18,2},{3,19},{19,3},{4,20},{20... | collective-permute-start | bytes 1572872 | tf_op jit(solution)/shard_map/ppermute | solution.py:338
  71.2 11.5 %collective-permute-start.3 = (f32[128,256]{1,0:T(8,128)}, f32[128,256]{1,0:T(8,128)S(1)}, u32[]{:S(2)}, u32[]{:S(2)}) collective-permute-start(f32[128,256]{1,0:T(8,128)} %get-tuple-element.49), channel_id=1, source_target_pairs={{0,8},{1,9},{2,10},{3,11},{4,12},{5,13},{6,14},{7,15},{16,24},{17,... | collective-permute-start | bytes 393224 | tf_op jit(solution)/shard_map/ppermute | solution.py:333
  91.6 1.5 collective-permute-start.5
  93.8 3.9 %collective-permute-start.6 = (f32[8,1024]{1,0:T(8,128)S(1)}, f32[8,1024]{1,0:T(8,128)S(1)}, u32[]{:S(2)}, u32[]{:S(2)}) collective-permute-start(f32[8,1024]{1,0:T(8,128)S(1)} %add.241), channel_id=1, source_target_pairs={{0,2},{1,3},{2,0},{3,1},{4,6},{5,7},{6,4},{7,5},{8,10},{9,11},{10,... | collective-permute-start | bytes 98312 | tf_op jit(solution)/shard_map/ppermute | solution.py:361
  97.8 3.9 %collective-permute-start.7 = (f32[8,1024]{1,0:T(8,128)S(1)}, f32[8,1024]{1,0:T(8,128)S(1)}, u32[]{:S(2)}, u32[]{:S(2)}) collective-permute-start(f32[8,1024]{1,0:T(8,128)S(1)} %add.242), channel_id=1, source_target_pairs={{0,4},{1,5},{2,6},{3,7},{4,0},{5,1},{6,2},{7,3},{8,12},{9,13},{10,... | collective-permute-start | bytes 98312 | tf_op jit(solution)/shard_map/ppermute | solution.py:361
  110.5 24.1 %copy-start.25 = (f32[128,256]{1,0:T(8,128)S(1)}, f32[128,256]{1,0:T(8,128)}, u32[]{:S(2)}) copy-start(f32[128,256]{1,0:T(8,128)} %get-tuple-element.64) | copy-start | bytes 393220
  111.9 9.9 %collective-permute-start.30 = (bf16[64,1024]{1,0:T(8,128)(2,1)S(1)}, bf16[64,1024]{1,0:T(8,128)(2,1)S(1)}, u32[]{:S(2)}, u32[]{:S(2)}) collective-permute-start(bf16[64,1024]{1,0:T(8,128)(2,1)S(1)} %get-tuple-element.97), channel_id=1, source_target_pairs={{0,9},{1,11},{2,13},{3,15},{4,25},{5,27},{6,29},{7,31},{8,0},{9,2}... | collective-permute-start | bytes 393224 | tf_op jit(solution)/shard_map/ppermute | solution.py:602
  111.9 9.8 %collective-permute-start.29 = (bf16[64,1024]{1,0:T(8,128)(2,1)S(1)}, bf16[64,1024]{1,0:T(8,128)(2,1)S(1)}, u32[]{:S(2)}, u32[]{:S(2)}) collective-permute-start(bf16[64,1024]{1,0:T(8,128)(2,1)S(1)} %get-tuple-element.98), channel_id=1, source_target_pairs={{0,1},{1,3},{2,5},{3,7},{4,17},{5,19},{6,21},{7,23},{8,9},{9,11},{... | collective-permute-start | bytes 393224 | tf_op jit(solution)/shard_map/ppermute | solution.py:602
  112.3 14.3 %collective-permute-start.28 = (bf16[64,1024]{1,0:T(8,128)(2,1)S(1)}, bf16[64,1024]{1,0:T(8,128)(2,1)S(1)}, u32[]{:S(2)}, u32[]{:S(2)}) collective-permute-start(bf16[64,1024]{1,0:T(8,128)(2,1)S(1)} %get-tuple-element.99), channel_id=1, source_target_pairs={{0,8},{1,10},{2,12},{3,14},{4,24},{5,26},{6,28},{7,30},{8,1},{9,3}... | collective-permute-start | bytes 393224 | tf_op jit(solution)/shard_map/ppermute | solution.py:602
  115.9 10.7 %collective-permute-start.27 = (bf16[64,1024]{1,0:T(8,128)(2,1)S(1)}, bf16[64,1024]{1,0:T(8,128)(2,1)S(1)}, u32[]{:S(2)}, u32[]{:S(2)}) collective-permute-start(bf16[64,1024]{1,0:T(8,128)(2,1)S(1)} %get-tuple-element.96), channel_id=1, source_target_pairs={{0,0},{1,2},{2,4},{3,6},{4,16},{5,18},{6,20},{7,22},{8,8},{9,10},{... | collective-permute-start | bytes 393224 | tf_op jit(solution)/shard_map/ppermute | solution.py:602
  126.7 7.1 %collective-permute-start.31 = (bf16[64,1024]{1,0:T(8,128)(2,1)S(1)}, bf16[64,1024]{1,0:T(8,128)(2,1)S(1)}, u32[]{:S(2)}, u32[]{:S(2)}) collective-permute-start(bf16[64,1024]{1,0:T(8,128)(2,1)S(1)} %add_convert_fusion.2), channel_id=1, source_target_pairs={{0,8},{8,0},{1,9},{9,1},{2,10},{10,2},{3,11},{11,3},{4,12},{12,4},... | collective-permute-start | bytes 393224 | tf_op jit(solution)/shard_map/ppermute | solution.py:361
  134.5 186.7 %all-gather.16.cloned.1.call-start = ((), (), s32[]{:S(2)}) async-start(), calls=%async_computation.8 | async-start | bytes 2359296 | tf_op jit(solution)/shard_map/all_gather | solution.py:610
  134.6 10.6 %collective-permute-start.8 = (f32[128,256]{1,0:T(8,128)S(1)}, f32[128,256]{1,0:T(8,128)S(1)}, u32[]{:S(2)}, u32[]{:S(2)}) collective-permute-start(f32[128,256]{1,0:T(8,128)S(1)} %copy-done.25), channel_id=1, source_target_pairs={{8,0},{9,1},{10,2},{11,3},{12,4},{13,5},{14,6},{15,7},{24,16},{25,... | collective-permute-start | bytes 393224 | tf_op jit(solution)/shard_map/ppermute | solution.py:333
  161.9 6.9 %collective-permute-start.9 = (f32[16,512]{1,0:T(8,128)}, f32[16,512]{1,0:T(8,128)S(1)}, u32[]{:S(2)}, u32[]{:S(2)}) collective-permute-start(f32[16,512]{1,0:T(8,128)} %get-tuple-element.66), channel_id=1, source_target_pairs={{8,0},{9,1},{10,2},{11,3},{12,4},{13,5},{14,6},{15,7},{24,16},{25,... | collective-permute-start | bytes 98312 | tf_op jit(solution)/shard_map/ppermute | solution.py:333
  175.6 11.7 %collective-permute-start.17 = (bf16[512,256]{0,1:T(8,128)(2,1)}, bf16[512,256]{0,1:T(8,128)(2,1)}, u32[]{:S(2)}, u32[]{:S(2)}) collective-permute-start(bf16[512,256]{0,1:T(8,128)(2,1)} %dynamic-slice_convert_fusion), channel_id=1, source_target_pairs={{0,16},{16,0},{1,17},{17,1},{2,18},{18,2},{3,19},{19,3},{4,20},{20... | collective-permute-start | bytes 786440 | tf_op jit(solution)/shard_map/ppermute | solution.py:356
  188.5 12.3 %collective-permute-start.18 = (bf16[512,256]{0,1:T(8,128)(2,1)S(1)}, bf16[512,256]{0,1:T(8,128)(2,1)S(1)}, u32[]{:S(2)}, u32[]{:S(2)}) collective-permute-start(bf16[512,256]{0,1:T(8,128)(2,1)S(1)} %fusion.29), channel_id=1, source_target_pairs={{0,8},{8,0},{1,9},{9,1},{2,10},{10,2},{3,11},{11,3},{4,12},{12,4},... | collective-permute-start | bytes 786440 | tf_op jit(solution)/shard_map/ppermute | solution.py:361
  202.7 122.6 %all-gather.14.cloned.1.call-start = ((), (), s32[]{:S(2)}) async-start(), calls=%async_computation.7 | async-start | bytes 2359296 | tf_op jit(solution)/shard_map/all_gather | solution.py:609
  203.8 6.4 %collective-permute-start.15 = (bf16[512,256]{1,0:T(8,128)(2,1)S(1)}, bf16[512,256]{1,0:T(8,128)(2,1)S(1)}, u32[]{:S(2)}, u32[]{:S(2)}) collective-permute-start(bf16[512,256]{1,0:T(8,128)(2,1)S(1)} %dynamic-slice_convert_fusion.1), channel_id=1, source_target_pairs={{0,16},{16,0},{1,17},{17,1},{2,18},{18,2},{3,19},{19,3},{4,20},{20... | collective-permute-start | bytes 786440 | tf_op jit(solution)/shard_map/ppermute | solution.py:356
  211.4 10.2 %collective-permute-start.16 = (bf16[512,256]{1,0:T(8,128)(2,1)S(1)}, bf16[512,256]{1,0:T(8,128)(2,1)S(1)}, u32[]{:S(2)}, u32[]{:S(2)}) collective-permute-start(bf16[512,256]{1,0:T(8,128)(2,1)S(1)} %fusion.28), channel_id=1, source_target_pairs={{0,8},{8,0},{1,9},{9,1},{2,10},{10,2},{3,11},{11,3},{4,12},{12,4},... | collective-permute-start | bytes 786440 | tf_op jit(solution)/shard_map/ppermute | solution.py:361
  223.4 118.8 %reduce-scatter.5.cloned.1.call-start = ((), (), s32[]{:S(2)}) async-start(), calls=%async_computation.5 | async-start | bytes 2359296 | tf_op jit(solution)/shard_map/reduce_scatter | solution.py:581
  229.3 114.1 %reduce-scatter.3.cloned.1.call-start = ((), (), s32[]{:S(2)}) async-start(), calls=%async_computation.4 | async-start | bytes 2359296 | tf_op jit(solution)/shard_map/reduce_scatter | solution.py:577
  237.4 3.6 %collective-permute-start.10 = (f32[8,2304]{1,0:T(8,128)S(1)}, f32[8,2304]{1,0:T(8,128)S(1)}, u32[]{:S(2)}, u32[]{:S(2)}) collective-permute-start(f32[8,2304]{1,0:T(8,128)S(1)} %select_maximum_fusion), channel_id=1, source_target_pairs={{0,1},{1,0},{2,3},{3,2},{4,5},{5,4},{6,7},{7,6},{8,9},{9,8},{10,11... | collective-permute-start | bytes 221192 | tf_op jit(solution)/shard_map/ppermute | solution.py:361
  240.9 11.9 %collective-permute-start.19 = (bf16[512,384]{1,0:T(8,128)(2,1)S(1)}, bf16[512,384]{1,0:T(8,128)(2,1)S(1)}, u32[]{:S(2)}, u32[]{:S(2)}) collective-permute-start(bf16[512,384]{1,0:T(8,128)(2,1)S(1)} %fusion.15), channel_id=1, source_target_pairs={{0,16},{16,0},{1,17},{17,1},{2,18},{18,2},{3,19},{19,3},{4,20},{20... | collective-permute-start | bytes 1179656 | tf_op jit(solution)/shard_map/ppermute | solution.py:356
  241.0 9.4 %collective-permute-start.11 = (f32[8,2304]{1,0:T(8,128)S(1)}, f32[8,2304]{1,0:T(8,128)S(1)}, u32[]{:S(2)}, u32[]{:S(2)}) collective-permute-start(f32[8,2304]{1,0:T(8,128)S(1)} %fusion.42), channel_id=1, source_target_pairs={{0,2},{1,3},{2,0},{3,1},{4,6},{5,7},{6,4},{7,5},{8,10},{9,11},{10,... | collective-permute-start | bytes 221192 | tf_op jit(solution)/shard_map/ppermute | solution.py:361
  250.5 4.8 %collective-permute-start.12 = (f32[8,2304]{1,0:T(8,128)S(1)}, f32[8,2304]{1,0:T(8,128)S(1)}, u32[]{:S(2)}, u32[]{:S(2)}) collective-permute-start(f32[8,2304]{1,0:T(8,128)S(1)} %add.253), channel_id=1, source_target_pairs={{0,4},{1,5},{2,6},{3,7},{4,0},{5,1},{6,2},{7,3},{8,12},{9,13},{10,... | collective-permute-start | bytes 221192 | tf_op jit(solution)/shard_map/ppermute | solution.py:361
  252.9 28.1 %collective-permute-start.20 = (bf16[512,384]{1,0:T(8,128)(2,1)S(1)}, bf16[512,384]{1,0:T(8,128)(2,1)S(1)}, u32[]{:S(2)}, u32[]{:S(2)}) collective-permute-start(bf16[512,384]{1,0:T(8,128)(2,1)S(1)} %fusion.37), channel_id=1, source_target_pairs={{0,8},{8,0},{1,9},{9,1},{2,10},{10,2},{3,11},{11,3},{4,12},{12,4},... | collective-permute-start | bytes 1179656 | tf_op jit(solution)/shard_map/ppermute | solution.py:361
  255.2 21.3 %collective-permute-start.13 = (f32[8,2304]{1,0:T(8,128)S(1)}, f32[8,2304]{1,0:T(8,128)S(1)}, u32[]{:S(2)}, u32[]{:S(2)}) collective-permute-start(f32[8,2304]{1,0:T(8,128)S(1)} %add.254), channel_id=1, source_target_pairs={{0,8},{8,0},{1,9},{9,1},{2,10},{10,2},{3,11},{11,3},{4,12},{12,4},... | collective-permute-start | bytes 221192 | tf_op jit(solution)/shard_map/ppermute | solution.py:361
  276.6 4.4 %collective-permute-start.14 = (f32[8,2304]{1,0:T(8,128)S(1)}, f32[8,2304]{1,0:T(8,128)S(1)}, u32[]{:S(2)}, u32[]{:S(2)}) collective-permute-start(f32[8,2304]{1,0:T(8,128)S(1)} %add.255), channel_id=1, source_target_pairs={{0,16},{16,0},{1,17},{17,1},{2,18},{18,2},{3,19},{19,3},{4,20},{20... | collective-permute-start | bytes 221192 | tf_op jit(solution)/shard_map/ppermute | solution.py:361
  281.2 8.1 %collective-permute-start.21 = (bf16[256,384]{1,0:T(8,128)(2,1)S(1)}, bf16[256,384]{1,0:T(8,128)(2,1)S(1)}, u32[]{:S(2)}, u32[]{:S(2)}) collective-permute-start(bf16[256,384]{1,0:T(8,128)(2,1)S(1)} %select_convert_fusion), channel_id=1, source_target_pairs={{0,4},{1,5},{2,6},{3,7},{4,0},{5,1},{6,2},{7,3},{8,12},{9,13},{10,... | collective-permute-start | bytes 589832 | tf_op jit(solution)/shard_map/ppermute | solution.py:361
  289.4 6.1 %collective-permute-start.22 = (bf16[128,384]{1,0:T(8,128)(2,1)S(1)}, bf16[128,384]{1,0:T(8,128)(2,1)S(1)}, u32[]{:S(2)}, u32[]{:S(2)}) collective-permute-start(bf16[128,384]{1,0:T(8,128)(2,1)S(1)} %select_convert_fusion.1), channel_id=1, source_target_pairs={{0,2},{1,3},{2,0},{3,1},{4,6},{5,7},{6,4},{7,5},{8,10},{9,11},{10,... | collective-permute-start | bytes 294920 | tf_op jit(solution)/shard_map/ppermute | solution.py:361
  295.6 1.3 collective-permute-start.23
  296.9 1.6 collective-permute-start.24
  298.6 8.9 %collective-permute-start.25 = (bf16[128,384]{1,0:T(8,128)(2,1)S(1)}, bf16[128,384]{1,0:T(8,128)(2,1)S(1)}, u32[]{:S(2)}, u32[]{:S(2)}) collective-permute-start(bf16[128,384]{1,0:T(8,128)(2,1)S(1)} %pad_maximum_fusion.4), channel_id=1, source_target_pairs={{0,2},{1,3},{2,0},{3,1},{4,6},{5,7},{6,4},{7,5},{8,10},{9,11},{10,... | collective-permute-start | bytes 294920 | tf_op jit(solution)/shard_map/ppermute | solution.py:361
  307.6 8.7 %collective-permute-start.26 = (bf16[256,384]{1,0:T(8,128)(2,1)S(1)}, bf16[256,384]{1,0:T(8,128)(2,1)S(1)}, u32[]{:S(2)}, u32[]{:S(2)}) collective-permute-start(bf16[256,384]{1,0:T(8,128)(2,1)S(1)} %pad_maximum_fusion.3), channel_id=1, source_target_pairs={{0,4},{1,5},{2,6},{3,7},{4,0},{5,1},{6,2},{7,3},{8,12},{9,13},{10,... | collective-permute-start | bytes 589832 | tf_op jit(solution)/shard_map/ppermute | solution.py:361
  332.7 10.7 %copy-start.6 = (bf16[128,1024]{1,0:T(8,128)(2,1)S(1)}, bf16[128,1024]{1,0:T(8,128)(2,1)}, u32[]{:S(2)}) copy-start(bf16[128,1024]{1,0:T(8,128)(2,1)} %param.21) | copy-start | bytes 786436
  (17 other events, 43.8 us)
Sparse Core Ops, SparseCore 0:
  9.7 24.4 all-gather.7
  35.8 22.7 all-gather.9
  134.7 29.3 all-gather.11
  202.8 21.2 all-gather.15
  225.5 23.9 all-gather.13
  251.6 40.2 reduce-scatter.4
  294.3 32.0 reduce-scatter.2

commit v3 on v2

--- a/solution.py
+++ b/solution.py
@@ -10,7 +10,6 @@
 PRE = 16
 LANES = 128
 EPS = 1e-05
-HIGHEST = lax.Precision.HIGHEST
 F32 = jnp.float32
 BF16 = jnp.bfloat16
 
@@ -19,10 +18,14 @@
     return lax.dot_general(a, b, (((da,), (db,)), ((), ())), preferred_element_type=F32)
 
 
-def mm_exact(a, b, da=1, db=0):
-    return lax.dot_general(
-        a, b, (((da,), (db,)), ((), ())), precision=HIGHEST, preferred_element_type=F32
-    )
+def mm_parts(a, b, parts, da=1, db=0):
+    total = None
+    for _ in range(parts):
+        high = a.astype(BF16)
+        term = mm(high, b, da, db)
+        total = term if total is None else total + term
+        a = a - high.astype(F32)
+    return total
 
 
 def iota(shape, dim):
@@ -30,7 +33,7 @@
 
 
 def head_map(channels, hdim):
-    return (jnp.right_shift(iota((LANES, channels), 1), hdim.bit_length() - 1) == iota((LANES, channels), 0)).astype(F32)
+    return (jnp.right_shift(iota((LANES, channels), 1), hdim.bit_length() - 1) == iota((LANES, channels), 0)).astype(BF16)
 
 
 def unit(u):
@@ -52,7 +55,7 @@
 
 
 def front_kernel(hdim, x_ref, halo_ref, gain_ref, w_ref, cw_ref, cb_ref, sb_ref, rate_ref,
-                 normed_ref, z_ref, raw_ref, pre_ref, xs_ref, kq_ref, dtb_ref, cums_ref,
+                 normed_ref, z_ref, raw_ref, pre_ref, xs_ref, kq_ref, dtb_ref, cums_ref, expc_ref, tail_ref, stepb_ref,
                  stin_ref, cd_ref, fin_ref, dtot_ref, buf, st, cd):
     step_id = pl.program_id(0)
     ch = z_ref.shape[1]
@@ -62,7 +65,7 @@
     @pl.when(step_id == 0)
     def _():
         hn = (unit(halo_ref[...].astype(F32)) * gain).astype(BF16)
-        hp = mm(hn, w_ref[:, ch : ch + conv_ch])
+        hp = mm(hn, w_ref[ch : ch + conv_ch, :], 1, 1)
         buf[0:PRE, :] = hp.astype(BF16).astype(F32)
         st[...] = jnp.zeros_like(st)
         cd[...] = jnp.ones_like(cd)
@@ -73,7 +76,7 @@
 
     normed = (unit(x_ref[...].astype(F32)) * gain).astype(BF16)
     normed_ref[...] = normed
-    proj = mm(normed, w_ref[...])
+    proj = mm(normed, w_ref[...], 1, 1)
     z_ref[...] = proj[:, :ch].astype(BF16)
     buf[PRE : PRE + BLOCK, :] = proj[:, ch : ch + conv_ch].astype(BF16).astype(F32)
     raw_ref[0] = buf[...].astype(BF16)
@@ -86,17 +89,22 @@
     dtb_ref[...] = dtb
     step = softplus(dtb)
     logs = step * rate_ref[0:1, :]
-    lower = (iota((BLOCK, BLOCK), 0) >= iota((BLOCK, BLOCK), 1)).astype(F32)
-    cums = mm_exact(lower, logs)
+    upper = (iota((BLOCK, BLOCK), 0) <= iota((BLOCK, BLOCK), 1)).astype(BF16)
+    cums = mm_parts(logs.T[:8, :], upper, 3)
+    cums = jnp.concatenate([cums, jnp.zeros((LANES - 8, BLOCK), F32)], axis=0).T
     cums_ref[...] = cums
     hmap = head_map(ch, hdim)
-    cums_b = mm_exact(cums, hmap)
-    xs = act[:, :ch] * mm_exact(step, hmap)
+    cums_b = mm_parts(cums, hmap, 3)
+    step_b = mm_parts(step, hmap, 2)
+    stepb_ref[...] = step_b.astype(BF16)
+    xs = act[:, :ch] * step_b
     xs_ref[...] = xs.astype(BF16)
     kq = act[:, ch:].astype(BF16)
     kq_ref[...] = kq
     last = cums_b[BLOCK - 1 : BLOCK, :]
     tail = jnp.exp(last - cums_b)
+    tail_ref[...] = tail.astype(BF16)
+    expc_ref[...] = jnp.exp(cums_b).astype(BF16)
     update = mm(kq[:, : kq.shape[1] // 2], (xs * tail).astype(BF16), 0, 0)
     stin_ref[0] = st[...]
     cd_ref[0] = cd[...]
@@ -127,14 +135,12 @@
     out_ref[...] = total
 
 
-def gate_kernel(hdim, kq_ref, cums_ref, ins_ref, pre_ref, z_ref, stin_ref, cd_ref, s0_ref,
+def gate_kernel(kq_ref, expc_ref, ins_ref, pre_ref, z_ref, stin_ref, cd_ref, s0_ref,
                 skip_ref, gain_ref, ow_ref, c_ref, mo_ref, a_ref, y_ref, stat_ref):
     ns = kq_ref.shape[1] // 2
     ch = ins_ref.shape[1]
-    hmap = head_map(ch, hdim)
     st = stin_ref[0] + cd_ref[0, 0:1, :] * s0_ref[...]
-    expc = jnp.exp(mm_exact(cums_ref[...], hmap))
-    carried = expc * mm(kq_ref[:, ns:], st.astype(BF16))
+    carried = expc_ref[...].astype(F32) * mm(kq_ref[:, ns:], st.astype(BF16))
     px = pre_ref[...]
     xc = px * sigmoid(px)
     mo = (ins_ref[...] + carried + skip_ref[0:1, :] * xc).astype(BF16)
@@ -152,18 +158,17 @@
     stat_ref[...] = both.T[:8, :]
 
 
-def back_gate_kernel(hdim, inner, stat_ref, mo_ref, a_ref, z_ref, c_ref, normed_ref, gain_ref, kq_ref, cums_ref,
-                     do_ref, dz_ref, og_ref, gz_ref, gg_ref, dst_ref, rd_ref, g0_ref, dst, rd):
+def back_gate_kernel(inner, stat_ref, mo_ref, a_ref, z_ref, c_ref, normed_ref, gain_ref, kq_ref, expc_ref, w_ref,
+                     do_ref, dz_ref, og_ref, gz_ref, gg_ref, gs_ref, dst_ref, rd_ref, g0_ref, dst, rd, og, gz):
     step_id = pl.program_id(0)
     ns = kq_ref.shape[1] // 2
-    ch = mo_ref.shape[1]
 
     @pl.when(step_id == 0)
     def _():
         dst[...] = jnp.zeros_like(dst)
         rd[...] = jnp.ones_like(rd)
-        og_ref[...] = jnp.zeros_like(og_ref)
-        gz_ref[...] = jnp.zeros_like(gz_ref)
+        og[...] = jnp.zeros_like(og)
+        gz[...] = jnp.zeros_like(gz)
         gg_ref[...] = jnp.zeros_like(gg_ref)
 
     stat = jnp.concatenate([stat_ref[...], jnp.zeros((LANES - 8, BLOCK), F32)], axis=0).T
@@ -178,20 +183,28 @@
     n = gated * r
     gg_ref[0:1, :] += jnp.sum(a * n, axis=0, keepdims=True)
     dgated = r * (a - n * (r * pj))
-    og_ref[...] += mm((n * gain_ref[0:1, :]).astype(BF16), c_ref[...], 0, 0)
+    og[...] += mm((n * gain_ref[0:1, :]).astype(BF16), c_ref[...], 0, 0)
     do = (dgated * silu).astype(BF16)
     do_ref[...] = do
     dz = (dgated * mo * (sz * (1.0 + zf * (1.0 - sz)))).astype(BF16)
     dz_ref[...] = dz
-    gz_ref[...] += mm(normed_ref[...], dz, 0, 0)
-    cums_b = mm_exact(cums_ref[...], head_map(ch, hdim))
+    gz[...] += mm(dz, normed_ref[...], 0, 0)
+    expc = expc_ref[...].astype(F32)
     dst_ref[0] = dst[...]
     rd_ref[0] = rd[...]
-    decay = jnp.exp(cums_b[BLOCK - 1 : BLOCK, :])
-    carry = mm(kq_ref[:, ns:], (do.astype(F32) * jnp.exp(cums_b)).astype(BF16), 0, 0)
+    decay = expc[BLOCK - 1 : BLOCK, :]
+    carry = mm(kq_ref[:, ns:], (do.astype(F32) * expc).astype(BF16), 0, 0)
     dst[...] = dst[...] * decay + carry
     rd[...] = rd[...] * decay
     g0_ref[...] = dst[...]
+
+    @pl.when(step_id == pl.num_programs(0) - 1)
+    def _():
+        og_ref[...] = og[...].astype(BF16)
+        gz_ref[...] = gz[...].astype(BF16)
+        gs_ref[...] = jnp.broadcast_to(
+            jnp.sum(gz[...] * w_ref[...].astype(F32), axis=0, keepdims=True), gs_ref.shape
+        )
 
 
 def back_intra_kernel(hdim, heads, kq_ref, xs_ref, cums_ref, do_ref, dxs_ref, dkq_ref, str_ref):
@@ -226,7 +239,7 @@
 
 
 def back_kernel(hdim, kq_ref, xs_ref, cums_ref, dtb_ref, pre_ref, raw_ref, do_ref, dxs_ref, dkq_ref, str_ref,
-                stin_ref, cd_ref, s0_ref, dst_ref, rd_ref, inc_ref, skip_ref, cw_ref, rate_ref,
+                expc_ref, tail_ref, stepb_ref, stin_ref, cd_ref, s0_ref, dst_ref, rd_ref, inc_ref, skip_ref, cw_ref, rate_ref,
                 dx_ref, ddt_ref, halo_ref, cg_ref, hg_ref, buf, rbuf):
     step_id = pl.program_id(0)
     ns = kq_ref.shape[1] // 2
@@ -246,9 +259,7 @@
     hmap = head_map(ch, hdim)
     keys, queries = kq_ref[:, :ns], kq_ref[:, ns:]
     cums = cums_ref[...]
-    cums_b = mm_exact(cums, hmap)
-    expc = jnp.exp(cums_b)
-    tail = jnp.exp(cums_b[BLOCK - 1 : BLOCK, :] - cums_b)
+    expc, tail = expc_ref[...].astype(F32), tail_ref[...].astype(F32)
     st = stin_ref[0] + cd_ref[0, 0:1, :] * s0_ref[...]
     dst = dst_ref[0] + rd_ref[0, 0:1, :] * inc_ref[...]
     st_low, dst_low = st.astype(BF16), dst.astype(BF16)
@@ -264,21 +275,21 @@
     dtb = dtb_ref[...]
     step = softplus(dtb)
     rate = rate_ref[0:1, :]
-    dxc = mm_exact(step, hmap) * dxs + skip_ref[0:1, :] * do
-    dstep = mm_exact(xc * dxs, hmap, 1, 1)
-    arr = mm_exact(do * carried, hmap, 1, 1)
-    upd = mm_exact(xs * dxs_up, hmap, 1, 1)
+    dxc = stepb_ref[...].astype(F32) * dxs + skip_ref[0:1, :] * do
+    dstep = mm_parts(xc * dxs, hmap, 1, 1, 1)
+    arr = mm_parts(do * carried, hmap, 1, 1, 1)
+    upd = mm_parts(xs * dxs_up, hmap, 1, 1, 1)
     rows, cols = iota((BLOCK, BLOCK), 0), iota((BLOCK, BLOCK), 1)
-    through = mm_exact(jnp.sum(st * dst, axis=0, keepdims=True) * jnp.ones((8, 1), F32), hmap, 1, 1)[0:1, :]
+    through = mm_parts(jnp.sum(st * dst, axis=0, keepdims=True) * jnp.ones((8, 1), F32), hmap, 2, 1, 1)[0:1, :]
     dlogs = (
         str_ref[...]
-        + mm_exact((cols >= rows).astype(F32), arr)
-        + mm_exact((cols < rows).astype(F32), upd)
+        + mm((cols >= rows).astype(BF16), arr.astype(BF16))
+        + mm((cols < rows).astype(BF16), upd.astype(BF16))
         + jnp.exp(cums[BLOCK - 1 : BLOCK, :]) * through
     )
     ddtb = (dstep + dlogs * rate) * sigmoid(dtb)
     ddt_ref[...] = ddtb.astype(BF16)
-    dskip = mm_exact(do * xc, hmap, 1, 1)
+    dskip = mm_parts(do * xc, hmap, 1, 1, 1)
     hg_ref[0:1, :] += jnp.sum(ddtb, axis=0, keepdims=True)
     hg_ref[1:2, :] += jnp.sum(dlogs * step, axis=0, keepdims=True) * rate
     hg_ref[2:3, :] += jnp.sum(dskip, axis=0, keepdims=True)
@@ -301,13 +312,6 @@
     halo_ref[...] = halo
 
 
-def assemble_kernel(ch, inner, z_ref, x_ref, kq_ref, out_ref):
-    for k in range(z_ref.shape[0]):
-        out_ref[:, k * ch : (k + 1) * ch] = z_ref[k].astype(F32)
-        out_ref[:, inner + k * ch : inner + (k + 1) * ch] = x_ref[k].astype(F32)
-    out_ref[:, 2 * inner :] = kq_ref[:, : out_ref.shape[1] - 2 * inner].astype(F32)
-
-
 def rows_of(width, rows=BLOCK, rev=None):
     if rev is None:
         return pl.BlockSpec((rows, width), lambda i: (i, 0))
@@ -344,17 +348,56 @@
     return jnp.take(stacked, (jnp.arange(dp) - d_id) % dp, axis=0)
 
 
-def scatter_dp(values, dp, d_id, axis=0):
+def join_lanes(stacked):
+    return jnp.concatenate([stacked[i] for i in range(stacked.shape[0])], axis=1)
+
+
+def broadcast_last(values, axis, size):
+    gap = size
+    while gap > 1:
+        pairs = [(i, i - gap // 2) for i in range(size - 1, -1, -gap)]
+        values = values + lax.ppermute(values, axis, pairs)
+        gap //= 2
+    return values
+
+
+def parts_dp(values, dp, d_id, axis=0):
     size = values.shape[axis] // dp
 
     def part(index):
         return lax.dynamic_slice_in_dim(values, index * size, size, axis)
 
-    total = part(d_id)
+    received = []
     for j in range(1, dp):
         sent = part((d_id + j) % dp).astype(BF16)
-        total = total + lax.ppermute(sent, "dp", [(i, (i + j) % dp) for i in range(dp)]).astype(F32)
-    return total
+        received.append(lax.ppermute(sent, "dp", [(i, (i + j) % dp) for i in range(dp)]))
+    return part(d_id), received
+
+
+def scatter_dp(values, dp, d_id, axis=0):
+    own, received = parts_dp(values, dp, d_id, axis)
+    return own + sum(part.astype(F32) for part in received)
+
+
+def shifted_ring(values, axis, size, by):
+    return lax.ppermute(values, axis, [(i, (i + by) % size) for i in range(size)])
+
+
+def others_over(values, axis, size):
+    low = values.astype(BF16)
+    return [shifted_ring(low, axis, size, j) for j in range(1, size)]
+
+
+def in_order(parts, index, size):
+    if size == 1:
+        return parts[0]
+    if size == 2:
+        first = index == 0
+        return jnp.concatenate(
+            [jnp.where(first, parts[0], parts[1]), jnp.where(first, parts[1], parts[0])], axis=0
+        )
+    stacked = jnp.take(jnp.stack(parts), (index - jnp.arange(size)) % size, axis=0)
+    return stacked.reshape((-1,) + parts[0].shape[1:])
 
 
 def swap(values, axis, size, bit):
@@ -380,6 +423,41 @@
         values = kept + swap(sent, axis, size, bit).astype(F32)
         bit //= 2
     return values
+
+
+def gather_chips(block, size):
+    return jnp.concatenate([block] + [swap(block, "tp", size, mask) for mask in range(2, size, 2)], axis=0)
+
+
+def gather_cores(blocks, size):
+    return jnp.concatenate([blocks, swap(blocks, "tp", size, 1)], axis=0)
+
+
+def source_block(block, index, size):
+    mask = block ^ index
+    return (mask >> 1) + (mask & 1) * (size // 2)
+
+
+def scatter_cores(values, size, index):
+    blocks = values.reshape((size // 2, 2, values.shape[0] // size) + values.shape[1:])
+    side = index & 1
+    own = lax.dynamic_index_in_dim(blocks, side, 1, keepdims=False)
+    sent = lax.dynamic_index_in_dim(blocks, 1 - side, 1, keepdims=False).astype(BF16)
+    return (own.astype(F32) + swap(sent, "tp", size, 1).astype(F32)).astype(BF16)
+
+
+def scatter_chips(blocks, size, index):
+    chip = index >> 1
+
+    def block(mask):
+        return lax.dynamic_index_in_dim(blocks, chip ^ mask, 0, keepdims=False)
+
+    parts = [swap(block(mask), "tp", size, 2 * mask) for mask in range(1, size // 2)]
+    return block(0), parts
+
+
+def add_up(own, parts):
+    return own.astype(F32) + sum(part.astype(F32) for part in parts)
 
 
 def gather_over(values, axis, size, index):
@@ -425,15 +503,17 @@
         return lax.dynamic_slice_in_dim(values, start, size, axis)
 
     share = tp // dp
+    in_t = in_weight.T
+    thin = 16
     own_cols = jnp.concatenate(
         [
-            cut(in_weight, k_id * ch, ch),
-            cut(in_weight, inner + k_id * ch, ch),
-            in_weight[:, 2 * inner : 2 * inner + 2 * ns],
-            cut(in_weight, inner + conv_all + k_id * lh, lh),
-            jnp.zeros((in_weight.shape[0], LANES - lh), BF16),
+            cut(in_t, k_id * ch, ch, 0),
+            cut(in_t, inner + k_id * ch, ch, 0),
+            in_t[2 * inner : 2 * inner + 2 * ns],
+            cut(in_t, inner + conv_all + k_id * lh, lh, 0),
+            jnp.zeros((thin - lh, in_t.shape[1]), BF16),
         ],
-        axis=1,
+        axis=0,
     )
     row_size = conv_all // dp
 
@@ -444,10 +524,14 @@
     small = jnp.concatenate(
         [conv_weight, conv_bias[None], wide(norm_gain[None]), wide(gate_gain[None]), wide(heads_own)], axis=0
     )
+    tail_rows = jnp.where(k_id == tp - 1, layer_input[-PRE:], jnp.zeros((PRE, width), BF16))
+    small, own_cols, tail_rows = lax.optimization_barrier((small, own_cols, tail_rows))
     small = gather_dp(small, dp, d_id).astype(F32)
-    w = gather_dp(own_cols, dp, d_id).reshape(width, cols)
+    w_parts = gather_dp(own_cols, dp, d_id)
+    w_parts, out_weight = lax.optimization_barrier((w_parts, out_weight))
+    w = jnp.pad(join_lanes(w_parts), ((0, LANES - thin), (0, 0)))
     x_all = lax.all_gather(layer_input, "tp", axis=0, tiled=True)
-    halo = lax.all_gather(shifted(layer_input[-PRE:], "cp", cp, 1), "tp", axis=0, tiled=True)[-PRE:]
+    halo = broadcast_last(shifted(tail_rows, "cp", cp, 1), "tp", tp)
     c_all = lax.all_gather(cotangent, "tp", axis=0, tiled=True)
     ow = gather_dp(cut(out_weight, (k_id % share) * ch, ch, 0), dp, d_id)
     ow = lax.dynamic_index_in_dim(ow, k_id // share, 0, keepdims=False)
@@ -482,21 +566,25 @@
     def params(**kw):
         return pltpu.CompilerParams(dimension_semantics=("arbitrary",), **kw)
 
-    normed, z, raw, pre, xs, kq, dtb, cums, stin, cd, fin, dtot = pl.pallas_call(
+    def cost(weight):
+        return pl.CostEstimate(flops=tokens * weight * ch, transcendentals=0, bytes_accessed=tokens * weight * 3600)
+
+    normed, z, raw, pre, xs, kq, dtb, cums, expc, tail, stepb, stin, cd, fin, dtot = pl.pallas_call(
         lambda *refs: front_kernel(hdim, *refs),
         grid=(nb,),
-        in_specs=[rows_of(width), fixed(PRE, width), fixed(1, width), fixed(width, cols), fixed(8, conv_ch),
+        in_specs=[rows_of(width), fixed(PRE, width), fixed(1, width), fixed(cols, width), fixed(8, conv_ch),
                   fixed(8, conv_ch), fixed(8, LANES), fixed(8, LANES)],
         out_specs=[rows_of(width), rows_of(ch), slabs_of(PRE + BLOCK, conv_ch), rows_of(conv_ch), rows_of(ch),
-                   rows_of(2 * ns), rows_of(LANES), rows_of(LANES), slabs_of(ns, ch), slabs_of(8, ch),
-                   fixed(ns, ch), fixed(8, ch)],
+                   rows_of(2 * ns), rows_of(LANES), rows_of(LANES), rows_of(ch), rows_of(ch), rows_of(ch),
+                   slabs_of(ns, ch), slabs_of(8, ch), fixed(ns, ch), fixed(8, ch)],
         out_shape=[sds((tokens, width), BF16), sds((tokens, ch), BF16), sds((nb, PRE + BLOCK, conv_ch), BF16),
                    sds((tokens, conv_ch)), sds((tokens, ch), BF16), sds((tokens, 2 * ns), BF16),
-                   sds((tokens, LANES)), sds((tokens, LANES)), sds((nb, ns, ch)), sds((nb, 8, ch)),
+                   sds((tokens, LANES)), sds((tokens, LANES)), sds((tokens, ch), BF16), sds((tokens, ch), BF16),
+                   sds((tokens, ch), BF16), sds((nb, ns, ch)), sds((nb, 8, ch)),
                    sds((ns, ch)), sds((8, ch))],
         scratch_shapes=[pltpu.VMEM((PRE + BLOCK, conv_ch), F32), pltpu.VMEM((ns, ch), F32), pltpu.VMEM((8, ch), F32)],
         compiler_params=params(),
-        name="front",
+        name="front", cost_estimate=cost(12),
     )(x_all, halo, gain_row, w, cw, cb, sb, rate)
 
     s0 = carry_over(fin, dtot, "cp", cp, 1)
@@ -508,38 +596,60 @@
         out_specs=rows_of(ch),
         out_shape=sds((tokens, ch)),
         compiler_params=params(),
-        name="intra",
+        name="intra", cost_estimate=cost(5),
     )(kq, xs, cums)
 
     mo, a, y, stat = pl.pallas_call(
-        lambda *refs: gate_kernel(hdim, *refs),
+        gate_kernel,
         grid=(nb,),
-        in_specs=[rows_of(2 * ns), rows_of(LANES), rows_of(ch), rows_of(ch), rows_of(ch), slabs_of(ns, ch),
+        in_specs=[rows_of(2 * ns), rows_of(ch), rows_of(ch), rows_of(ch), rows_of(ch), slabs_of(ns, ch),
                   slabs_of(8, ch), fixed(ns, ch), fixed(8, ch), fixed(8, ch), fixed(ch, width), rows_of(width)],
         out_specs=[rows_of(ch), rows_of(ch), rows_of(width), pl.BlockSpec((8, BLOCK), lambda i: (0, i))],
         out_shape=[sds((tokens, ch), BF16), sds((tokens, ch), BF16), sds((tokens, width), BF16), sds((8, tokens))],
         compiler_params=params(),
-        name="gate",
-    )(kq, cums, inside, pre, z, stin, cd, s0, skip_b, own_gate, ow, c_all)
+        name="gate", cost_estimate=cost(7),
+    )(kq, expc, inside, pre, z, stin, cd, s0, skip_b, own_gate, ow, c_all)
 
     stats = sum_over(stat, "tp", tp)
-
-    do, dz, og, gz, gg, dstl, rd, g0 = pl.pallas_call(
-        lambda *refs: back_gate_kernel(hdim, inner, *refs),
+    stats, y = lax.optimization_barrier((stats, y))
+
+    do, dz, og, gz, gg, gain_z, dstl, rd, g0 = pl.pallas_call(
+        lambda *refs: back_gate_kernel(inner, *refs),
         grid=(nb,),
         in_specs=[pl.BlockSpec((8, BLOCK), lambda i: (0, nb - 1 - i)), rows_of(ch, rev=nb), rows_of(ch, rev=nb),
                   rows_of(ch, rev=nb), rows_of(width, rev=nb), rows_of(width, rev=nb), fixed(8, ch),
-                  rows_of(2 * ns, rev=nb), rows_of(LANES, rev=nb)],
-        out_specs=[rows_of(ch, rev=nb), rows_of(ch, rev=nb), fixed(ch, width), fixed(width, ch), fixed(8, ch),
+                  rows_of(2 * ns, rev=nb), rows_of(ch, rev=nb), fixed(ch, width)],
+        out_specs=[rows_of(ch, rev=nb), rows_of(ch, rev=nb), fixed(ch, width), fixed(ch, width), fixed(8, ch),
+                   fixed(8, width),
                    slabs_of(ns, ch, nb), slabs_of(8, ch, nb), fixed(ns, ch)],
-        out_shape=[sds((tokens, ch), BF16), sds((tokens, ch), BF16), sds((ch, width)), sds((width, ch)), sds((8, ch)),
+        out_shape=[sds((tokens, ch), BF16), sds((tokens, ch), BF16), sds((ch, width), BF16), sds((ch, width), BF16), sds((8, ch)),
+                   sds((8, width)),
                    sds((nb, ns, ch)), sds((nb, 8, ch)), sds((ns, ch))],
-        scratch_shapes=[pltpu.VMEM((ns, ch), F32), pltpu.VMEM((8, ch), F32)],
+        scratch_shapes=[pltpu.VMEM((ns, ch), F32), pltpu.VMEM((8, ch), F32), pltpu.VMEM((ch, width), F32),
+                        pltpu.VMEM((ch, width), F32)],
         compiler_params=params(),
-        name="back_gate",
-    )(stats, mo, a, z, c_all, normed, own_gate, kq, cums)
+        name="back_gate", cost_estimate=cost(8),
+    )(stats, mo, a, z, c_all, normed, own_gate, kq, expc, w)
 
     incoming = carry_over(g0, dtot, "cp", cp, -1)
+
+    grp = dp * cp
+    quarter = ch // grp
+    c_id = lax.axis_index("cp")
+    src = d_id * cp + c_id
+    og_parts = []
+    for j in range(grp):
+        pairs = []
+        for d in range(dp):
+            for p in range(cp):
+                for k in range(tp):
+                    piece = (d * cp + p + j) % grp
+                    slot = (k % share) * grp + piece
+                    pairs.append(((d * cp + p) * tp + k, (k // share) * cp * tp + (slot % cp) * tp + slot // cp))
+        send = cut(og, ((src + j) % grp) * quarter, quarter, 0)
+        og_parts.append(lax.ppermute(send, ("dp", "cp", "tp"), pairs))
+    gz_own, gz_parts = parts_dp(gz, dp, d_id, 1)
+    y_sum = lax.psum_scatter(y, "tp", scatter_dimension=0, tiled=True)
 
     dxs, dkq, stri = pl.pallas_call(
         lambda *refs: back_intra_kernel(hdim, lh, *refs),
@@ -548,15 +658,20 @@
         out_specs=[rows_of(ch), rows_of(2 * ns), rows_of(LANES)],
         out_shape=[sds((tokens, ch)), sds((tokens, 2 * ns)), sds((tokens, LANES))],
         compiler_params=params(),
-        name="back_intra",
+        name="back_intra", cost_estimate=cost(7),
     )(kq, xs, cums, do)
+
+    dxs, gz_parts, y_sum = lax.optimization_barrier((dxs, gz_parts, y_sum))
+    gz_own = gz_own.astype(F32) + sum(part.astype(F32) for part in gz_parts)
+    gz_others = others_over(gz_own, "cp", cp)
 
     dxbc, ddt, dhalo, cg, hg = pl.pallas_call(
         lambda *refs: back_kernel(hdim, *refs),
         grid=(nb,),
         in_specs=[rows_of(2 * ns, rev=nb), rows_of(ch, rev=nb), rows_of(LANES, rev=nb), rows_of(LANES, rev=nb),
                   rows_of(conv_ch, rev=nb), slabs_of(PRE + BLOCK, conv_ch, nb), rows_of(ch, rev=nb),
-                  rows_of(ch, rev=nb), rows_of(2 * ns, rev=nb), rows_of(LANES, rev=nb), slabs_of(ns, ch, nb),
+                  rows_of(ch, rev=nb), rows_of(2 * ns, rev=nb), rows_of(LANES, rev=nb), rows_of(ch, rev=nb),
+                  rows_of(ch, rev=nb), rows_of(ch, rev=nb), slabs_of(ns, ch, nb),
                   slabs_of(8, ch, nb), fixed(ns, ch), slabs_of(ns, ch, nb), slabs_of(8, ch, nb), fixed(ns, ch),
                   fixed(8, ch), fixed(8, conv_ch), fixed(8, LANES)],
         out_specs=[rows_of(conv_ch, rev=nb), rows_of(LANES, rev=nb), fixed(PRE, conv_ch), fixed(8, conv_ch),
@@ -565,99 +680,150 @@
                    sds((8, LANES))],
         scratch_shapes=[pltpu.VMEM((2 * PRE + BLOCK, conv_ch), F32), pltpu.VMEM((PRE + BLOCK, conv_ch), F32)],
         compiler_params=params(),
-        name="back",
-    )(kq, xs, cums, dtb, pre, raw, do, dxs, dkq, stri, stin, cd, s0, dstl, rd, incoming, skip_b, cw, rate)
+        name="back", cost_estimate=cost(9),
+    )(kq, xs, cums, dtb, pre, raw, do, dxs, dkq, stri, expc, tail, stepb, stin, cd, s0, dstl, rd, incoming, skip_b, cw, rate)
+
+    def spread(values, total, start):
+        return lax.dynamic_update_slice_in_dim(
+            jnp.zeros(values.shape[:-1] + (total,), F32), values, start, values.ndim - 1
+        )
+
+    def full(values):
+        return jnp.pad(values, ((0, 0), (0, conv_all - values.shape[1])))
 
     back_halo = shifted(dhalo, "cp", cp, -1)
-    dxbc = jnp.concatenate([dxbc[:-PRE], (dxbc[-PRE:].astype(F32) + back_halo).astype(BF16)], axis=0)
-    dproj = jnp.concatenate([dz, dxbc, ddt], axis=1)
-    dn_part = mm(dproj, w, 1, 1).astype(BF16)
-    grad_rest = mm(normed, dproj[:, ch:], 0, 0)
-
-    y_own = lax.psum_scatter(y, "tp", scatter_dimension=0, tiled=True).astype(F32)
+    rest = jnp.concatenate([dxbc, ddt], axis=1)
+    grad_main = mm(rest, normed, 0, 0)
+    og_own = sum(part.astype(F32) for part in og_parts).astype(BF16)
+    og_others = [shifted_ring(og_own, "cp", cp, j) for j in range(1, cp)]
+    dn_main = mm(jnp.concatenate([dz, rest], axis=1), w).astype(BF16)
+    back_halo, dn_main, grad_main, gz_others, og_others = lax.optimization_barrier(
+        (back_halo, dn_main, grad_main, gz_others, og_others)
+    )
+    half = width // dp
+    og_own = in_order([og_own] + og_others, c_id, cp)
+    og_rows = og_own.shape[0]
+    zg = jnp.concatenate(
+        [add_up(gz_own, gz_others).astype(BF16)] + [og_own[:, j * half : (j + 1) * half] for j in range(dp)], axis=0
+    )
+    zg = lax.all_gather(zg, "tp", axis=0, tiled=False)
+
+    halo_low = jnp.pad(back_halo.astype(BF16), ((0, 0), (0, LANES)))
+    grad_rest = grad_main + mm(halo_low, normed[-PRE:], 0, 0)
+    dn_fix = (dn_main[-PRE:].astype(F32) + mm(halo_low, w[ch:])).astype(BF16)
+    dn_part = lax.dynamic_update_slice_in_dim(dn_main, dn_fix, tokens - PRE, 0)
+
+    steps = [("tp", tp), ("dp", dp), ("cp", cp)]
+    steps = [(axis, size, 1 << i) for axis, size in steps for i in range(size.bit_length() - 1)]
+
+    def pack_next(values):
+        if steps:
+            axis, size, bit = steps.pop(0)
+            values = values + swap(values, axis, size, bit)
+        return values
+
+    x_dt = jnp.concatenate([grad_rest[:ch], grad_rest[conv_ch : conv_ch + thin]], axis=0)
+    x_own, x_parts = parts_dp(x_dt, dp, d_id, 1)
+    dn_cores = scatter_cores(dn_part, tp, k_id)
+    kq_cores = scatter_cores(grad_rest[ch:conv_ch], tp, k_id)
+    x_parts, dn_cores, kq_cores, grad_rest = lax.optimization_barrier((x_parts, dn_cores, kq_cores, grad_rest))
+    x_own = add_up(x_own, x_parts)
+    x_others = others_over(x_own, "cp", cp)
+    dn_own, dn_parts = scatter_chips(dn_cores, tp, k_id)
+    kq_own, kq_parts = scatter_chips(kq_cores, tp, k_id)
+
+    conv_part = jnp.concatenate([spread(cg[: taps + 1, :ch], inner, k_id * ch), cg[: taps + 1, ch:]], axis=1)
+    gate_part = spread(gg[0:1] / own_gate[0:1], inner, k_id * ch)
+    head_part = spread(hg[0:3, :lh], heads, k_id * lh).reshape(1, 3 * heads)
+    gain_part = (gain_z[0:1] + jnp.sum(grad_rest * w[ch:].astype(F32), axis=0, keepdims=True)) / gain_row
+    pack = jnp.concatenate([conv_part, full(gate_part), full(head_part), full(gain_part)], axis=0)
+    pack = pack_next(pack)
+    kq_parts, pack = lax.optimization_barrier((kq_parts, pack))
+    kq_sum = scatter_dp(add_up(kq_own, kq_parts), dp, d_id, 1)
+    pack = pack_next(pack)
+    x_others, kq_sum, pack, dn_parts = lax.optimization_barrier((x_others, kq_sum, pack, dn_parts))
+    xg = lax.all_gather(add_up(x_own, x_others).astype(BF16), "tp", axis=0, tiled=False)
+    dn_sum = add_up(dn_own, dn_parts)
+    kq_sum = sum_over(kq_sum, "cp", cp, BF16)
+    pack = pack_next(pack)
+    kq_sum, pack = lax.optimization_barrier((kq_sum, pack))
+    kqg = gather_chips(kq_sum.astype(BF16), tp)
+    pack = pack_next(pack)
+    kqg, pack = lax.optimization_barrier((kqg, pack))
+    kqg = gather_cores(kqg, tp)
+    while steps:
+        pack = pack_next(pack)
+    place = source_block(jnp.arange(tp, dtype=jnp.int32), k_id, tp)
+    kqg = jnp.take(kqg.reshape(tp, -1, kqg.shape[1]), place, axis=0).reshape(kqg.shape)
+
+    y_own = y_sum.astype(F32)
     r_own = lax.rsqrt(cut(stats, k_id * own_rows, own_rows)[0] * (1.0 / inner) + EPS)[:, None]
     u = layer_input.astype(F32)
     layer_output = (u + y_own * r_own).astype(BF16)
-    dn = lax.psum_scatter(dn_part, "tp", scatter_dimension=0, tiled=True).astype(F32)
+    dn = dn_sum
     q = lax.rsqrt(jnp.mean(u * u, axis=-1, keepdims=True) + EPS)
     m = u * q
     dg = dn * gain_row
     input_grad = cotangent.astype(F32) + q * (dg - m * jnp.mean(dg * m, axis=-1, keepdims=True))
 
-    grp = dp * cp
-    quarter = ch // grp
-    c_id = lax.axis_index("cp")
-    src = d_id * cp + c_id
-    og_low = og.astype(BF16)
-    og_own = jnp.zeros((quarter, width), F32)
-    for j in range(grp):
-        pairs = []
-        for d in range(dp):
-            for p in range(cp):
-                for k in range(tp):
-                    piece = (d * cp + p + j) % grp
-                    slot = (k % share) * grp + piece
-                    pairs.append(((d * cp + p) * tp + k, (k // share) * cp * tp + (slot % cp) * tp + slot // cp))
-        send = cut(og_low, ((src + j) % grp) * quarter, quarter, 0)
-        og_own = og_own + lax.ppermute(send, ("dp", "cp", "tp"), pairs).astype(F32)
-    og_own = gather_over(og_own.astype(BF16), "cp", cp, c_id)
-    out_grad = lax.all_gather(og_own, "tp", axis=0, tiled=True).astype(F32)
-
-    def total_of(values):
-        return sum_over(scatter_dp(values, dp, d_id), "cp", cp, BF16)
-
-    zg = lax.all_gather(total_of(gz).astype(BF16), "tp", axis=0, tiled=False)
-    xg = lax.all_gather(total_of(grad_rest[:, :ch]).astype(BF16), "tp", axis=0, tiled=False)
-    dt_grad = lax.dynamic_update_slice_in_dim(
-        jnp.zeros((width, LANES), F32), grad_rest[:, ch + 2 * ns : ch + 2 * ns + lh], k_id * lh, 1
-    )
-    kqg = total_of(jnp.concatenate([grad_rest[:, ch : ch + 2 * ns], dt_grad], axis=1))
-    kqg = scatter_over(kqg, "tp", tp, k_id).astype(BF16)
-    kqg = gather_over(kqg, "tp", tp, k_id)
-    half = kqg.shape[0]
-    tile = 64
     proj_all = in_weight.shape[1]
+    grid_shape = sds((proj_all, half))
+
+    def widen_out_kernel(src_ref, out_ref):
+        for j in range(dp):
+            out_ref[:, j * half : (j + 1) * half] = src_ref[0, j * og_rows : (j + 1) * og_rows, :].astype(F32)
+
+    def widen_pair_kernel(src_ref, *refs):
+        out_ref = refs[-1]
+        out_ref[:ch, :] = src_ref[0, :ch, :].astype(F32)
+        out_ref[ch:, :] = src_ref[1, :ch, :].astype(F32)
+
+    out_grad = pl.pallas_call(
+        widen_out_kernel, grid=(tp,),
+        in_specs=[pl.BlockSpec((1, ch, half), lambda i: (i, 1, 0))], out_specs=rows_of(width, og_rows),
+        out_shape=sds((tp * og_rows, width)), compiler_params=params(), name="widen_out", cost_estimate=cost(6),
+    )(zg)
     in_grad = pl.pallas_call(
-        lambda *refs: assemble_kernel(ch, inner, *refs),
-        grid=(half // tile,),
-        in_specs=[pl.BlockSpec((tp, tile, ch), lambda i: (0, i, 0)), pl.BlockSpec((tp, tile, ch), lambda i: (0, i, 0)),
-                  rows_of(2 * ns + LANES, tile)],
-        out_specs=rows_of(proj_all, tile),
-        out_shape=sds((half, proj_all)),
-        compiler_params=params(),
-        name="assemble",
-    )(zg, xg, kqg)
-
-    gain_part = jnp.sum(jnp.concatenate([gz, grad_rest], axis=1) * w.astype(F32), axis=1) / gain
-
-    def spread(values, total, start):
-        return lax.dynamic_update_slice_in_dim(
-            jnp.zeros(values.shape[:-1] + (total,), F32), values, start, values.ndim - 1
-        )
-
-    def spread_conv(values):
-        return jnp.concatenate([spread(values[:, :ch], inner, k_id * ch), values[:, ch:]], axis=1)
-
-    def full(values):
-        return jnp.pad(values, ((0, 0), (0, conv_all - values.shape[1])))
-
-    conv_part = spread_conv(cg[: taps + 1])
-    gate_part = spread(gg[0:1] / own_gate[0:1], inner, k_id * ch)
-    head_part = spread(hg[0:3, :lh], heads, k_id * lh).reshape(1, 3 * heads)
-    pack = jnp.concatenate([conv_part, full(gate_part), full(gain_part[None]), full(head_part)], axis=0)
-    pack = sum_over(sum_over(sum_over(pack, "tp", tp), "cp", cp), "dp", dp)
+        widen_pair_kernel, grid=(tp // 2,),
+        in_specs=[pl.BlockSpec((2, ch, half), lambda i: (i, 0, 0))], out_specs=rows_of(half, 2 * ch),
+        out_shape=grid_shape, compiler_params=params(), name="widen_z", cost_estimate=cost(5),
+    )(zg)
+    xg, in_grad, out_grad, input_grad = lax.optimization_barrier((xg, in_grad, out_grad, input_grad))
+
+    in_grad = pl.pallas_call(
+        widen_pair_kernel, grid=(tp // 2,),
+        in_specs=[pl.BlockSpec((2, ch + thin, half), lambda i: (i, 0, 0)), pl.BlockSpec(memory_space=pl.ANY)],
+        out_specs=pl.BlockSpec((2 * ch, half), lambda i: (i + tp // 2, 0)),
+        out_shape=grid_shape, input_output_aliases={1: 0}, compiler_params=params(), name="widen_x", cost_estimate=cost(5),
+    )(xg, in_grad)
+    last = jnp.concatenate([kqg, xg[:, ch : ch + lh].reshape(heads, half)], axis=0)
+    strip = last.shape[0]
+
+    def last_kernel(src_ref, old_ref, out_ref, wide_ref, sem):
+        wide_ref[...] = src_ref[...].astype(F32)
+        copy = pltpu.make_async_copy(wide_ref, out_ref.at[pl.ds(proj_all - strip, strip)], sem)
+        copy.start()
+        copy.wait()
+
+    in_grad = pl.pallas_call(
+        last_kernel,
+        in_specs=[pl.BlockSpec(memory_space=pltpu.VMEM), pl.BlockSpec(memory_space=pl.ANY)],
+        out_specs=pl.BlockSpec(memory_space=pl.ANY),
+        out_shape=grid_shape, input_output_aliases={1: 0},
+        scratch_shapes=[pltpu.VMEM((strip, half), F32), pltpu.SemaphoreType.DMA], name="widen_kq",
+    )(last, in_grad).T
 
     def own(values):
         size = values.shape[-1] // dp
         return lax.dynamic_slice_in_dim(values, d_id * size, size, values.ndim - 1)
 
     conv_own = own(pack[: taps + 1])
-    head_own = own(pack[taps + 3, : 3 * heads].reshape(3, heads))
-    gate_all, gain_all = pack[taps + 1, :inner], pack[taps + 2, :width]
+    head_own = own(pack[taps + 2, : 3 * heads].reshape(3, heads))
+    gate_all = pack[taps + 1, :inner]
     return (
         layer_output,
         input_grad,
-        own(gain_all),
+        own(pack[taps + 3, :width]),
         in_grad,
         conv_own[:taps],
         conv_own[taps],

time: 354 us -> 259 us (0.73)
  waiting for transfers between devices: 131 us -> 64.5 us
  local copies, waits for them, and re-layouts: 45.1 us -> 22.5 us
  starting transfers between devices: 49.7 us -> 64 us
  blocking collectives: 13.6 us -> 0 us
  other arithmetic: 25.5 us -> 17.8 us
    ppermute x18 -> x21, waiting for transfers between devices: 87.4 us -> 29 us  [swap(): return lax.ppermute(values, axis, [(i, i ^ bit) for i in range(size)])]
    all_gather x1 -> x0, blocking collectives: 13.6 us -> none  [local(): lax.all_gather(shifted(layer_input[-PRE:], 'cp', cp, 1), 'tp', axis=0, ti...]
    unnamed x56 -> x40, local copies, waits for them, and re-layouts: 15.2 us -> 2.68 us
    ppermute x7 -> x13, waiting for transfers between devices: 22.7 us -> 10.4 us  [the longest x3 8.96 us: parts_dp(): lax.ppermute(sent, 'dp', [(i, (i + j) % dp) for i in range(dp)])]
    reduce_scatter x2 -> x1, waiting for transfers between devices: 0.02 us -> 11 us  [local(): y_sum = lax.psum_scatter(y, 'tp', scatter_dimension=0, tiled=True)]
    ppermute x7 -> x13, starting transfers between devices: 12.5 us -> 22.9 us  [the longest x3 8.11 us: shifted_ring(): lax.ppermute(values, axis, [(i, (i + by) % size) for i in range(size)])]
    convert_element_type x11 -> x8, other arithmetic: 10.1 us -> 1.69 us  [the longest x1 0.82 us: local(): add_up(x_own, x_others).astype(BF16)]
    ppermute x18 -> x21, starting transfers between devices: 19.7 us -> 28 us  [swap(): return lax.ppermute(values, axis, [(i, i ^ bit) for i in range(size)])]
  transfers between devices with their start and end apart: 39 -> 46, of which waited for: 22 -> 17; matrix products, arithmetic and copies ran while one was open for 20% -> 17% of each run, Pallas kernels for 13% -> 19%
where the time goes in v3:
time: 259 us; the launch traced here: 257 us
  waiting for transfers between devices  64.5 us (25%)
  starting transfers between devices  64 us (25%)
  Pallas kernels  62 us (24%)
  local copies, waits for them, and re-layouts  22.5 us (9%)
  other arithmetic  17.8 us (7%)
  between operations  14.7 us (6%)
  matrix products  11.2 us (4%)
    ppermute x21, waiting for transfers between devices, swap(): return lax.ppermute(values, axis, [(i, i ^ bit) for i in range(size)])  29 us
    ppermute x21, starting transfers between devices, swap(): return lax.ppermute(values, axis, [(i, i ^ bit) for i in range(size)])  28 us
    ppermute x3, waiting for transfers between devices, gather_dp(): lax.ppermute(values, 'dp', [(i, (i - j) % dp) for i in range(dp)])  13.3 us
    pallas_call x1, Pallas kernels, local(): pl.pallas_call(lambda *refs: front_kernel(hdim, *refs), grid=(nb,), in_sp...  11.4 us
    dot_general x4, matrix products, mm(): lax.dot_general(a, b, (((da,), (db,)), ((), ())), preferred_element_type=...  11.2 us
    reduce_scatter x1, waiting for transfers between devices, local(): y_sum = lax.psum_scatter(y, 'tp', scatter_dimension=0, tiled=True)  11 us
    ppermute x3, waiting for transfers between devices, parts_dp(): lax.ppermute(sent, 'dp', [(i, (i + j) % dp) for i in range(dp)])  8.96 us
    pallas_call x1, Pallas kernels, local(): pl.pallas_call(lambda *refs: back_kernel(hdim, *refs), grid=(nb,), in_spe...  8.79 us
  transfers between devices with their start and end apart: 46, of which 17 were waited for; matrix products, arithmetic and copies ran while one was open for 17% of the time, Pallas kernels for 19%

profile of v3, /device:TPU:0, one launch (start us, length us, event | category | flops | bytes accessed | tf_op | source)
XLA Modules:
  0.0 256.7 jit_solution(17167747089196402290)
XLA Ops:
  14.8 3.0 %collective-permute-start.4 = (bf16[8,1152]{1,0:T(8,128)(2,1)S(1)}, bf16[8,1152]{1,0:T(8,128)(2,1)S(1)}, u32[]{:S(2)}, u32[]{:S(2)}) collective-permute-start(bf16[8,1152]{1,0:T(8,128)(2,1)S(1)} %concatenate.50), channel_id=1, source_target_pairs={{0,16},{16,0},{1,17},{17,1},{2,18},{18,2},{3,19},{19,3},{4,20},{20... | collective-permute-start | bytes 55304 | tf_op jit(solution)/shard_map/ppermute | solution.py:342
  17.8 4.5 %collective-permute-start = (bf16[16,1024]{1,0:T(8,128)(2,1)S(1)}, bf16[16,1024]{1,0:T(8,128)(2,1)S(1)}, u32[]{:S(2)}, u32[]{:S(2)}) collective-permute-start(bf16[16,1024]{1,0:T(8,128)(2,1)S(1)} %slice_select_fusion), channel_id=1, source_target_pairs={{0,8},{1,9},{2,10},{3,11},{4,12},{5,13},{6,14},{7,15},{16,24},{17,... | collective-permute-start | bytes 98312 | tf_op jit(solution)/shard_map/ppermute | solution.py:337
  28.1 13.3 %collective-permute-done.5 = bf16[784,512]{1,0:T(8,128)(2,1)S(1)} collective-permute-done((bf16[784,512]{1,0:T(8,128)(2,1)S(1)}, bf16[784,512]{1,0:T(8,128)(2,1)S(1)}, u32[]{:S(2)}, u32[]{:S(2)}) %collective-permute-start.5) | collective-permute-done | bytes 802848 | tf_op jit(solution)/shard_map/ppermute | solution.py:342
  47.6 1.5 fusion.3.refs_3_.refs_9_
  49.1 11.4 %front.1 = (bf16[1024,1024]{1,0:T(8,128)(2,1)}, bf16[1024,256]{1,0:T(8,128)(2,1)}, bf16[4,272,512]{2,1,0:T(8,128)(2,1)}, f32[1024,512]{1,0:T(8,128)}, bf16[1024,...) custom-call(bf16[1024,1024]{1,0:T(8,128)(2,1)} %all-gather.7.cloned., ...), custom_call_target="tpu_custom_call" | custom-call | flops 3145728 | bytes 44236800 | tf_op jit(solution)/shard_map/front/pallas_call | solution.py:572
  60.6 1.5 collective-permute-start.6
  64.6 4.5 %intra.1.ins_ref = f32[1024,256]{1,0:T(8,128)} custom-call(bf16[1024,256]{1,0:T(8,128)(2,1)} %get-tuple-element.87.refs_0_.kq_ref.refs_7_, bf16[1024,256]{1,0:T(8,128)(2,1)} %get-tuple-element.88.refs_1_, f32[1024,128]{1,0:T(8,128)} %get-tuple-element.89.refs_2_), custom_call_target="tpu_custom_call" | custom-call | flops 1310720 | bytes 18432000 | tf_op jit(solution)/shard_map/intra/pallas_call | solution.py:592
  69.7 6.5 %gate.1 = (bf16[1024,256]{1,0:T(8,128)(2,1)}, bf16[1024,256]{1,0:T(8,128)(2,1)}, bf16[1024,1024]{1,0:T(8,128)(2,1)}, f32[8,1024]{1,0:T(8,128)}) custom-call(bf16[1024,256]{1,0:T(8,128)(2,1)} %get-tuple-element.87.refs_0_.kq_ref.refs_7_, bf16[1024,256]{1,0:T(8,128)(2,1)} %get-tuple-element.90.expc_ref.refs_8_.refs_10_, f32[1024,256]{1,0:T(8,128)} %intra.1.ins_ref, ...), custom_call_target="tpu_custom_call" | custom-call | flops 1835008 | bytes 25804800 | tf_op jit(solution)/shard_map/gate/pallas_call | solution.py:602
  78.5 1.5 collective-permute-start.9
  80.0 2.4 collective-permute-done.9
  82.4 1.6 collective-permute-start.10
  84.0 2.3 collective-permute-done.10
  87.1 8.1 %back_gate.1 = (bf16[1024,256]{1,0:T(8,128)(2,1)}, bf16[1024,256]{1,0:T(8,128)(2,1)}, bf16[256,1024]{1,0:T(8,128)(2,1)}, bf16[256,1024]{1,0:T(8,128)(2,1)}, f32[...) custom-call(f32[8,1024]{1,0:T(8,128)} %add.333.refs_0_, ...), custom_call_target="tpu_custom_call" | custom-call | flops 2097152 | bytes 29491200 | tf_op jit(solution)/shard_map/back_gate/pallas_call | solution.py:616
  97.1 2.5 collective-permute-start.18
  99.6 1.6 collective-permute-start.17
  101.2 2.7 %collective-permute-start.16 = (bf16[64,1024]{1,0:T(8,128)(2,1)S(1)}, bf16[64,1024]{1,0:T(8,128)(2,1)S(1)}, u32[]{:S(2)}, u32[]{:S(2)}) collective-permute-start(bf16[64,1024]{1,0:T(8,128)(2,1)S(1)} %get-tuple-element.174), channel_id=1, source_target_pairs={{0,8},{1,10},{2,12},{3,14},{4,24},{5,26},{6,28},{7,30},{8,1},{9,3}... | collective-permute-start | bytes 393224 | tf_op jit(solution)/shard_map/ppermute | solution.py:650
  104.8 1.5 collective-permute-start.11
  106.3 6.4 %back_intra.1 = (f32[1024,256]{1,0:T(8,128)}, f32[1024,256]{1,0:T(8,128)}, f32[1024,128]{1,0:T(8,128)}) custom-call(bf16[1024,256]{1,0:T(8,128)(2,1)} %get-tuple-element.87.refs_0_.kq_ref.refs_7_, bf16[1024,256]{1,0:T(8,128)(2,1)} %get-tuple-element.88.refs_1_, f32[1024,128]{1,0:T(8,128)} %get-tuple-element.89.refs_2_, ...), custom_call_target="tpu_custom_call" | custom-call | flops 1835008 | bytes 25804800 | tf_op jit(solution)/shard_map/back_intra/pallas_call | solution.py:654
  115.6 2.2 collective-permute-start.19
  117.8 11.0 %reduce-scatter.2.cloned.1.call-done = bf16[128,1024]{1,0:T(8,128)(2,1)} async-done(((bf16[1024,1024]{1,0:T(8,128)(2,1)}), bf16[128,1024]{1,0:T(8,128)(2,1)}) %reduce-scatter.2.cloned.1.call-update) | async-done | bytes 262160 | tf_op jit(solution)/shard_map/reduce_scatter | solution.py:652
  129.4 8.8 %back.1 = (bf16[1024,512]{1,0:T(8,128)(2,1)}, bf16[1024,128]{1,0:T(8,128)(2,1)}, f32[16,512]{1,0:T(8,128)}, f32[8,512]{1,0:T(8,128)}, f32[8,128]{1,0:T(8,128)}) custom-call(bf16[1024,256]{1,0:T(8,128)(2,1)} %get-tuple-element.87.refs_0_.kq_ref.refs_7_, bf16[1024,256]{1,0:T(8,128)(2,1)} %get-tuple-element.88.refs_1_, f32[1024,128]{1,0:T(8,128)} %get-tuple-element.89.refs_2_, ...), custom_call_target="tpu_custom_call" | custom-call | flops 2359296 | bytes 33177600 | tf_op jit(solution)/shard_map/back/pallas_call | solution.py:668
  140.6 3.6 %collective-permute-start.14 = (bf16[256,512]{1,0:T(8,128)(2,1)S(1)}, bf16[256,512]{1,0:T(8,128)(2,1)S(1)}, u32[]{:S(2)}, u32[]{:S(2)}) collective-permute-start(bf16[256,512]{1,0:T(8,128)(2,1)S(1)} %fusion.32), channel_id=1, source_target_pairs={{0,8},{8,0},{1,9},{9,1},{2,10},{10,2},{3,11},{11,3},{4,12},{12,4},... | collective-permute-start | bytes 786440 | tf_op jit(solution)/shard_map/ppermute | solution.py:383
  144.2 5.2 %convolution_convert_fusion = bf16[1024,1024]{1,0:T(8,128)(2,1)} fusion(bf16[1024,128]{1,0:T(8,128)(2,1)} %get-tuple-element.121, bf16[1024,512]{1,0:T(8,128)(2,1)} %get-tuple-element.120, bf16[1024,256]{1,0:T(8,128)(2,1)} %get-tuple-element.119, bf16[784,512]{1,0:T(8,128)(2,1)S(1)} %copy-done.5, bf16[784,512]{1,0:T(8,128)(2,1)S(1)} %get-tuple-element.162), kind=kOutput, calls=%fused_computation.7 | convolution fusion | flops 1892024320 | bytes 5537792 | tf_op jit(solution)/shard_map/dot_general | solution.py:18
  149.4 3.1 %fusion.9 = f32[640,1024]{1,0:T(8,128)} fusion(bf16[1024,1024]{1,0:T(8,128)(2,1)S(1)} %copy-done.2, bf16[1024,128]{1,0:T(8,128)(2,1)S(1)} %copy-done.13, bf16[1024,512]{1,0:T(8,128)(2,1)S(1)} %copy-done.10), kind=kOutput, calls=%fused_computation.17 | convolution fusion | flops 1344798720 | bytes 6029312 | tf_op jit(solution)/shard_map/dot_general | solution.py:18
  154.6 1.6 fusion.37
  157.7 5.0 %collective-permute-start.21 = (bf16[4,128,1024]{2,1,0:T(8,128)(2,1)S(1)}, bf16[4,128,1024]{2,1,0:T(8,128)(2,1)S(1)}, u32[]{:S(2)}, u32[]{:S(2)}) collective-permute-start(bf16[4,128,1024]{2,1,0:T(8,128)(2,1)S(1)} %dynamic-slice_bitcast_fusion), channel_id=1, source_target_pairs={{0,1},{1,0},{2,3},{3,2},{4,5},{5,4},{6,7},{7,6},{8,9},{9,8},{10,11... | collective-permute-start | bytes 3145736 | tf_op jit(solution)/shard_map/ppermute | solution.py:404
  165.6 1.6 collective-permute-start.20
  167.7 6.6 %collective-permute-done.20 = bf16[272,512]{1,0:T(8,128)(2,1)S(1)} collective-permute-done((bf16[272,512]{1,0:T(8,128)(2,1)S(1)}, bf16[272,512]{1,0:T(8,128)(2,1)S(1)}, u32[]{:S(2)}, u32[]{:S(2)}) %collective-permute-start.20) | collective-permute-done | bytes 278560 | tf_op jit(solution)/shard_map/ppermute | solution.py:373
  176.2 3.2 %collective-permute-start.25 = (bf16[32,1024]{1,0:T(8,128)(2,1)S(1)}, bf16[32,1024]{1,0:T(8,128)(2,1)S(1)}, u32[]{:S(2)}, u32[]{:S(2)}) collective-permute-start(bf16[32,1024]{1,0:T(8,128)(2,1)S(1)} %get-tuple-element.180), channel_id=1, source_target_pairs={{0,4},{1,5},{2,6},{3,7},{4,0},{5,1},{6,2},{7,3},{8,12},{9,13},{10,... | collective-permute-start | bytes 196616 | tf_op jit(solution)/shard_map/ppermute | solution.py:404
  179.5 2.3 collective-permute-start.23
  181.9 1.5 collective-permute-start.32
  183.5 3.3 %collective-permute-start.31 = (bf16[128,1024]{1,0:T(8,128)(2,1)S(1)}, bf16[128,1024]{1,0:T(8,128)(2,1)S(1)}, u32[]{:S(2)}, u32[]{:S(2)}) collective-permute-start(bf16[128,1024]{1,0:T(8,128)(2,1)S(1)} %get-tuple-element.167), channel_id=1, source_target_pairs={{0,4},{1,5},{2,6},{3,7},{4,0},{5,1},{6,2},{7,3},{8,12},{9,13},{10,... | collective-permute-start | bytes 786440 | tf_op jit(solution)/shard_map/ppermute | solution.py:404
  186.8 5.7 %collective-permute-done.25 = bf16[32,1024]{1,0:T(8,128)(2,1)S(1)} collective-permute-done((bf16[32,1024]{1,0:T(8,128)(2,1)S(1)}, bf16[32,1024]{1,0:T(8,128)(2,1)S(1)}, u32[]{:S(2)}, u32[]{:S(2)}) %collective-permute-start.25) | collective-permute-done | bytes 65568 | tf_op jit(solution)/shard_map/ppermute | solution.py:404
  192.6 1.7 collective-permute-start.28
  194.3 2.3 collective-permute-done.28
  196.6 2.0 collective-permute-start.29
  198.6 7.3 %collective-permute-done.29 = f32[8,2304]{1,0:T(8,128)S(1)} collective-permute-done((f32[8,2304]{1,0:T(8,128)S(1)}, f32[8,2304]{1,0:T(8,128)S(1)}, u32[]{:S(2)}, u32[]{:S(2)}) %collective-permute-start.29) | collective-permute-done | bytes 73760 | tf_op jit(solution)/shard_map/ppermute | solution.py:404
  207.9 2.5 collective-permute-start.33
  211.6 1.6 collective-permute-done.33
  213.2 1.6 collective-permute-done.34
  214.8 1.7 collective-permute-start.37
  216.5 1.6 collective-permute-start.36
  220.0 1.8 collective-permute-done.36
  224.8 3.6 %collective-permute-done.39 = f32[8,2304]{1,0:T(8,128)S(1)} collective-permute-done((f32[8,2304]{1,0:T(8,128)S(1)}, f32[8,2304]{1,0:T(8,128)S(1)}, u32[]{:S(2)}, u32[]{:S(2)}) %collective-permute-start.39) | collective-permute-done | bytes 73760 | tf_op jit(solution)/shard_map/ppermute | solution.py:404
  232.3 4.2 %widen_z.1.refs_0_ = f32[4384,512]{1,0:T(8,128)} custom-call(bf16[8,512,512]{2,1,0:T(8,128)(2,1)} %bitcast.97), custom_call_target="tpu_custom_call" | custom-call | flops 1310720 | bytes 18432000 | tf_op jit(solution)/shard_map/widen_z/pallas_call | solution.py:786
  236.5 6.0 %widen_out.1 = f32[1024,1024]{1,0:T(8,128)} custom-call(bf16[8,512,512]{2,1,0:T(8,128)(2,1)} %bitcast.98), custom_call_target="tpu_custom_call" | custom-call | flops 1572864 | bytes 22118400 | tf_op jit(solution)/shard_map/widen_out/pallas_call | solution.py:781
  243.4 4.2 %widen_x.1.old_ref = f32[4384,512]{1,0:T(8,128)} custom-call(bf16[8,272,512]{2,1,0:T(8,128)(2,1)} %bitcast.102, f32[4384,512]{1,0:T(8,128)} %widen_z.1.refs_0_), custom_call_target="tpu_custom_call", output_to_operand_aliasing={{}: (1, {})} | custom-call | flops 1310720 | bytes 18432000 | tf_op jit(solution)/shard_map/widen_x/pallas_call | solution.py:793
  248.4 1.8 widen_kq.1
  (225 shorter events, 56.2 us)
Async XLA Ops:
  7.2 42.0 %all-gather.7.cloned.1.call-start = ((), (), s32[]{:S(2)}) async-start(), calls=%async_computation.1 | async-start | bytes 2359296 | tf_op jit(solution)/shard_map/all_gather | solution.py:533
  7.9 61.2 %all-gather.9.cloned.1.call-start = ((), (), s32[]{:S(2)}) async-start(), calls=%async_computation.2 | async-start | bytes 2359296 | tf_op jit(solution)/shard_map/all_gather | solution.py:535
  14.8 8.2 %collective-permute-start.4 = (bf16[8,1152]{1,0:T(8,128)(2,1)S(1)}, bf16[8,1152]{1,0:T(8,128)(2,1)S(1)}, u32[]{:S(2)}, u32[]{:S(2)}) collective-permute-start(bf16[8,1152]{1,0:T(8,128)(2,1)S(1)} %concatenate.50), channel_id=1, source_target_pairs={{0,16},{16,0},{1,17},{17,1},{2,18},{18,2},{3,19},{19,3},{4,20},{20... | collective-permute-start | bytes 55304 | tf_op jit(solution)/shard_map/ppermute | solution.py:342
  17.8 7.3 %collective-permute-start = (bf16[16,1024]{1,0:T(8,128)(2,1)S(1)}, bf16[16,1024]{1,0:T(8,128)(2,1)S(1)}, u32[]{:S(2)}, u32[]{:S(2)}) collective-permute-start(bf16[16,1024]{1,0:T(8,128)(2,1)S(1)} %slice_select_fusion), channel_id=1, source_target_pairs={{0,8},{1,9},{2,10},{3,11},{4,12},{5,13},{6,14},{7,15},{16,24},{17,... | collective-permute-start | bytes 98312 | tf_op jit(solution)/shard_map/ppermute | solution.py:337
  22.3 19.1 %collective-permute-start.5 = (bf16[784,512]{1,0:T(8,128)(2,1)S(1)}, bf16[784,512]{1,0:T(8,128)(2,1)S(1)}, u32[]{:S(2)}, u32[]{:S(2)}) collective-permute-start(bf16[784,512]{1,0:T(8,128)(2,1)S(1)} %concatenate.51), channel_id=1, source_target_pairs={{0,16},{16,0},{1,17},{17,1},{2,18},{18,2},{3,19},{19,3},{4,20},{20... | collective-permute-start | bytes 2408456 | tf_op jit(solution)/shard_map/ppermute | solution.py:342
  22.9 105.9 %reduce-scatter.2.cloned.1.call-start = ((), (), s32[]{:S(2)}) async-start(), calls=%async_computation.3 | async-start | bytes 2359296 | tf_op jit(solution)/shard_map/reduce_scatter | solution.py:652
  25.1 0.8 collective-permute-start.1
  26.0 0.8 collective-permute-start.2
  26.8 19.2 %collective-permute-start.3 = (bf16[16,1024]{1,0:T(8,128)(2,1)S(1)}, bf16[16,1024]{1,0:T(8,128)(2,1)S(1)}, u32[]{:S(2)}, u32[]{:S(2)}) collective-permute-start(bf16[16,1024]{1,0:T(8,128)(2,1)S(1)} %add.324), channel_id=1, source_target_pairs={{7,6},{5,4},{3,2},{1,0},{15,14},{13,12},{11,10},{9,8},{23,22},{21,... | collective-permute-start | bytes 98312 | tf_op jit(solution)/shard_map/ppermute | solution.py:359
  42.8 19.3 %collective-permute-start.7 = (bf16[256,1024]{1,0:T(8,128)(2,1)S(1)}, bf16[256,1024]{1,0:T(8,128)(2,1)}, u32[]{:S(2)}, u32[]{:S(2)}) collective-permute-start(bf16[256,1024]{1,0:T(8,128)(2,1)S(1)} %constant_dynamic-slice_fusion.10), channel_id=1, source_target_pairs={{0,16},{16,0},{1,17},{17,1},{2,18},{18,2},{3,19},{19,3},{4,20},{20... | collective-permute-start | bytes 1572872 | tf_op jit(solution)/shard_map/ppermute | solution.py:342
  60.6 8.5 %collective-permute-start.6 = (f32[128,256]{1,0:T(8,128)}, f32[128,256]{1,0:T(8,128)S(1)}, u32[]{:S(2)}, u32[]{:S(2)}) collective-permute-start(f32[128,256]{1,0:T(8,128)} %get-tuple-element.95), channel_id=1, source_target_pairs={{0,8},{1,9},{2,10},{3,11},{4,12},{5,13},{6,14},{7,15},{16,24},{17,... | collective-permute-start | bytes 393224 | tf_op jit(solution)/shard_map/ppermute | solution.py:337
  76.3 1.5 collective-permute-start.8
  78.5 3.9 %collective-permute-start.9 = (f32[8,1024]{1,0:T(8,128)S(1)}, f32[8,1024]{1,0:T(8,128)S(1)}, u32[]{:S(2)}, u32[]{:S(2)}) collective-permute-start(f32[8,1024]{1,0:T(8,128)S(1)} %add.331), channel_id=1, source_target_pairs={{0,2},{1,3},{2,0},{3,1},{4,6},{5,7},{6,4},{7,5},{8,10},{9,11},{10,... | collective-permute-start | bytes 98312 | tf_op jit(solution)/shard_map/ppermute | solution.py:404
  82.4 3.9 %collective-permute-start.10 = (f32[8,1024]{1,0:T(8,128)S(1)}, f32[8,1024]{1,0:T(8,128)S(1)}, u32[]{:S(2)}, u32[]{:S(2)}) collective-permute-start(f32[8,1024]{1,0:T(8,128)S(1)} %add.332), channel_id=1, source_target_pairs={{0,4},{1,5},{2,6},{3,7},{4,0},{5,1},{6,2},{7,3},{8,12},{9,13},{10,... | collective-permute-start | bytes 98312 | tf_op jit(solution)/shard_map/ppermute | solution.py:404
  87.0 145.3 %all-gather.13.cloned.1.call-start = ((), (), s32[]{:S(2)}) async-start(), calls=%async_computation.5 | async-start | bytes 4718592 | tf_op jit(solution)/shard_map/all_gather | solution.py:709
  96.4 16.3 %collective-permute-start.15 = (bf16[64,1024]{1,0:T(8,128)(2,1)S(1)}, bf16[64,1024]{1,0:T(8,128)(2,1)S(1)}, u32[]{:S(2)}, u32[]{:S(2)}) collective-permute-start(bf16[64,1024]{1,0:T(8,128)(2,1)S(1)} %get-tuple-element.171), channel_id=1, source_target_pairs={{0,0},{1,2},{2,4},{3,6},{4,16},{5,18},{6,20},{7,22},{8,8},{9,10},{... | collective-permute-start | bytes 393224 | tf_op jit(solution)/shard_map/ppermute | solution.py:650
  97.1 17.0 %collective-permute-start.18 = (bf16[64,1024]{1,0:T(8,128)(2,1)S(1)}, bf16[64,1024]{1,0:T(8,128)(2,1)S(1)}, u32[]{:S(2)}, u32[]{:S(2)}) collective-permute-start(bf16[64,1024]{1,0:T(8,128)(2,1)S(1)} %get-tuple-element.172), channel_id=1, source_target_pairs={{0,9},{1,11},{2,13},{3,15},{4,25},{5,27},{6,29},{7,31},{8,0},{9,2}... | collective-permute-start | bytes 393224 | tf_op jit(solution)/shard_map/ppermute | solution.py:650
  99.6 14.5 %collective-permute-start.17 = (bf16[64,1024]{1,0:T(8,128)(2,1)S(1)}, bf16[64,1024]{1,0:T(8,128)(2,1)S(1)}, u32[]{:S(2)}, u32[]{:S(2)}) collective-permute-start(bf16[64,1024]{1,0:T(8,128)(2,1)S(1)} %get-tuple-element.173), channel_id=1, source_target_pairs={{0,1},{1,3},{2,5},{3,7},{4,17},{5,19},{6,21},{7,23},{8,9},{9,11},{... | collective-permute-start | bytes 393224 | tf_op jit(solution)/shard_map/ppermute | solution.py:650
  101.2 14.3 %collective-permute-start.16 = (bf16[64,1024]{1,0:T(8,128)(2,1)S(1)}, bf16[64,1024]{1,0:T(8,128)(2,1)S(1)}, u32[]{:S(2)}, u32[]{:S(2)}) collective-permute-start(bf16[64,1024]{1,0:T(8,128)(2,1)S(1)} %get-tuple-element.174), channel_id=1, source_target_pairs={{0,8},{1,10},{2,12},{3,14},{4,24},{5,26},{6,28},{7,30},{8,1},{9,3}... | collective-permute-start | bytes 393224 | tf_op jit(solution)/shard_map/ppermute | solution.py:650
  104.8 13.0 %collective-permute-start.11 = (bf16[256,512]{1,0:T(8,128)(2,1)S(1)}, bf16[256,512]{1,0:T(8,128)(2,1)S(1)}, u32[]{:S(2)}, u32[]{:S(2)}) collective-permute-start(bf16[256,512]{1,0:T(8,128)(2,1)S(1)} %constant_dynamic-slice_fusion.9), channel_id=1, source_target_pairs={{0,16},{16,0},{1,17},{17,1},{2,18},{18,2},{3,19},{19,3},{4,20},{20... | collective-permute-start | bytes 786440 | tf_op jit(solution)/shard_map/ppermute | solution.py:373
  112.8 16.0 %collective-permute-start.12 = (f32[128,256]{1,0:T(8,128)S(1)}, f32[128,256]{1,0:T(8,128)S(1)}, u32[]{:S(2)}, u32[]{:S(2)}) collective-permute-start(f32[128,256]{1,0:T(8,128)S(1)} %copy-done.19), channel_id=1, source_target_pairs={{8,0},{9,1},{10,2},{11,3},{12,4},{13,5},{14,6},{15,7},{24,16},{25,... | collective-permute-start | bytes 393224 | tf_op jit(solution)/shard_map/ppermute | solution.py:337
  115.6 36.9 %collective-permute-start.19 = (bf16[64,1024]{1,0:T(8,128)(2,1)S(1)}, bf16[64,1024]{1,0:T(8,128)(2,1)S(1)}, u32[]{:S(2)}, u32[]{:S(2)}) collective-permute-start(bf16[64,1024]{1,0:T(8,128)(2,1)S(1)} %add_convert_fusion.2), channel_id=1, source_target_pairs={{0,8},{8,0},{1,9},{9,1},{2,10},{10,2},{3,11},{11,3},{4,12},{12,4},... | collective-permute-start | bytes 393224 | tf_op jit(solution)/shard_map/ppermute | solution.py:383
  139.0 13.5 %collective-permute-start.13 = (bf16[16,512]{1,0:T(8,128)(2,1)S(1)}, bf16[16,512]{1,0:T(8,128)(2,1)S(1)}, u32[]{:S(2)}, u32[]{:S(2)}) collective-permute-start(bf16[16,512]{1,0:T(8,128)(2,1)S(1)} %convert.18), channel_id=1, source_target_pairs={{8,0},{9,1},{10,2},{11,3},{12,4},{13,5},{14,6},{15,7},{24,16},{25,... | collective-permute-start | bytes 49160 | tf_op jit(solution)/shard_map/ppermute | solution.py:337
  140.6 12.0 %collective-permute-start.14 = (bf16[256,512]{1,0:T(8,128)(2,1)S(1)}, bf16[256,512]{1,0:T(8,128)(2,1)S(1)}, u32[]{:S(2)}, u32[]{:S(2)}) collective-permute-start(bf16[256,512]{1,0:T(8,128)(2,1)S(1)} %fusion.32), channel_id=1, source_target_pairs={{0,8},{8,0},{1,9},{9,1},{2,10},{10,2},{3,11},{11,3},{4,12},{12,4},... | collective-permute-start | bytes 786440 | tf_op jit(solution)/shard_map/ppermute | solution.py:383
  153.6 88.9 %all-gather.11.cloned.1.call-start = ((), (), s32[]{:S(2)}) async-start(), calls=%async_computation.4 | async-start | bytes 2506752 | tf_op jit(solution)/shard_map/all_gather | solution.py:745
  157.7 9.5 %collective-permute-start.21 = (bf16[4,128,1024]{2,1,0:T(8,128)(2,1)S(1)}, bf16[4,128,1024]{2,1,0:T(8,128)(2,1)S(1)}, u32[]{:S(2)}, u32[]{:S(2)}) collective-permute-start(bf16[4,128,1024]{2,1,0:T(8,128)(2,1)S(1)} %dynamic-slice_bitcast_fusion), channel_id=1, source_target_pairs={{0,1},{1,0},{2,3},{3,2},{4,5},{5,4},{6,7},{7,6},{8,9},{9,8},{10,11... | collective-permute-start | bytes 3145736 | tf_op jit(solution)/shard_map/ppermute | solution.py:404
  165.0 2.1 collective-permute-start.22
  165.6 8.7 %collective-permute-start.20 = (bf16[272,512]{1,0:T(8,128)(2,1)S(1)}, bf16[272,512]{1,0:T(8,128)(2,1)S(1)}, u32[]{:S(2)}, u32[]{:S(2)}) collective-permute-start(bf16[272,512]{1,0:T(8,128)(2,1)S(1)} %fusion.18), channel_id=1, source_target_pairs={{0,16},{16,0},{1,17},{17,1},{2,18},{18,2},{3,19},{19,3},{4,20},{20... | collective-permute-start | bytes 835592 | tf_op jit(solution)/shard_map/ppermute | solution.py:373
  175.7 6.2 %collective-permute-start.27 = (f32[8,2304]{1,0:T(8,128)S(1)}, f32[8,2304]{1,0:T(8,128)S(1)}, u32[]{:S(2)}, u32[]{:S(2)}) collective-permute-start(f32[8,2304]{1,0:T(8,128)S(1)} %select_maximum_fusion), channel_id=1, source_target_pairs={{0,1},{1,0},{2,3},{3,2},{4,5},{5,4},{6,7},{7,6},{8,9},{9,8},{10,11... | collective-permute-start | bytes 221192 | tf_op jit(solution)/shard_map/ppermute | solution.py:404
  175.8 7.7 %collective-permute-start.26 = (bf16[32,1024]{1,0:T(8,128)(2,1)S(1)}, bf16[32,1024]{1,0:T(8,128)(2,1)S(1)}, u32[]{:S(2)}, u32[]{:S(2)}) collective-permute-start(bf16[32,1024]{1,0:T(8,128)(2,1)S(1)} %get-tuple-element.179), channel_id=1, source_target_pairs={{0,6},{1,7},{2,4},{3,5},{4,2},{5,3},{6,0},{7,1},{8,14},{9,15},{10,... | collective-permute-start | bytes 196616 | tf_op jit(solution)/shard_map/ppermute | solution.py:404
  176.2 16.3 %collective-permute-start.25 = (bf16[32,1024]{1,0:T(8,128)(2,1)S(1)}, bf16[32,1024]{1,0:T(8,128)(2,1)S(1)}, u32[]{:S(2)}, u32[]{:S(2)}) collective-permute-start(bf16[32,1024]{1,0:T(8,128)(2,1)S(1)} %get-tuple-element.180), channel_id=1, source_target_pairs={{0,4},{1,5},{2,6},{3,7},{4,0},{5,1},{6,2},{7,3},{8,12},{9,13},{10,... | collective-permute-start | bytes 196616 | tf_op jit(solution)/shard_map/ppermute | solution.py:404
  179.4 13.1 %collective-permute-start.24 = (bf16[32,1024]{1,0:T(8,128)(2,1)S(1)}, bf16[32,1024]{1,0:T(8,128)(2,1)S(1)}, u32[]{:S(2)}, u32[]{:S(2)}) collective-permute-start(bf16[32,1024]{1,0:T(8,128)(2,1)S(1)} %get-tuple-element.181), channel_id=1, source_target_pairs={{0,2},{1,3},{2,0},{3,1},{4,6},{5,7},{6,4},{7,5},{8,10},{9,11},{10,... | collective-permute-start | bytes 196616 | tf_op jit(solution)/shard_map/ppermute | solution.py:404
  179.5 26.5 %collective-permute-start.23 = (bf16[272,512]{1,0:T(8,128)(2,1)S(1)}, bf16[272,512]{1,0:T(8,128)(2,1)S(1)}, u32[]{:S(2)}, u32[]{:S(2)}) collective-permute-start(bf16[272,512]{1,0:T(8,128)(2,1)S(1)} %fusion.55), channel_id=1, source_target_pairs={{0,8},{8,0},{1,9},{9,1},{2,10},{10,2},{3,11},{11,3},{4,12},{12,4},... | collective-permute-start | bytes 835592 | tf_op jit(solution)/shard_map/ppermute | solution.py:383
  181.9 24.1 %collective-permute-start.32 = (bf16[128,1024]{1,0:T(8,128)(2,1)S(1)}, bf16[128,1024]{1,0:T(8,128)(2,1)S(1)}, u32[]{:S(2)}, u32[]{:S(2)}) collective-permute-start(bf16[128,1024]{1,0:T(8,128)(2,1)S(1)} %get-tuple-element.166), channel_id=1, source_target_pairs={{0,6},{1,7},{2,4},{3,5},{4,2},{5,3},{6,0},{7,1},{8,14},{9,15},{10,... | collective-permute-start | bytes 786440 | tf_op jit(solution)/shard_map/ppermute | solution.py:404
  183.5 22.6 %collective-permute-start.31 = (bf16[128,1024]{1,0:T(8,128)(2,1)S(1)}, bf16[128,1024]{1,0:T(8,128)(2,1)S(1)}, u32[]{:S(2)}, u32[]{:S(2)}) collective-permute-start(bf16[128,1024]{1,0:T(8,128)(2,1)S(1)} %get-tuple-element.167), channel_id=1, source_target_pairs={{0,4},{1,5},{2,6},{3,7},{4,0},{5,1},{6,2},{7,3},{8,12},{9,13},{10,... | collective-permute-start | bytes 786440 | tf_op jit(solution)/shard_map/ppermute | solution.py:404
  192.5 13.5 %collective-permute-start.30 = (bf16[128,1024]{1,0:T(8,128)(2,1)S(1)}, bf16[128,1024]{1,0:T(8,128)(2,1)S(1)}, u32[]{:S(2)}, u32[]{:S(2)}) collective-permute-start(bf16[128,1024]{1,0:T(8,128)(2,1)S(1)} %get-tuple-element.168), channel_id=1, source_target_pairs={{0,2},{1,3},{2,0},{3,1},{4,6},{5,7},{6,4},{7,5},{8,10},{9,11},{10,... | collective-permute-start | bytes 786440 | tf_op jit(solution)/shard_map/ppermute | solution.py:404
  192.6 4.0 %collective-permute-start.28 = (bf16[32,512]{1,0:T(8,128)(2,1)S(1)}, bf16[32,512]{1,0:T(8,128)(2,1)S(1)}, u32[]{:S(2)}, u32[]{:S(2)}) collective-permute-start(bf16[32,512]{1,0:T(8,128)(2,1)S(1)} %dynamic-slice_convert_fusion.1), channel_id=1, source_target_pairs={{0,16},{16,0},{1,17},{17,1},{2,18},{18,2},{3,19},{19,3},{4,20},{20... | collective-permute-start | bytes 98312 | tf_op jit(solution)/shard_map/ppermute | solution.py:373
  196.6 9.4 %collective-permute-start.29 = (f32[8,2304]{1,0:T(8,128)S(1)}, f32[8,2304]{1,0:T(8,128)S(1)}, u32[]{:S(2)}, u32[]{:S(2)}) collective-permute-start(f32[8,2304]{1,0:T(8,128)S(1)} %fusion.59), channel_id=1, source_target_pairs={{0,2},{1,3},{2,0},{3,1},{4,6},{5,7},{6,4},{7,5},{8,10},{9,11},{10,... | collective-permute-start | bytes 221192 | tf_op jit(solution)/shard_map/ppermute | solution.py:404
  206.0 17.6 %copy-start.9 = (bf16[128,1024]{1,0:T(8,128)(2,1)S(1)}, bf16[128,1024]{1,0:T(8,128)(2,1)}, u32[]{:S(2)}) copy-start(bf16[128,1024]{1,0:T(8,128)(2,1)} %param.21) | copy-start | bytes 786436
  206.0 17.6 %copy-start.12 = (bf16[128,1024]{1,0:T(8,128)(2,1)S(1)}, bf16[128,1024]{1,0:T(8,128)(2,1)}, u32[]{:S(2)}) copy-start(bf16[128,1024]{1,0:T(8,128)(2,1)} %reduce-scatter.2.cloned.1.call-done) | copy-start | bytes 786436
  207.9 5.2 %collective-permute-start.33 = (bf16[32,512]{1,0:T(8,128)(2,1)S(1)}, bf16[32,512]{1,0:T(8,128)(2,1)S(1)}, u32[]{:S(2)}, u32[]{:S(2)}) collective-permute-start(bf16[32,512]{1,0:T(8,128)(2,1)S(1)} %convert_element_type.215), channel_id=1, source_target_pairs={{0,8},{8,0},{1,9},{9,1},{2,10},{10,2},{3,11},{11,3},{4,12},{12,4},... | collective-permute-start | bytes 98312 | tf_op jit(solution)/shard_map/ppermute | solution.py:404
  210.5 4.4 %collective-permute-start.34 = (f32[8,2304]{1,0:T(8,128)S(1)}, f32[8,2304]{1,0:T(8,128)S(1)}, u32[]{:S(2)}, u32[]{:S(2)}) collective-permute-start(f32[8,2304]{1,0:T(8,128)S(1)} %add.375), channel_id=1, source_target_pairs={{0,4},{1,5},{2,6},{3,7},{4,0},{5,1},{6,2},{7,3},{8,12},{9,13},{10,... | collective-permute-start | bytes 221192 | tf_op jit(solution)/shard_map/ppermute | solution.py:404
  214.8 5.2 %collective-permute-start.37 = (bf16[32,512]{1,0:T(8,128)(2,1)S(1)}, bf16[32,512]{1,0:T(8,128)(2,1)S(1)}, u32[]{:S(2)}, u32[]{:S(2)}) collective-permute-start(bf16[32,512]{1,0:T(8,128)(2,1)S(1)} %convert_add_fusion.5), channel_id=1, source_target_pairs={{0,6},{1,7},{2,4},{3,5},{4,2},{5,3},{6,0},{7,1},{8,14},{9,15},{10,... | collective-permute-start | bytes 98312 | tf_op jit(solution)/shard_map/ppermute | solution.py:404
  216.5 5.3 %collective-permute-start.36 = (bf16[32,512]{1,0:T(8,128)(2,1)S(1)}, bf16[32,512]{1,0:T(8,128)(2,1)S(1)}, u32[]{:S(2)}, u32[]{:S(2)}) collective-permute-start(bf16[32,512]{1,0:T(8,128)(2,1)S(1)} %convert_add_fusion.5), channel_id=1, source_target_pairs={{0,4},{1,5},{2,6},{3,7},{4,0},{5,1},{6,2},{7,3},{8,12},{9,13},{10,... | collective-permute-start | bytes 98312 | tf_op jit(solution)/shard_map/ppermute | solution.py:404
  218.2 4.0 %collective-permute-start.35 = (bf16[32,512]{1,0:T(8,128)(2,1)S(1)}, bf16[32,512]{1,0:T(8,128)(2,1)S(1)}, u32[]{:S(2)}, u32[]{:S(2)}) collective-permute-start(bf16[32,512]{1,0:T(8,128)(2,1)S(1)} %convert_add_fusion.5), channel_id=1, source_target_pairs={{0,2},{1,3},{2,0},{3,1},{4,6},{5,7},{6,4},{7,5},{8,10},{9,11},{10,... | collective-permute-start | bytes 98312 | tf_op jit(solution)/shard_map/ppermute | solution.py:404
  218.4 4.4 %collective-permute-start.38 = (f32[8,2304]{1,0:T(8,128)S(1)}, f32[8,2304]{1,0:T(8,128)S(1)}, u32[]{:S(2)}, u32[]{:S(2)}) collective-permute-start(f32[8,2304]{1,0:T(8,128)S(1)} %add.385), channel_id=1, source_target_pairs={{0,16},{16,0},{1,17},{17,1},{2,18},{18,2},{3,19},{19,3},{4,20},{20... | collective-permute-start | bytes 221192 | tf_op jit(solution)/shard_map/ppermute | solution.py:404
  222.7 5.6 %collective-permute-start.39 = (f32[8,2304]{1,0:T(8,128)S(1)}, f32[8,2304]{1,0:T(8,128)S(1)}, u32[]{:S(2)}, u32[]{:S(2)}) collective-permute-start(f32[8,2304]{1,0:T(8,128)S(1)} %add.386), channel_id=1, source_target_pairs={{0,8},{8,0},{1,9},{9,1},{2,10},{10,2},{3,11},{11,3},{4,12},{12,4},... | collective-permute-start | bytes 221192 | tf_op jit(solution)/shard_map/ppermute | solution.py:404
  224.8 6.8 %collective-permute-start.40 = (bf16[128,512]{1,0:T(8,128)(2,1)S(1)}, bf16[128,512]{1,0:T(8,128)(2,1)S(1)}, u32[]{:S(2)}, u32[]{:S(2)}) collective-permute-start(bf16[128,512]{1,0:T(8,128)(2,1)S(1)} %pad_maximum_fusion.4), channel_id=1, source_target_pairs={{0,1},{1,0},{2,3},{3,2},{4,5},{5,4},{6,7},{7,6},{8,9},{9,8},{10,11... | collective-permute-start | bytes 393224 | tf_op jit(solution)/shard_map/ppermute | solution.py:404
  (18 other events, 96.8 us)
Sparse Core Ops, SparseCore 0:
  9.6 25.0 all-gather.6
  36.3 21.4 all-gather.8
  87.1 41.6 reduce-scatter.1
  153.7 45.5 all-gather.12
  207.0 24.1 all-gather.10

commit v4 on v3

--- a/solution.py
+++ b/solution.py
@@ -473,7 +473,7 @@
 def carry_over(state, decay, axis, size, way):
     total = None
     for j in range(size - 1, 0, -1):
-        part = shifted(state, axis, size, way * j)
+        part = shifted(state.astype(BF16), axis, size, way * j).astype(F32)
         if total is None:
             total = part
         else:
@@ -533,8 +533,7 @@
     x_all = lax.all_gather(layer_input, "tp", axis=0, tiled=True)
     halo = broadcast_last(shifted(tail_rows, "cp", cp, 1), "tp", tp)
     c_all = lax.all_gather(cotangent, "tp", axis=0, tiled=True)
-    ow = gather_dp(cut(out_weight, (k_id % share) * ch, ch, 0), dp, d_id)
-    ow = lax.dynamic_index_in_dim(ow, k_id // share, 0, keepdims=False)
+    ow = cut(out_weight, (k_id % share) * ch, ch, 0)
 
     def row_of(index, size, at=0):
         return small[:, index, at : at + size].reshape(-1)
@@ -588,6 +587,8 @@
     )(x_all, halo, gain_row, w, cw, cb, sb, rate)
 
     s0 = carry_over(fin, dtot, "cp", cp, 1)
+    cums, ow = lax.optimization_barrier((cums, ow))
+    ow = lax.dynamic_index_in_dim(gather_dp(ow, dp, d_id), k_id // share, 0, keepdims=False)
 
     inside = pl.pallas_call(
         lambda *refs: intra_kernel(hdim, lh, *refs),
@@ -637,17 +638,6 @@
     quarter = ch // grp
     c_id = lax.axis_index("cp")
     src = d_id * cp + c_id
-    og_parts = []
-    for j in range(grp):
-        pairs = []
-        for d in range(dp):
-            for p in range(cp):
-                for k in range(tp):
-                    piece = (d * cp + p + j) % grp
-                    slot = (k % share) * grp + piece
-                    pairs.append(((d * cp + p) * tp + k, (k // share) * cp * tp + (slot % cp) * tp + slot // cp))
-        send = cut(og, ((src + j) % grp) * quarter, quarter, 0)
-        og_parts.append(lax.ppermute(send, ("dp", "cp", "tp"), pairs))
     gz_own, gz_parts = parts_dp(gz, dp, d_id, 1)
     y_sum = lax.psum_scatter(y, "tp", scatter_dimension=0, tiled=True)
 
@@ -661,10 +651,9 @@
         name="back_intra", cost_estimate=cost(7),
     )(kq, xs, cums, do)
 
-    dxs, gz_parts, y_sum = lax.optimization_barrier((dxs, gz_parts, y_sum))
+    dxs, gz_parts = lax.optimization_barrier((dxs, gz_parts))
     gz_own = gz_own.astype(F32) + sum(part.astype(F32) for part in gz_parts)
     gz_others = others_over(gz_own, "cp", cp)
-
     dxbc, ddt, dhalo, cg, hg = pl.pallas_call(
         lambda *refs: back_kernel(hdim, *refs),
         grid=(nb,),
@@ -692,27 +681,35 @@
         return jnp.pad(values, ((0, 0), (0, conv_all - values.shape[1])))
 
     back_halo = shifted(dhalo, "cp", cp, -1)
+    dxbc, y_sum = lax.optimization_barrier((dxbc, y_sum))
     rest = jnp.concatenate([dxbc, ddt], axis=1)
     grad_main = mm(rest, normed, 0, 0)
-    og_own = sum(part.astype(F32) for part in og_parts).astype(BF16)
-    og_others = [shifted_ring(og_own, "cp", cp, j) for j in range(1, cp)]
-    dn_main = mm(jnp.concatenate([dz, rest], axis=1), w).astype(BF16)
-    back_halo, dn_main, grad_main, gz_others, og_others = lax.optimization_barrier(
-        (back_halo, dn_main, grad_main, gz_others, og_others)
-    )
-    half = width // dp
-    og_own = in_order([og_own] + og_others, c_id, cp)
-    og_rows = og_own.shape[0]
-    zg = jnp.concatenate(
-        [add_up(gz_own, gz_others).astype(BF16)] + [og_own[:, j * half : (j + 1) * half] for j in range(dp)], axis=0
-    )
-    zg = lax.all_gather(zg, "tp", axis=0, tiled=False)
+    back_halo, grad_main, gz_others = lax.optimization_barrier((back_halo, grad_main, gz_others))
+    zg = lax.all_gather(add_up(gz_own, gz_others).astype(BF16), "tp", axis=0, tiled=False)
 
     halo_low = jnp.pad(back_halo.astype(BF16), ((0, 0), (0, LANES)))
     grad_rest = grad_main + mm(halo_low, normed[-PRE:], 0, 0)
+    x_dt = jnp.concatenate([grad_rest[:ch], grad_rest[conv_ch : conv_ch + thin]], axis=0)
+    x_own, x_parts = parts_dp(x_dt, dp, d_id, 1)
+    grad_rest, rest, x_own = lax.optimization_barrier((grad_rest, rest, x_own))
+    dn_main = mm(jnp.concatenate([dz, rest], axis=1), w).astype(BF16)
     dn_fix = (dn_main[-PRE:].astype(F32) + mm(halo_low, w[ch:])).astype(BF16)
     dn_part = lax.dynamic_update_slice_in_dim(dn_main, dn_fix, tokens - PRE, 0)
-
+    dn_part, x_parts = lax.optimization_barrier((dn_part, x_parts))
+    x_own = add_up(x_own, x_parts)
+    x_own, dn_part, grad_rest, og = lax.optimization_barrier((x_own, dn_part, grad_rest, og))
+    x_others = others_over(x_own, "cp", cp)
+    og_parts = []
+    for j in range(grp):
+        pairs = []
+        for d in range(dp):
+            for p in range(cp):
+                for k in range(tp):
+                    piece = (d * cp + p + j) % grp
+                    slot = (k % share) * grp + piece
+                    pairs.append(((d * cp + p) * tp + k, (k // share) * cp * tp + (slot % cp) * tp + slot // cp))
+        send = cut(og, ((src + j) % grp) * quarter, quarter, 0)
+        og_parts.append(lax.ppermute(send, ("dp", "cp", "tp"), pairs))
     steps = [("tp", tp), ("dp", dp), ("cp", cp)]
     steps = [(axis, size, 1 << i) for axis, size in steps for i in range(size.bit_length() - 1)]
 
@@ -722,13 +719,14 @@
             values = values + swap(values, axis, size, bit)
         return values
 
-    x_dt = jnp.concatenate([grad_rest[:ch], grad_rest[conv_ch : conv_ch + thin]], axis=0)
-    x_own, x_parts = parts_dp(x_dt, dp, d_id, 1)
     dn_cores = scatter_cores(dn_part, tp, k_id)
     kq_cores = scatter_cores(grad_rest[ch:conv_ch], tp, k_id)
-    x_parts, dn_cores, kq_cores, grad_rest = lax.optimization_barrier((x_parts, dn_cores, kq_cores, grad_rest))
-    x_own = add_up(x_own, x_parts)
-    x_others = others_over(x_own, "cp", cp)
+    dn_cores, kq_cores, grad_rest, zg, og_parts = lax.optimization_barrier(
+        (dn_cores, kq_cores, grad_rest, zg, og_parts)
+    )
+    half = width // dp
+    og_own = sum(part.astype(F32) for part in og_parts).astype(BF16)
+    og_others = [shifted_ring(og_own, "cp", cp, j) for j in range(1, cp)]
     dn_own, dn_parts = scatter_chips(dn_cores, tp, k_id)
     kq_own, kq_parts = scatter_chips(kq_cores, tp, k_id)
 
@@ -741,12 +739,36 @@
     kq_parts, pack = lax.optimization_barrier((kq_parts, pack))
     kq_sum = scatter_dp(add_up(kq_own, kq_parts), dp, d_id, 1)
     pack = pack_next(pack)
-    x_others, kq_sum, pack, dn_parts = lax.optimization_barrier((x_others, kq_sum, pack, dn_parts))
-    xg = lax.all_gather(add_up(x_own, x_others).astype(BF16), "tp", axis=0, tiled=False)
+    x_others, kq_sum, pack, og_others = lax.optimization_barrier((x_others, kq_sum, pack, og_others))
+    og_own = in_order([og_own] + og_others, c_id, cp)
+    og_rows = og_own.shape[0]
+    x_own = add_up(x_own, x_others).astype(BF16)
+    xg = jnp.concatenate(
+        [x_own[:ch]] + [og_own[:, j * half : (j + 1) * half] for j in range(dp)] + [x_own[ch:]], axis=0
+    )
+    xg = lax.all_gather(xg, "tp", axis=0, tiled=False)
+    dn_parts, kq_sum = lax.optimization_barrier((dn_parts, kq_sum))
     dn_sum = add_up(dn_own, dn_parts)
     kq_sum = sum_over(kq_sum, "cp", cp, BF16)
     pack = pack_next(pack)
-    kq_sum, pack = lax.optimization_barrier((kq_sum, pack))
+    proj_all = in_weight.shape[1]
+    grid_shape = sds((proj_all, half))
+
+    def widen_out_kernel(src_ref, out_ref):
+        for j in range(dp):
+            out_ref[:, j * half : (j + 1) * half] = src_ref[0, j * og_rows : (j + 1) * og_rows, :].astype(F32)
+
+    def widen_pair_kernel(src_ref, *refs):
+        out_ref = refs[-1]
+        out_ref[:ch, :] = src_ref[0, :ch, :].astype(F32)
+        out_ref[ch:, :] = src_ref[1, :ch, :].astype(F32)
+
+    in_grad = pl.pallas_call(
+        widen_pair_kernel, grid=(tp // 2,),
+        in_specs=[pl.BlockSpec((2, ch, half), lambda i: (i, 0, 0))], out_specs=rows_of(half, 2 * ch),
+        out_shape=grid_shape, compiler_params=params(), name="widen_z", cost_estimate=cost(5),
+    )(zg)
+    kq_sum, pack, in_grad = lax.optimization_barrier((kq_sum, pack, in_grad))
     kqg = gather_chips(kq_sum.astype(BF16), tp)
     pack = pack_next(pack)
     kqg, pack = lax.optimization_barrier((kqg, pack))
@@ -766,37 +788,13 @@
     dg = dn * gain_row
     input_grad = cotangent.astype(F32) + q * (dg - m * jnp.mean(dg * m, axis=-1, keepdims=True))
 
-    proj_all = in_weight.shape[1]
-    grid_shape = sds((proj_all, half))
-
-    def widen_out_kernel(src_ref, out_ref):
-        for j in range(dp):
-            out_ref[:, j * half : (j + 1) * half] = src_ref[0, j * og_rows : (j + 1) * og_rows, :].astype(F32)
-
-    def widen_pair_kernel(src_ref, *refs):
-        out_ref = refs[-1]
-        out_ref[:ch, :] = src_ref[0, :ch, :].astype(F32)
-        out_ref[ch:, :] = src_ref[1, :ch, :].astype(F32)
-
-    out_grad = pl.pallas_call(
-        widen_out_kernel, grid=(tp,),
-        in_specs=[pl.BlockSpec((1, ch, half), lambda i: (i, 1, 0))], out_specs=rows_of(width, og_rows),
-        out_shape=sds((tp * og_rows, width)), compiler_params=params(), name="widen_out", cost_estimate=cost(6),
-    )(zg)
     in_grad = pl.pallas_call(
         widen_pair_kernel, grid=(tp // 2,),
-        in_specs=[pl.BlockSpec((2, ch, half), lambda i: (i, 0, 0))], out_specs=rows_of(half, 2 * ch),
-        out_shape=grid_shape, compiler_params=params(), name="widen_z", cost_estimate=cost(5),
-    )(zg)
-    xg, in_grad, out_grad, input_grad = lax.optimization_barrier((xg, in_grad, out_grad, input_grad))
-
-    in_grad = pl.pallas_call(
-        widen_pair_kernel, grid=(tp // 2,),
-        in_specs=[pl.BlockSpec((2, ch + thin, half), lambda i: (i, 0, 0)), pl.BlockSpec(memory_space=pl.ANY)],
+        in_specs=[pl.BlockSpec((2, ch, half), lambda i: (i, 0, 0)), pl.BlockSpec(memory_space=pl.ANY)],
         out_specs=pl.BlockSpec((2 * ch, half), lambda i: (i + tp // 2, 0)),
         out_shape=grid_shape, input_output_aliases={1: 0}, compiler_params=params(), name="widen_x", cost_estimate=cost(5),
     )(xg, in_grad)
-    last = jnp.concatenate([kqg, xg[:, ch : ch + lh].reshape(heads, half)], axis=0)
+    last = jnp.concatenate([kqg, xg[:, 2 * ch : 2 * ch + lh].reshape(heads, half)], axis=0)
     strip = last.shape[0]
 
     def last_kernel(src_ref, old_ref, out_ref, wide_ref, sem):
@@ -812,6 +810,12 @@
         out_shape=grid_shape, input_output_aliases={1: 0},
         scratch_shapes=[pltpu.VMEM((strip, half), F32), pltpu.SemaphoreType.DMA], name="widen_kq",
     )(last, in_grad).T
+    out_grad = pl.pallas_call(
+        widen_out_kernel, grid=(tp,),
+        in_specs=[pl.BlockSpec((1, ch, half), lambda i: (i, 1, 0))], out_specs=rows_of(width, og_rows),
+        out_shape=sds((tp * og_rows, width)), compiler_params=params(), name="widen_out", cost_estimate=cost(6),
+    )(xg)
+
 
     def own(values):
         size = values.shape[-1] // dp

time: 259 us -> 276 us (1.066)
  other arithmetic: 17.8 us -> 29.1 us
  local copies, waits for them, and re-layouts: 22.5 us -> 30.2 us
  matrix products: 11.2 us -> 6.2 us
  waiting for transfers between devices: 64.5 us -> 68.6 us
    ppermute x21, waiting for transfers between devices: 29 us -> 40.9 us  [swap(): return lax.ppermute(values, axis, [(i, i ^ bit) for i in range(size)])]
    reduce_scatter x1, waiting for transfers between devices: 11 us -> 0.01 us  [local(): y_sum = lax.psum_scatter(y, 'tp', scatter_dimension=0, tiled=True)]
    ppermute x3, waiting for transfers between devices: 8.96 us -> 3.17 us  [parts_dp(): lax.ppermute(sent, 'dp', [(i, (i + j) % dp) for i in range(dp)])]
    ppermute x3, waiting for transfers between devices: 0.01 us -> 5.7 us  [broadcast_last(): values = values + lax.ppermute(values, axis, pairs)]
    ppermute x3, waiting for transfers between devices: 0.01 us -> 5.27 us  [shifted_ring(): lax.ppermute(values, axis, [(i, (i + by) % size) for i in range(size)])]
    dot_general x4, matrix products: 11.2 us -> 6.2 us  [mm(): lax.dot_general(a, b, (((da,), (db,)), ((), ())), preferred_element_type=...]
    ppermute x3, waiting for transfers between devices: 13.3 us -> 8.61 us  [gather_dp(): lax.ppermute(values, 'dp', [(i, (i - j) % dp) for i in range(dp)])]
    convert_element_type x1 -> x5, other arithmetic: 0.82 us -> 4.19 us  [the longest x4 3.15 us: carry_over(): part = shifted(state.astype(BF16), axis, size, way * j).astype(F32)]
  transfers between devices with their start and end apart: 46 -> 46, of which waited for: 17 -> 21; matrix products, arithmetic and copies ran while one was open for 17% -> 20% of each run, Pallas kernels for 19% -> 16%
where the time goes in v4:
time: 276 us; the launch traced here: 274 us
  waiting for transfers between devices  68.6 us (25%)
  starting transfers between devices  63.3 us (23%)
  Pallas kernels  62.3 us (23%)
  local copies, waits for them, and re-layouts  30.2 us (11%)
  other arithmetic  29.1 us (11%)
  between operations  14.7 us (5%)
  matrix products  6.2 us (2%)
    ppermute x21, waiting for transfers between devices, swap(): return lax.ppermute(values, axis, [(i, i ^ bit) for i in range(size)])  40.9 us
    ppermute x21, starting transfers between devices, swap(): return lax.ppermute(values, axis, [(i, i ^ bit) for i in range(size)])  28.2 us
    pallas_call x1, Pallas kernels, local(): pl.pallas_call(lambda *refs: front_kernel(hdim, *refs), grid=(nb,), in_sp...  11.4 us
    ppermute x3, starting transfers between devices, shifted_ring(): lax.ppermute(values, axis, [(i, (i + by) % size) for i in range(size)])  10.2 us
    pallas_call x1, Pallas kernels, local(): pl.pallas_call(lambda *refs: back_kernel(hdim, *refs), grid=(nb,), in_spe...  8.77 us
    ppermute x4, starting transfers between devices, shifted(): return lax.ppermute(values, axis, pairs)  8.77 us
    ppermute x3, waiting for transfers between devices, gather_dp(): lax.ppermute(values, 'dp', [(i, (i - j) % dp) for i in range(dp)])  8.61 us
    pallas_call x2, Pallas kernels, local(): pl.pallas_call(widen_pair_kernel, grid=(tp // 2,), in_specs=[pl.BlockSpec...  8.58 us
  transfers between devices with their start and end apart: 46, of which 21 were waited for; matrix products, arithmetic and copies ran while one was open for 20% of the time, Pallas kernels for 16%

profile of v4, /device:TPU:0, one launch (start us, length us, event | category | flops | bytes accessed | tf_op | source)
XLA Modules:
  0.0 274.4 jit_solution(11717937802986242724)
XLA Ops:
  10.9 1.7 slice.160
  14.0 1.9 dynamic-slice_bitcast_fusion.4
  15.8 3.1 %concatenate.50 = bf16[784,512]{1,0:T(8,128)(2,1)S(1)} concatenate(bf16[256,512]{1,0:T(8,128)(2,1)} %get-tuple-element.185, bf16[256,512]{1,0:T(8,128)(2,1)} %get-tuple-element.184, bf16[256,512]{1,0:T(8,128)(2,1)} %slice.160, bf16[4,512]{1,0:T(4,128)(2,1)S(1)} %fusion.44, bf16[12,512]{1,0:T(8,128)(2,1)S(1)} %broadcast_in_dim.57), dimensions={0} | concatenate | bytes 1605632 | tf_op jit(solution)/shard_map/concatenate | solution.py:508
  19.0 3.0 %collective-permute-start.4 = (bf16[8,1152]{1,0:T(8,128)(2,1)S(1)}, bf16[8,1152]{1,0:T(8,128)(2,1)S(1)}, u32[]{:S(2)}, u32[]{:S(2)}) collective-permute-start(bf16[8,1152]{1,0:T(8,128)(2,1)S(1)} %concatenate.49), channel_id=1, source_target_pairs={{0,16},{16,0},{1,17},{17,1},{2,18},{18,2},{3,19},{19,3},{4,20},{20... | collective-permute-start | bytes 55304 | tf_op jit(solution)/shard_map/ppermute | solution.py:342
  22.1 4.5 %collective-permute-start = (bf16[16,1024]{1,0:T(8,128)(2,1)S(1)}, bf16[16,1024]{1,0:T(8,128)(2,1)S(1)}, u32[]{:S(2)}, u32[]{:S(2)}) collective-permute-start(bf16[16,1024]{1,0:T(8,128)(2,1)S(1)} %slice_select_fusion), channel_id=1, source_target_pairs={{0,8},{1,9},{2,10},{3,11},{4,12},{5,13},{6,14},{7,15},{16,24},{17,... | collective-permute-start | bytes 98312 | tf_op jit(solution)/shard_map/ppermute | solution.py:337
  33.4 5.7 %collective-permute-done.3 = bf16[16,1024]{1,0:T(8,128)(2,1)S(1)} collective-permute-done((bf16[16,1024]{1,0:T(8,128)(2,1)S(1)}, bf16[16,1024]{1,0:T(8,128)(2,1)S(1)}, u32[]{:S(2)}, u32[]{:S(2)}) %collective-permute-start.3) | collective-permute-done | bytes 32800 | tf_op jit(solution)/shard_map/ppermute | solution.py:359
  39.7 6.1 %collective-permute-done.5 = bf16[784,512]{1,0:T(8,128)(2,1)} collective-permute-done((bf16[784,512]{1,0:T(8,128)(2,1)S(1)}, bf16[784,512]{1,0:T(8,128)(2,1)}, u32[]{:S(2)}, u32[]{:S(2)}) %collective-permute-start.5) | collective-permute-done | bytes 802848 | tf_op jit(solution)/shard_map/ppermute | solution.py:342
  49.7 11.4 %front.1 = (bf16[1024,1024]{1,0:T(8,128)(2,1)}, bf16[1024,256]{1,0:T(8,128)(2,1)}, bf16[4,272,512]{2,1,0:T(8,128)(2,1)}, f32[1024,512]{1,0:T(8,128)}, bf16[1024,...) custom-call(bf16[1024,1024]{1,0:T(8,128)(2,1)} %all-gather.7.cloned., ...), custom_call_target="tpu_custom_call" | custom-call | flops 3145728 | bytes 44236800 | tf_op jit(solution)/shard_map/front/pallas_call | solution.py:571
  65.8 4.5 %intra.1.ins_ref = f32[1024,256]{1,0:T(8,128)} custom-call(bf16[1024,256]{1,0:T(8,128)(2,1)} %get-tuple-element.100.refs_0_.kq_ref.refs_7_, bf16[1024,256]{1,0:T(8,128)(2,1)} %get-tuple-element.101.refs_1_, f32[1024,128]{1,0:T(8,128)} %get-tuple-element.104.refs_2_), custom_call_target="tpu_custom_call" | custom-call | flops 1310720 | bytes 18432000 | tf_op jit(solution)/shard_map/intra/pallas_call | solution.py:593
  71.0 2.5 collective-permute-done.7
  74.6 6.5 %gate.1 = (bf16[1024,256]{1,0:T(8,128)(2,1)}, bf16[1024,256]{1,0:T(8,128)(2,1)}, bf16[1024,1024]{1,0:T(8,128)(2,1)}, f32[8,1024]{1,0:T(8,128)}) custom-call(bf16[1024,256]{1,0:T(8,128)(2,1)} %get-tuple-element.100.refs_0_.kq_ref.refs_7_, bf16[1024,256]{1,0:T(8,128)(2,1)} %get-tuple-element.108.expc_ref.refs_8_.refs_10_, f32[1024,256]{1,0:T(8,128)} %intra.1.ins_ref, ...), custom_call_target="tpu_custom_call" | custom-call | flops 1835008 | bytes 25804800 | tf_op jit(solution)/shard_map/gate/pallas_call | solution.py:603
  83.3 1.6 collective-permute-start.9
  84.9 2.3 collective-permute-done.9
  87.3 1.7 collective-permute-start.10
  89.0 2.2 collective-permute-done.10
  91.9 8.0 %back_gate.1 = (bf16[1024,256]{1,0:T(8,128)(2,1)}, bf16[1024,256]{1,0:T(8,128)(2,1)}, bf16[256,1024]{1,0:T(8,128)(2,1)}, bf16[256,1024]{1,0:T(8,128)(2,1)}, f32[...) custom-call(f32[8,1024]{1,0:T(8,128)} %add.333.refs_0_, ...), custom_call_target="tpu_custom_call" | custom-call | flops 2097152 | bytes 29491200 | tf_op jit(solution)/shard_map/back_gate/pallas_call | solution.py:617
  103.5 6.4 %back_intra.1 = (f32[1024,256]{1,0:T(8,128)}, f32[1024,256]{1,0:T(8,128)}, f32[1024,128]{1,0:T(8,128)}) custom-call(bf16[1024,256]{1,0:T(8,128)(2,1)} %get-tuple-element.100.refs_0_.kq_ref.refs_7_, bf16[1024,256]{1,0:T(8,128)(2,1)} %get-tuple-element.101.refs_1_, f32[1024,128]{1,0:T(8,128)} %get-tuple-element.104.refs_2_, ...), custom_call_target="tpu_custom_call" | custom-call | flops 1835008 | bytes 25804800 | tf_op jit(solution)/shard_map/back_intra/pallas_call | solution.py:644
  111.4 8.8 %back.1 = (bf16[1024,512]{1,0:T(8,128)(2,1)}, bf16[1024,128]{1,0:T(8,128)(2,1)}, f32[16,512]{1,0:T(8,128)}, f32[8,512]{1,0:T(8,128)}, f32[8,128]{1,0:T(8,128)}) custom-call(bf16[1024,256]{1,0:T(8,128)(2,1)} %get-tuple-element.100.refs_0_.kq_ref.refs_7_, bf16[1024,256]{1,0:T(8,128)(2,1)} %get-tuple-element.101.refs_1_, ...), custom_call_target="tpu_custom_call" | custom-call | flops 2359296 | bytes 33177600 | tf_op jit(solution)/shard_map/back/pallas_call | solution.py:657
  122.5 1.8 fusion.35
  124.3 3.5 %collective-permute-start.14 = (bf16[256,512]{1,0:T(8,128)(2,1)}, bf16[256,512]{1,0:T(8,128)(2,1)}, u32[]{:S(2)}, u32[]{:S(2)}) collective-permute-start(bf16[256,512]{1,0:T(8,128)(2,1)} %fusion.35), channel_id=1, source_target_pairs={{0,8},{8,0},{1,9},{9,1},{2,10},{10,2},{3,11},{11,3},{4,12},{12,4},... | collective-permute-start | bytes 786440 | tf_op jit(solution)/shard_map/ppermute | solution.py:383
  129.3 3.1 %fusion.53 = f32[640,1024]{1,0:T(8,128)} fusion(bf16[1024,640]{1,0:T(8,128)(2,1)S(1)} %constant_dynamic-update-slice_fusion.2, bf16[1024,1024]{1,0:T(8,128)(2,1)S(1)} %copy-done.5), kind=kOutput, calls=%fused_computation.155 | convolution fusion | flops 1342177280 | bytes 6029312 | tf_op jit(solution)/shard_map/dot_general | solution.py:18
  133.5 4.5 %collective-permute-done.14 = bf16[256,512]{1,0:T(8,128)(2,1)} collective-permute-done((bf16[256,512]{1,0:T(8,128)(2,1)}, bf16[256,512]{1,0:T(8,128)(2,1)}, u32[]{:S(2)}, u32[]{:S(2)}) %collective-permute-start.14) | collective-permute-done | bytes 262176 | tf_op jit(solution)/shard_map/ppermute | solution.py:383
  138.0 1.8 add_convert_fusion.1
  143.8 1.6 collective-permute-start.15
  145.5 2.3 convolution_convert_fusion
  148.1 3.2 %collective-permute-done.15 = bf16[272,512]{1,0:T(8,128)(2,1)S(1)} collective-permute-done((bf16[272,512]{1,0:T(8,128)(2,1)S(1)}, bf16[272,512]{1,0:T(8,128)(2,1)S(1)}, u32[]{:S(2)}, u32[]{:S(2)}) %collective-permute-start.15) | collective-permute-done | bytes 278560 | tf_op jit(solution)/shard_map/ppermute | solution.py:373
  158.1 5.8 %collective-permute-start.20 = (bf16[64,1024]{1,0:T(8,128)(2,1)S(1)}, bf16[64,1024]{1,0:T(8,128)(2,1)}, u32[]{:S(2)}, u32[]{:S(2)}) collective-permute-start(bf16[64,1024]{1,0:T(8,128)(2,1)S(1)} %get-tuple-element.196), channel_id=1, source_target_pairs={{0,1},{1,3},{2,5},{3,7},{4,17},{5,19},{6,21},{7,23},{8,9},{9,11},{... | collective-permute-start | bytes 393224 | tf_op jit(solution)/shard_map/ppermute | solution.py:712
  164.7 3.0 %collective-permute-start.25 = (bf16[272,512]{1,0:T(8,128)(2,1)}, bf16[272,512]{1,0:T(8,128)(2,1)}, u32[]{:S(2)}, u32[]{:S(2)}) collective-permute-start(bf16[272,512]{1,0:T(8,128)(2,1)} %convert_element_type.212), channel_id=1, source_target_pairs={{0,8},{8,0},{1,9},{9,1},{2,10},{10,2},{3,11},{11,3},{4,12},{12,4},... | collective-permute-start | bytes 835592 | tf_op jit(solution)/shard_map/ppermute | solution.py:383
  167.7 1.6 fusion.2
  169.3 3.1 %collective-permute-done.21 = bf16[64,1024]{1,0:T(8,128)(2,1)} collective-permute-done((bf16[64,1024]{1,0:T(8,128)(2,1)S(1)}, bf16[64,1024]{1,0:T(8,128)(2,1)}, u32[]{:S(2)}, u32[]{:S(2)}) %collective-permute-start.21) | collective-permute-done | bytes 131104 | tf_op jit(solution)/shard_map/ppermute | solution.py:712
  172.4 2.1 multiply_reduce_fusion
  175.4 10.0 %collective-permute-start.29 = (f32[8,2304]{1,0:T(8,128)S(1)}, f32[8,2304]{1,0:T(8,128)S(1)}, u32[]{:S(2)}, u32[]{:S(2)}) collective-permute-start(f32[8,2304]{1,0:T(8,128)S(1)} %select_maximum_fusion), channel_id=1, source_target_pairs={{0,1},{1,0},{2,3},{3,2},{4,5},{5,4},{6,7},{7,6},{8,9},{9,8},{10,11... | collective-permute-start | bytes 221192 | tf_op jit(solution)/shard_map/ppermute | solution.py:404
  187.0 1.9 collective-permute-start.28
  190.8 1.8 collective-permute-done.28
  193.9 3.7 %collective-permute-start.32 = (bf16[64,1024]{1,0:T(8,128)(2,1)S(1)}, bf16[64,1024]{1,0:T(8,128)(2,1)S(1)}, u32[]{:S(2)}, u32[]{:S(2)}) collective-permute-start(bf16[64,1024]{1,0:T(8,128)(2,1)S(1)} %add_convert_fusion.2), channel_id=1, source_target_pairs={{0,8},{8,0},{1,9},{9,1},{2,10},{10,2},{3,11},{11,3},{4,12},{12,4},... | collective-permute-start | bytes 393224 | tf_op jit(solution)/shard_map/ppermute | solution.py:383
  197.6 1.9 collective-permute-start.31
  199.5 2.4 collective-permute-done.31
  207.3 2.1 collective-permute-start.24
  210.7 4.4 %widen_z.1.refs_0_ = f32[4384,512]{1,0:T(8,128)} custom-call(bf16[8,256,512]{2,1,0:T(8,128)(2,1)} %bitcast.105), custom_call_target="tpu_custom_call" | custom-call | flops 1310720 | bytes 18432000 | tf_op jit(solution)/shard_map/widen_z/pallas_call | solution.py:766
  215.0 16.2 %collective-permute-done.34 = f32[8,2304]{1,0:T(8,128)S(1)} collective-permute-done((f32[8,2304]{1,0:T(8,128)S(1)}, f32[8,2304]{1,0:T(8,128)S(1)}, u32[]{:S(2)}, u32[]{:S(2)}) %collective-permute-start.34) | collective-permute-done | bytes 73760 | tf_op jit(solution)/shard_map/ppermute | solution.py:404
  231.7 4.6 %collective-permute-done.33 = bf16[32,512]{1,0:T(8,128)(2,1)S(1)} collective-permute-done((bf16[32,512]{1,0:T(8,128)(2,1)S(1)}, bf16[32,512]{1,0:T(8,128)(2,1)S(1)}, u32[]{:S(2)}, u32[]{:S(2)}) %collective-permute-start.33) | collective-permute-done | bytes 32800 | tf_op jit(solution)/shard_map/ppermute | solution.py:404
  237.5 2.4 collective-permute-start.35
  240.3 1.6 collective-permute-done.37
  242.0 2.3 collective-permute-done.38
  246.1 4.0 %collective-permute-done.39 = f32[8,2304]{1,0:T(8,128)S(1)} collective-permute-done((f32[8,2304]{1,0:T(8,128)S(1)}, f32[8,2304]{1,0:T(8,128)S(1)}, u32[]{:S(2)}, u32[]{:S(2)}) %collective-permute-start.39) | collective-permute-done | bytes 73760 | tf_op jit(solution)/shard_map/ppermute | solution.py:404
  254.9 6.0 %widen_out.1 = f32[1024,1024]{1,0:T(8,128)} custom-call(bf16[8,528,512]{2,1,0:T(8,128)(2,1)} %bitcast.99), custom_call_target="tpu_custom_call" | custom-call | flops 1572864 | bytes 22118400 | tf_op jit(solution)/shard_map/widen_out/pallas_call | solution.py:813
  260.9 4.2 %widen_x.1.old_ref = f32[4384,512]{1,0:T(8,128)} custom-call(bf16[8,528,512]{2,1,0:T(8,128)(2,1)} %bitcast.100, f32[4384,512]{1,0:T(8,128)} %widen_z.1.refs_0_), custom_call_target="tpu_custom_call", output_to_operand_aliasing={{}: (1, {})} | custom-call | flops 1310720 | bytes 18432000 | tf_op jit(solution)/shard_map/widen_x/pallas_call | solution.py:791
  265.9 2.0 widen_kq.1
  (248 shorter events, 68.9 us)
Async XLA Ops:
  7.2 40.0 %copy-start = (bf16[1024,1024]{1,0:T(8,128)(2,1)S(1)}, bf16[1024,1024]{1,0:T(8,128)(2,1)}, u32[]{:S(2)}) copy-start(bf16[1024,1024]{1,0:T(8,128)(2,1)} %param.20) | copy-start | bytes 6291460
  7.2 42.5 %all-gather.7.cloned.1.call-start = ((), (), s32[]{:S(2)}) async-start(), calls=%async_computation.1 | async-start | bytes 2359296 | tf_op jit(solution)/shard_map/all_gather | solution.py:533
  7.9 66.6 %all-gather.9.cloned.1.call-start = ((), (), s32[]{:S(2)}) async-start(), calls=%async_computation.2 | async-start | bytes 2359296 | tf_op jit(solution)/shard_map/all_gather | solution.py:535
  19.0 8.2 %collective-permute-start.4 = (bf16[8,1152]{1,0:T(8,128)(2,1)S(1)}, bf16[8,1152]{1,0:T(8,128)(2,1)S(1)}, u32[]{:S(2)}, u32[]{:S(2)}) collective-permute-start(bf16[8,1152]{1,0:T(8,128)(2,1)S(1)} %concatenate.49), channel_id=1, source_target_pairs={{0,16},{16,0},{1,17},{17,1},{2,18},{18,2},{3,19},{19,3},{4,20},{20... | collective-permute-start | bytes 55304 | tf_op jit(solution)/shard_map/ppermute | solution.py:342
  22.1 6.5 %collective-permute-start = (bf16[16,1024]{1,0:T(8,128)(2,1)S(1)}, bf16[16,1024]{1,0:T(8,128)(2,1)S(1)}, u32[]{:S(2)}, u32[]{:S(2)}) collective-permute-start(bf16[16,1024]{1,0:T(8,128)(2,1)S(1)} %slice_select_fusion), channel_id=1, source_target_pairs={{0,8},{1,9},{2,10},{3,11},{4,12},{5,13},{6,14},{7,15},{16,24},{17,... | collective-permute-start | bytes 98312 | tf_op jit(solution)/shard_map/ppermute | solution.py:337
  26.6 19.2 %collective-permute-start.5 = (bf16[784,512]{1,0:T(8,128)(2,1)S(1)}, bf16[784,512]{1,0:T(8,128)(2,1)}, u32[]{:S(2)}, u32[]{:S(2)}) collective-permute-start(bf16[784,512]{1,0:T(8,128)(2,1)S(1)} %concatenate.50), channel_id=1, source_target_pairs={{0,16},{16,0},{1,17},{17,1},{2,18},{18,2},{3,19},{19,3},{4,20},{20... | collective-permute-start | bytes 2408456 | tf_op jit(solution)/shard_map/ppermute | solution.py:342
  27.2 100.7 %reduce-scatter.2.cloned.1.call-start = ((), (), s32[]{:S(2)}) async-start(), calls=%async_computation.3 | async-start | bytes 2359296 | tf_op jit(solution)/shard_map/reduce_scatter | solution.py:642
  28.5 1.4 collective-permute-start.1
  30.0 0.8 collective-permute-start.2
  30.9 8.3 %collective-permute-start.3 = (bf16[16,1024]{1,0:T(8,128)(2,1)S(1)}, bf16[16,1024]{1,0:T(8,128)(2,1)S(1)}, u32[]{:S(2)}, u32[]{:S(2)}) collective-permute-start(bf16[16,1024]{1,0:T(8,128)(2,1)S(1)} %add.324), channel_id=1, source_target_pairs={{7,6},{5,4},{3,2},{1,0},{15,14},{13,12},{11,10},{9,8},{23,22},{21,... | collective-permute-start | bytes 98312 | tf_op jit(solution)/shard_map/ppermute | solution.py:359
  61.2 12.3 %collective-permute-start.7 = (bf16[256,1024]{1,0:T(8,128)(2,1)S(1)}, bf16[256,1024]{1,0:T(8,128)(2,1)S(1)}, u32[]{:S(2)}, u32[]{:S(2)}) collective-permute-start(bf16[256,1024]{1,0:T(8,128)(2,1)S(1)} %copy-done.15), channel_id=1, source_target_pairs={{0,16},{16,0},{1,17},{17,1},{2,18},{18,2},{3,19},{19,3},{4,20},{20... | collective-permute-start | bytes 1572872 | tf_op jit(solution)/shard_map/ppermute | solution.py:342
  63.6 6.7 %collective-permute-start.6 = (bf16[128,256]{1,0:T(8,128)(2,1)S(1)}, bf16[128,256]{1,0:T(8,128)(2,1)S(1)}, u32[]{:S(2)}, u32[]{:S(2)}) collective-permute-start(bf16[128,256]{1,0:T(8,128)(2,1)S(1)} %convert_element_type.184), channel_id=1, source_target_pairs={{0,8},{1,9},{2,10},{3,11},{4,12},{5,13},{6,14},{7,15},{16,24},{17,... | collective-permute-start | bytes 196616 | tf_op jit(solution)/shard_map/ppermute | solution.py:337
  81.1 1.5 collective-permute-start.8
  83.3 3.9 %collective-permute-start.9 = (f32[8,1024]{1,0:T(8,128)S(1)}, f32[8,1024]{1,0:T(8,128)S(1)}, u32[]{:S(2)}, u32[]{:S(2)}) collective-permute-start(f32[8,1024]{1,0:T(8,128)S(1)} %add.331), channel_id=1, source_target_pairs={{0,2},{1,3},{2,0},{3,1},{4,6},{5,7},{6,4},{7,5},{8,10},{9,11},{10,... | collective-permute-start | bytes 98312 | tf_op jit(solution)/shard_map/ppermute | solution.py:404
  87.3 3.9 %collective-permute-start.10 = (f32[8,1024]{1,0:T(8,128)S(1)}, f32[8,1024]{1,0:T(8,128)S(1)}, u32[]{:S(2)}, u32[]{:S(2)}) collective-permute-start(f32[8,1024]{1,0:T(8,128)S(1)} %add.332), channel_id=1, source_target_pairs={{0,4},{1,5},{2,6},{3,7},{4,0},{5,1},{6,2},{7,3},{8,12},{9,13},{10,... | collective-permute-start | bytes 98312 | tf_op jit(solution)/shard_map/ppermute | solution.py:404
  91.8 80.6 %all-gather.11.cloned.1.call-start = ((), (), s32[]{:S(2)}) async-start(), calls=%async_computation.4 | async-start | bytes 2359296 | tf_op jit(solution)/shard_map/all_gather | solution.py:688
  100.9 9.8 %collective-permute-start.11 = (bf16[256,512]{1,0:T(8,128)(2,1)S(1)}, bf16[256,512]{1,0:T(8,128)(2,1)S(1)}, u32[]{:S(2)}, u32[]{:S(2)}) collective-permute-start(bf16[256,512]{1,0:T(8,128)(2,1)S(1)} %constant_dynamic-slice_fusion.9), channel_id=1, source_target_pairs={{0,16},{16,0},{1,17},{17,1},{2,18},{18,2},{3,19},{19,3},{4,20},{20... | collective-permute-start | bytes 786440 | tf_op jit(solution)/shard_map/ppermute | solution.py:373
  102.2 7.7 %collective-permute-start.12 = (bf16[128,256]{1,0:T(8,128)(2,1)S(1)}, bf16[128,256]{1,0:T(8,128)(2,1)S(1)}, u32[]{:S(2)}, u32[]{:S(2)}) collective-permute-start(bf16[128,256]{1,0:T(8,128)(2,1)S(1)} %convert_element_type.186), channel_id=1, source_target_pairs={{8,0},{9,1},{10,2},{11,3},{12,4},{13,5},{14,6},{15,7},{24,16},{25,... | collective-permute-start | bytes 196616 | tf_op jit(solution)/shard_map/ppermute | solution.py:337
  121.1 12.5 %collective-permute-start.13 = (bf16[16,512]{1,0:T(8,128)(2,1)S(1)}, bf16[16,512]{1,0:T(8,128)(2,1)S(1)}, u32[]{:S(2)}, u32[]{:S(2)}) collective-permute-start(bf16[16,512]{1,0:T(8,128)(2,1)S(1)} %convert.18), channel_id=1, source_target_pairs={{8,0},{9,1},{10,2},{11,3},{12,4},{13,5},{14,6},{15,7},{24,16},{25,... | collective-permute-start | bytes 49160 | tf_op jit(solution)/shard_map/ppermute | solution.py:337
  124.3 13.7 %collective-permute-start.14 = (bf16[256,512]{1,0:T(8,128)(2,1)}, bf16[256,512]{1,0:T(8,128)(2,1)}, u32[]{:S(2)}, u32[]{:S(2)}) collective-permute-start(bf16[256,512]{1,0:T(8,128)(2,1)} %fusion.35), channel_id=1, source_target_pairs={{0,8},{8,0},{1,9},{9,1},{2,10},{10,2},{3,11},{11,3},{4,12},{12,4},... | collective-permute-start | bytes 786440 | tf_op jit(solution)/shard_map/ppermute | solution.py:383
  139.8 114.3 %all-gather.13.cloned.1.call-start = ((), (), s32[]{:S(2)}) async-start(), calls=%async_computation.5 | async-start | bytes 4866048 | tf_op jit(solution)/shard_map/all_gather | solution.py:749
  143.8 7.4 %collective-permute-start.15 = (bf16[272,512]{1,0:T(8,128)(2,1)S(1)}, bf16[272,512]{1,0:T(8,128)(2,1)S(1)}, u32[]{:S(2)}, u32[]{:S(2)}) collective-permute-start(bf16[272,512]{1,0:T(8,128)(2,1)S(1)} %fusion.21), channel_id=1, source_target_pairs={{0,16},{16,0},{1,17},{17,1},{2,18},{18,2},{3,19},{19,3},{4,20},{20... | collective-permute-start | bytes 835592 | tf_op jit(solution)/shard_map/ppermute | solution.py:373
  152.5 12.1 %collective-permute-start.16 = (bf16[4,128,1024]{2,1,0:T(8,128)(2,1)}, bf16[4,128,1024]{2,1,0:T(8,128)(2,1)}, u32[]{:S(2)}, u32[]{:S(2)}) collective-permute-start(bf16[4,128,1024]{2,1,0:T(8,128)(2,1)} %dynamic-slice_bitcast_fusion), channel_id=1, source_target_pairs={{0,1},{1,0},{2,3},{3,2},{4,5},{5,4},{6,7},{7,6},{8,9},{9,8},{10,11... | collective-permute-start | bytes 3145736 | tf_op jit(solution)/shard_map/ppermute | solution.py:404
  154.9 9.7 %collective-permute-start.17 = (bf16[4,32,1024]{2,1,0:T(8,128)(2,1)S(1)}, bf16[4,32,1024]{2,1,0:T(8,128)(2,1)S(1)}, u32[]{:S(2)}, u32[]{:S(2)}) collective-permute-start(bf16[4,32,1024]{2,1,0:T(8,128)(2,1)S(1)} %fusion.36), channel_id=1, source_target_pairs={{0,1},{1,0},{2,3},{3,2},{4,5},{5,4},{6,7},{7,6},{8,9},{9,8},{10,11... | collective-permute-start | bytes 786440 | tf_op jit(solution)/shard_map/ppermute | solution.py:404
  156.8 12.5 %collective-permute-start.18 = (bf16[64,1024]{1,0:T(8,128)(2,1)S(1)}, bf16[64,1024]{1,0:T(8,128)(2,1)}, u32[]{:S(2)}, u32[]{:S(2)}) collective-permute-start(bf16[64,1024]{1,0:T(8,128)(2,1)S(1)} %get-tuple-element.198), channel_id=1, source_target_pairs={{0,0},{1,2},{2,4},{3,6},{4,16},{5,18},{6,20},{7,22},{8,8},{9,10},{... | collective-permute-start | bytes 393224 | tf_op jit(solution)/shard_map/ppermute | solution.py:712
  158.1 11.2 %collective-permute-start.19 = (bf16[64,1024]{1,0:T(8,128)(2,1)S(1)}, bf16[64,1024]{1,0:T(8,128)(2,1)}, u32[]{:S(2)}, u32[]{:S(2)}) collective-permute-start(bf16[64,1024]{1,0:T(8,128)(2,1)S(1)} %get-tuple-element.197), channel_id=1, source_target_pairs={{0,8},{1,10},{2,12},{3,14},{4,24},{5,26},{6,28},{7,30},{8,1},{9,3}... | collective-permute-start | bytes 393224 | tf_op jit(solution)/shard_map/ppermute | solution.py:712
  158.1 11.3 %collective-permute-start.20 = (bf16[64,1024]{1,0:T(8,128)(2,1)S(1)}, bf16[64,1024]{1,0:T(8,128)(2,1)}, u32[]{:S(2)}, u32[]{:S(2)}) collective-permute-start(bf16[64,1024]{1,0:T(8,128)(2,1)S(1)} %get-tuple-element.196), channel_id=1, source_target_pairs={{0,1},{1,3},{2,5},{3,7},{4,17},{5,19},{6,21},{7,23},{8,9},{9,11},{... | collective-permute-start | bytes 393224 | tf_op jit(solution)/shard_map/ppermute | solution.py:712
  164.6 7.8 %collective-permute-start.21 = (bf16[64,1024]{1,0:T(8,128)(2,1)S(1)}, bf16[64,1024]{1,0:T(8,128)(2,1)}, u32[]{:S(2)}, u32[]{:S(2)}) collective-permute-start(bf16[64,1024]{1,0:T(8,128)(2,1)S(1)} %get-tuple-element.195), channel_id=1, source_target_pairs={{0,9},{1,11},{2,13},{3,15},{4,25},{5,27},{6,29},{7,31},{8,0},{9,2}... | collective-permute-start | bytes 393224 | tf_op jit(solution)/shard_map/ppermute | solution.py:712
  164.7 37.2 %collective-permute-start.25 = (bf16[272,512]{1,0:T(8,128)(2,1)}, bf16[272,512]{1,0:T(8,128)(2,1)}, u32[]{:S(2)}, u32[]{:S(2)}) collective-permute-start(bf16[272,512]{1,0:T(8,128)(2,1)} %convert_element_type.212), channel_id=1, source_target_pairs={{0,8},{8,0},{1,9},{9,1},{2,10},{10,2},{3,11},{11,3},{4,12},{12,4},... | collective-permute-start | bytes 835592 | tf_op jit(solution)/shard_map/ppermute | solution.py:383
  175.4 13.6 %collective-permute-start.29 = (f32[8,2304]{1,0:T(8,128)S(1)}, f32[8,2304]{1,0:T(8,128)S(1)}, u32[]{:S(2)}, u32[]{:S(2)}) collective-permute-start(f32[8,2304]{1,0:T(8,128)S(1)} %select_maximum_fusion), channel_id=1, source_target_pairs={{0,1},{1,0},{2,3},{3,2},{4,5},{5,4},{6,7},{7,6},{8,9},{9,8},{10,11... | collective-permute-start | bytes 221192 | tf_op jit(solution)/shard_map/ppermute | solution.py:404
  185.4 4.3 %collective-permute-start.26 = (bf16[32,1024]{1,0:T(8,128)(2,1)S(1)}, bf16[32,1024]{1,0:T(8,128)(2,1)S(1)}, u32[]{:S(2)}, u32[]{:S(2)}) collective-permute-start(bf16[32,1024]{1,0:T(8,128)(2,1)S(1)} %get-tuple-element.205), channel_id=1, source_target_pairs={{0,2},{1,3},{2,0},{3,1},{4,6},{5,7},{6,4},{7,5},{8,10},{9,11},{10,... | collective-permute-start | bytes 196616 | tf_op jit(solution)/shard_map/ppermute | solution.py:404
  186.6 4.3 %collective-permute-start.27 = (bf16[32,1024]{1,0:T(8,128)(2,1)S(1)}, bf16[32,1024]{1,0:T(8,128)(2,1)S(1)}, u32[]{:S(2)}, u32[]{:S(2)}) collective-permute-start(bf16[32,1024]{1,0:T(8,128)(2,1)S(1)} %get-tuple-element.204), channel_id=1, source_target_pairs={{0,4},{1,5},{2,6},{3,7},{4,0},{5,1},{6,2},{7,3},{8,12},{9,13},{10,... | collective-permute-start | bytes 196616 | tf_op jit(solution)/shard_map/ppermute | solution.py:404
  187.0 5.6 %collective-permute-start.28 = (bf16[32,1024]{1,0:T(8,128)(2,1)S(1)}, bf16[32,1024]{1,0:T(8,128)(2,1)S(1)}, u32[]{:S(2)}, u32[]{:S(2)}) collective-permute-start(bf16[32,1024]{1,0:T(8,128)(2,1)S(1)} %get-tuple-element.203), channel_id=1, source_target_pairs={{0,6},{1,7},{2,4},{3,5},{4,2},{5,3},{6,0},{7,1},{8,14},{9,15},{10,... | collective-permute-start | bytes 196616 | tf_op jit(solution)/shard_map/ppermute | solution.py:404
  192.6 6.9 %collective-permute-start.30 = (bf16[32,512]{1,0:T(8,128)(2,1)S(1)}, bf16[32,512]{1,0:T(8,128)(2,1)S(1)}, u32[]{:S(2)}, u32[]{:S(2)}) collective-permute-start(bf16[32,512]{1,0:T(8,128)(2,1)S(1)} %dynamic-slice_convert_fusion.1), channel_id=1, source_target_pairs={{0,16},{16,0},{1,17},{17,1},{2,18},{18,2},{3,19},{19,3},{4,20},{20... | collective-permute-start | bytes 98312 | tf_op jit(solution)/shard_map/ppermute | solution.py:373
  193.9 8.8 %collective-permute-start.32 = (bf16[64,1024]{1,0:T(8,128)(2,1)S(1)}, bf16[64,1024]{1,0:T(8,128)(2,1)S(1)}, u32[]{:S(2)}, u32[]{:S(2)}) collective-permute-start(bf16[64,1024]{1,0:T(8,128)(2,1)S(1)} %add_convert_fusion.2), channel_id=1, source_target_pairs={{0,8},{8,0},{1,9},{9,1},{2,10},{10,2},{3,11},{11,3},{4,12},{12,4},... | collective-permute-start | bytes 393224 | tf_op jit(solution)/shard_map/ppermute | solution.py:383
  197.6 4.4 %collective-permute-start.31 = (f32[8,2304]{1,0:T(8,128)S(1)}, f32[8,2304]{1,0:T(8,128)S(1)}, u32[]{:S(2)}, u32[]{:S(2)}) collective-permute-start(f32[8,2304]{1,0:T(8,128)S(1)} %fusion.56), channel_id=1, source_target_pairs={{0,2},{1,3},{2,0},{3,1},{4,6},{5,7},{6,4},{7,5},{8,10},{9,11},{10,... | collective-permute-start | bytes 221192 | tf_op jit(solution)/shard_map/ppermute | solution.py:404
  205.9 25.4 %collective-permute-start.22 = (bf16[128,1024]{1,0:T(8,128)(2,1)}, bf16[128,1024]{1,0:T(8,128)(2,1)S(1)}, u32[]{:S(2)}, u32[]{:S(2)}) collective-permute-start(bf16[128,1024]{1,0:T(8,128)(2,1)} %get-tuple-element.192), channel_id=1, source_target_pairs={{0,2},{1,3},{2,0},{3,1},{4,6},{5,7},{6,4},{7,5},{8,10},{9,11},{10,... | collective-permute-start | bytes 786440 | tf_op jit(solution)/shard_map/ppermute | solution.py:404
  207.2 24.1 %collective-permute-start.23 = (bf16[128,1024]{1,0:T(8,128)(2,1)}, bf16[128,1024]{1,0:T(8,128)(2,1)S(1)}, u32[]{:S(2)}, u32[]{:S(2)}) collective-permute-start(bf16[128,1024]{1,0:T(8,128)(2,1)} %get-tuple-element.191), channel_id=1, source_target_pairs={{0,4},{1,5},{2,6},{3,7},{4,0},{5,1},{6,2},{7,3},{8,12},{9,13},{10,... | collective-permute-start | bytes 786440 | tf_op jit(solution)/shard_map/ppermute | solution.py:404
  207.3 24.0 %collective-permute-start.24 = (bf16[128,1024]{1,0:T(8,128)(2,1)S(1)}, bf16[128,1024]{1,0:T(8,128)(2,1)S(1)}, u32[]{:S(2)}, u32[]{:S(2)}) collective-permute-start(bf16[128,1024]{1,0:T(8,128)(2,1)S(1)} %get-tuple-element.190), channel_id=1, source_target_pairs={{0,6},{1,7},{2,4},{3,5},{4,2},{5,3},{6,0},{7,1},{8,14},{9,15},{10,... | collective-permute-start | bytes 786440 | tf_op jit(solution)/shard_map/ppermute | solution.py:404
  210.1 21.2 %collective-permute-start.34 = (f32[8,2304]{1,0:T(8,128)S(1)}, f32[8,2304]{1,0:T(8,128)S(1)}, u32[]{:S(2)}, u32[]{:S(2)}) collective-permute-start(f32[8,2304]{1,0:T(8,128)S(1)} %add.375), channel_id=1, source_target_pairs={{0,4},{1,5},{2,6},{3,7},{4,0},{5,1},{6,2},{7,3},{8,12},{9,13},{10,... | collective-permute-start | bytes 221192 | tf_op jit(solution)/shard_map/ppermute | solution.py:404
  215.0 29.8 %copy-start.20 = (bf16[128,1024]{1,0:T(8,128)(2,1)S(1)}, bf16[128,1024]{1,0:T(8,128)(2,1)}, u32[]{:S(2)}) copy-start(bf16[128,1024]{1,0:T(8,128)(2,1)} %reduce-scatter.2.cloned.1.call-done) | copy-start | bytes 786436
  231.3 5.0 %collective-permute-start.33 = (bf16[32,512]{1,0:T(8,128)(2,1)S(1)}, bf16[32,512]{1,0:T(8,128)(2,1)S(1)}, u32[]{:S(2)}, u32[]{:S(2)}) collective-permute-start(bf16[32,512]{1,0:T(8,128)(2,1)S(1)} %convert_element_type.229), channel_id=1, source_target_pairs={{0,8},{8,0},{1,9},{9,1},{2,10},{10,2},{3,11},{11,3},{4,12},{12,4},... | collective-permute-start | bytes 98312 | tf_op jit(solution)/shard_map/ppermute | solution.py:404
  236.3 5.5 %collective-permute-start.37 = (bf16[32,512]{1,0:T(8,128)(2,1)S(1)}, bf16[32,512]{1,0:T(8,128)(2,1)S(1)}, u32[]{:S(2)}, u32[]{:S(2)}) collective-permute-start(bf16[32,512]{1,0:T(8,128)(2,1)S(1)} %convert_add_fusion.6), channel_id=1, source_target_pairs={{0,6},{1,7},{2,4},{3,5},{4,2},{5,3},{6,0},{7,1},{8,14},{9,15},{10,... | collective-permute-start | bytes 98312 | tf_op jit(solution)/shard_map/ppermute | solution.py:404
  236.8 5.1 %collective-permute-start.36 = (bf16[32,512]{1,0:T(8,128)(2,1)S(1)}, bf16[32,512]{1,0:T(8,128)(2,1)S(1)}, u32[]{:S(2)}, u32[]{:S(2)}) collective-permute-start(bf16[32,512]{1,0:T(8,128)(2,1)S(1)} %convert_add_fusion.6), channel_id=1, source_target_pairs={{0,4},{1,5},{2,6},{3,7},{4,0},{5,1},{6,2},{7,3},{8,12},{9,13},{10,... | collective-permute-start | bytes 98312 | tf_op jit(solution)/shard_map/ppermute | solution.py:404
  237.5 4.5 %collective-permute-start.35 = (bf16[32,512]{1,0:T(8,128)(2,1)S(1)}, bf16[32,512]{1,0:T(8,128)(2,1)S(1)}, u32[]{:S(2)}, u32[]{:S(2)}) collective-permute-start(bf16[32,512]{1,0:T(8,128)(2,1)S(1)} %convert_add_fusion.6), channel_id=1, source_target_pairs={{0,2},{1,3},{2,0},{3,1},{4,6},{5,7},{6,4},{7,5},{8,10},{9,11},{10,... | collective-permute-start | bytes 98312 | tf_op jit(solution)/shard_map/ppermute | solution.py:404
  239.9 4.4 %collective-permute-start.38 = (f32[8,2304]{1,0:T(8,128)S(1)}, f32[8,2304]{1,0:T(8,128)S(1)}, u32[]{:S(2)}, u32[]{:S(2)}) collective-permute-start(f32[8,2304]{1,0:T(8,128)S(1)} %add.384), channel_id=1, source_target_pairs={{0,16},{16,0},{1,17},{17,1},{2,18},{18,2},{3,19},{19,3},{4,20},{20... | collective-permute-start | bytes 221192 | tf_op jit(solution)/shard_map/ppermute | solution.py:404
  244.3 5.9 %collective-permute-start.39 = (f32[8,2304]{1,0:T(8,128)S(1)}, f32[8,2304]{1,0:T(8,128)S(1)}, u32[]{:S(2)}, u32[]{:S(2)}) collective-permute-start(f32[8,2304]{1,0:T(8,128)S(1)} %add.385), channel_id=1, source_target_pairs={{0,8},{8,0},{1,9},{9,1},{2,10},{10,2},{3,11},{11,3},{4,12},{12,4},... | collective-permute-start | bytes 221192 | tf_op jit(solution)/shard_map/ppermute | solution.py:404
  246.1 7.3 %collective-permute-start.40 = (bf16[128,512]{1,0:T(8,128)(2,1)S(1)}, bf16[128,512]{1,0:T(8,128)(2,1)S(1)}, u32[]{:S(2)}, u32[]{:S(2)}) collective-permute-start(bf16[128,512]{1,0:T(8,128)(2,1)S(1)} %pad_maximum_fusion.4), channel_id=1, source_target_pairs={{0,1},{1,0},{2,3},{3,2},{4,5},{5,4},{6,7},{7,6},{8,9},{9,8},{10,11... | collective-permute-start | bytes 393224 | tf_op jit(solution)/shard_map/ppermute | solution.py:404
  (24 other events, 185.7 us)
Sparse Core Ops, SparseCore 0:
  9.6 24.2 all-gather.6
  35.5 22.2 all-gather.8
  91.9 29.4 reduce-scatter.1
  139.9 22.4 all-gather.10
  204.8 38.9 all-gather.12
